TPU v7x, 256 devices: a whole 4x4x8 slice. The times are simulated.
256 devices in a mesh: tm: 8 (over y, x_lo), space: 32 (over z, x_hi, core).
Axes of the slice: x: 4 (x_hi: 2, x_lo: 2; x = x_hi * 2 + x_lo), y: 4, z: 8, core: 2. Of those that a mesh axis runs over, the one named last changes fastest.
Arguments:
- starts: float32 [8, 256, 256, 128], P('tm', 'space'), may hold values from -6 to 6
- material: int32 [256, 256, 128], P('space'), may hold values from 0 to 7, as said below
- source: float32 [256, 256, 128], P('space'), may hold values from -6 to 6
Outputs:
- next_starts: float32 [8, 256, 256, 128], P('tm', 'space')
Inputs may be any that keep to these rules, and one draw needn't show every extreme that they name: `material`: index into the table of 8 conductivities.
All inputs are finite; a program needn't handle non-finite values.
Results may differ from a plain program's by a relative error of at most 0.0001.
Values sent between devices are 32-bit elements; how exact they have to be, the bound alone decides.
No kernel may reach another device: no remote copies, remote signals or barrier semaphores. Data moves between devices by JAX's collectives and lax.ppermute only.
A program may use at most 64 MiB of HBM per device.

v0:
```python
import jax
import jax.numpy as jnp
from jax import lax
from jax.sharding import PartitionSpec as P

FSTEPS = 4
CSTEPS = 2
DEPTH = 2


conductivity_table = (1.0, 0.72, 0.52, 0.37, 0.26, 0.18, 0.13, 0.09)
fine_step = 0.15
coarse_step = 0.3


def with_halo(cells, sides, width):
    for axis, dim in sides:
        count = lax.axis_size(axis)
        ends = count - 1
        head = lax.slice_in_dim(cells, 0, width, axis=dim)
        tail = lax.slice_in_dim(cells, cells.shape[dim] - width, cells.shape[dim], axis=dim)
        cells = jnp.concatenate(
            [
                lax.ppermute(tail, axis, [(i, (i + 1) % count) for i in range(ends)]),
                cells,
                lax.ppermute(head, axis, [((i + 1) % count, i) for i in range(ends)]),
            ],
            axis=dim,
        )
    return cells


def shifted(x, axis, by):
    length = lax.axis_size(axis)
    pairs = [(i, i + by) for i in range(length) if 0 <= i + by < length]
    return lax.ppermute(x, axis, pairs)


def lookup(material):
    result = jnp.zeros(material.shape, jnp.float32)
    for number in range(8):
        result = jnp.where(material == number, jnp.float32(conductivity_table[number]), result)
    return result


def restrict(values):
    lead_dims = values.shape[:-3]
    folded = values.reshape(
        lead_dims + (values.shape[-3] // 2, 2, values.shape[-2] // 2, 2, values.shape[-1])
    )
    return jnp.mean(folded, axis=(-4, -2))


def prolong(values):
    lead_dims = values.shape[:-3]
    rows_x = values.shape[-3]
    rows_y = values.shape[-2]
    rows_z = values.shape[-1]
    spread = jnp.broadcast_to(
        values[..., :, None, :, None, :], lead_dims + (rows_x, 2, rows_y, 2, rows_z)
    )
    return spread.reshape(lead_dims + (rows_x * 2, rows_y * 2, rows_z))


def make_faces(cond_pad, weight_x, weight_y, weight_z):
    own = cond_pad[1:-1]
    face_x = weight_x * 0.5 * (cond_pad[1:] + cond_pad[:-1])
    pad_y = jnp.pad(own, ((0, 0), (1, 1), (0, 0)))
    face_y = weight_y * 0.5 * (pad_y[:, 1:] + pad_y[:, :-1])
    pad_z = jnp.pad(own, ((0, 0), (0, 0), (1, 1)))
    face_z = weight_z * 0.5 * (pad_z[:, :, 1:] + pad_z[:, :, :-1])
    return (face_x, face_y, face_z)


def diffuse(padded, face_x, face_y, face_z, source_in, step_size):
    current = padded[1:-1]
    grad_x = face_x * (padded[1:] - padded[:-1])
    flux = grad_x[1:] - grad_x[:-1]
    field_y = jnp.pad(current, ((0, 0), (1, 1), (0, 0)))
    grad_y = face_y * (field_y[:, 1:] - field_y[:, :-1])
    flux = flux + grad_y[:, 1:] - grad_y[:, :-1]
    field_z = jnp.pad(current, ((0, 0), (0, 0), (1, 1)))
    grad_z = face_z * (field_z[:, :, 1:] - field_z[:, :, :-1])
    flux = flux + grad_z[:, :, 1:] - grad_z[:, :, :-1]
    return current + step_size * (flux + source_in)


def local(starts, material, source):
    slab_index = lax.axis_index("tm")
    slab_count = lax.axis_size("tm")
    width_x = source.shape[0]
    conduct = lookup(material)
    coef_all = jnp.stack([conduct, source])
    coef_ext = with_halo(coef_all, (("space", 1),), DEPTH)
    ext_x, ext_y, ext_z = make_faces(coef_ext[0], 1.0, 1.0, 1.0)
    coarse_cond = restrict(coef_ext[0, DEPTH - 2 : DEPTH + width_x + 2])
    coarse_x, coarse_y, coarse_z = make_faces(coarse_cond, 0.25, 0.25, 1.0)
    coarse_source = restrict(source)
    near_x = ext_x[DEPTH - 1 : DEPTH + width_x]
    near_y = ext_y[DEPTH - 1 : DEPTH - 1 + width_x]
    near_z = ext_z[DEPTH - 1 : DEPTH - 1 + width_x]

    def coarse_run(current):
        reduced = restrict(current)
        for step_num in range(CSTEPS):
            padded = with_halo(reduced, (("space", 0),), 1)
            reduced = diffuse(padded, coarse_x, coarse_y, coarse_z, coarse_source, coarse_step)
        return reduced

    current = starts[0]
    coarse_now = prolong(coarse_run(current))
    fine_current = current
    for step_num in range(FSTEPS):
        padded = with_halo(fine_current, (("space", 0),), 1)
        fine_current = diffuse(padded, near_x, near_y, near_z, source, fine_step)
    offset = fine_current - coarse_now
    chain_start = current
    for round_num in range(slab_count - 1):
        passing = prolong(coarse_run(chain_start)) + offset
        arrived = shifted(passing, "tm", 1)
        chain_start = jnp.where(slab_index > round_num, arrived, chain_start)
    current = chain_start
    coarse_now = prolong(coarse_run(current))
    last_end = coarse_now + offset
    newest = shifted(last_end, "tm", 1 - slab_count)
    return jnp.where(slab_index == 0, newest, current)[None]


def solution(mesh):
    in_specs = (P("tm", "space", None, None), P("space", None, None), P("space", None, None))
    out_specs = P("tm", "space", None, None)
    return jax.shard_map(local, mesh=mesh, in_specs=in_specs, out_specs=out_specs, check_vma=False)
```

profile of v0, /device:TPU:1, one launch (start us, length us, event | category | flops | bytes accessed | tf_op | source)
XLA Modules:
  0.0 489.5 jit_solution(14604272688136346296)
XLA Ops:
  3.0 6.0 %collective-permute-start = (f32[2,2,256,128]{3,2,1,0:T(8,128)}, f32[2,2,256,128]{3,2,1,0:T(8,128)}, u32[]{:S(2)}, u32[]{:S(2)}) collective-permute-start(f32[2,2,256,128]{3,2,1,0:T(8,128)} %get-tuple-element.21), channel_id=1, source_target_pairs={{0,1},{1,2},{2,3},{3,4},{4,5},{5,6},{6,7},{7,8},{8,9},{9,10},{10,1... | collective-permute-start | bytes 1572872 | tf_op jit(solution)/shard_map/ppermute | solution.py:24
  13.6 5.1 %collective-permute-start.7 = (f32[1,256,128]{2,1,0:T(8,128)}, f32[1,256,128]{2,1,0:T(8,128)}, u32[]{:S(2)}, u32[]{:S(2)}) collective-permute-start(f32[1,256,128]{2,1,0:T(8,128)} %get-tuple-element.33), channel_id=1, source_target_pairs={{0,1},{1,2},{2,3},{3,4},{4,5},{5,6},{6,7},{7,8},{8,9},{9,10},{10,1... | collective-permute-start | bytes 393224 | tf_op jit(solution)/shard_map/ppermute | solution.py:24
  24.6 5.1 %collective-permute-start.3 = (f32[1,128,128]{2,1,0:T(8,128)S(1)}, f32[1,128,128]{2,1,0:T(8,128)}, u32[]{:S(2)}, u32[]{:S(2)}) collective-permute-start(f32[1,128,128]{2,1,0:T(8,128)S(1)} %get-tuple-element.65), channel_id=1, source_target_pairs={{0,1},{1,2},{2,3},{3,4},{4,5},{5,6},{6,7},{7,8},{8,9},{9,10},{10,1... | collective-permute-start | bytes 196616 | tf_op jit(solution)/shard_map/ppermute | solution.py:24
  40.9 5.1 %collective-permute-start.9 = (f32[1,256,128]{2,1,0:T(8,128)}, f32[1,256,128]{2,1,0:T(8,128)}, u32[]{:S(2)}, u32[]{:S(2)}) collective-permute-start(f32[1,256,128]{2,1,0:T(8,128)} %get-tuple-element.31), channel_id=1, source_target_pairs={{0,1},{1,2},{2,3},{3,4},{4,5},{5,6},{6,7},{7,8},{8,9},{9,10},{10,1... | collective-permute-start | bytes 393224 | tf_op jit(solution)/shard_map/ppermute | solution.py:24
  55.9 5.1 %collective-permute-start.5 = (f32[1,128,128]{2,1,0:T(8,128)S(1)}, f32[1,128,128]{2,1,0:T(8,128)S(1)}, u32[]{:S(2)}, u32[]{:S(2)}) collective-permute-start(f32[1,128,128]{2,1,0:T(8,128)S(1)} %get-tuple-element.63), channel_id=1, source_target_pairs={{0,1},{1,2},{2,3},{3,4},{4,5},{5,6},{6,7},{7,8},{8,9},{9,10},{10,1... | collective-permute-start | bytes 196616 | tf_op jit(solution)/shard_map/ppermute | solution.py:24
  69.9 6.7 %collective-permute-start.11 = (f32[1,256,128]{2,1,0:T(8,128)S(1)}, f32[1,256,128]{2,1,0:T(8,128)S(1)}, u32[]{:S(2)}, u32[]{:S(2)}) collective-permute-start(f32[1,256,128]{2,1,0:T(8,128)S(1)} %get-tuple-element.29), channel_id=1, source_target_pairs={{0,1},{1,2},{2,3},{3,4},{4,5},{5,6},{6,7},{7,8},{8,9},{9,10},{10,1... | collective-permute-start | bytes 393224 | tf_op jit(solution)/shard_map/ppermute | solution.py:24
  82.9 5.9 %collective-permute-start.13 = (f32[1,256,128]{2,1,0:T(8,128)S(1)}, f32[1,256,128]{2,1,0:T(8,128)S(1)}, u32[]{:S(2)}, u32[]{:S(2)}) collective-permute-start(f32[1,256,128]{2,1,0:T(8,128)S(1)} %get-tuple-element.27), channel_id=1, source_target_pairs={{0,1},{1,2},{2,3},{3,4},{4,5},{5,6},{6,7},{7,8},{8,9},{9,10},{10,1... | collective-permute-start | bytes 393224 | tf_op jit(solution)/shard_map/ppermute | solution.py:24
  97.5 17.2 %collective-permute-done.14 = f32[8,256,128]{2,1,0:T(8,128)} collective-permute-done((f32[8,256,128]{2,1,0:T(8,128)}, f32[8,256,128]{2,1,0:T(8,128)}, u32[]{:S(2)}, u32[]{:S(2)}) %collective-permute-start.14) | collective-permute-done | bytes 1048608 | tf_op jit(solution)/shard_map/ppermute | solution.py:36
  120.9 10.9 %collective-permute-start.16 = (f32[1,128,128]{2,1,0:T(8,128)S(1)}, f32[1,128,128]{2,1,0:T(8,128)S(1)}, u32[]{:S(2)}, u32[]{:S(2)}) collective-permute-start(f32[1,128,128]{2,1,0:T(8,128)S(1)} %get-tuple-element.61), channel_id=1, source_target_pairs={{0,1},{1,2},{2,3},{3,4},{4,5},{5,6},{6,7},{7,8},{8,9},{9,10},{10,1... | collective-permute-start | bytes 196616 | tf_op jit(solution)/shard_map/ppermute | solution.py:24
  135.9 5.9 %collective-permute-start.18 = (f32[1,128,128]{2,1,0:T(8,128)S(1)}, f32[1,128,128]{2,1,0:T(8,128)S(1)}, u32[]{:S(2)}, u32[]{:S(2)}) collective-permute-start(f32[1,128,128]{2,1,0:T(8,128)S(1)} %get-tuple-element.59), channel_id=1, source_target_pairs={{0,1},{1,2},{2,3},{3,4},{4,5},{5,6},{6,7},{7,8},{8,9},{9,10},{10,1... | collective-permute-start | bytes 196616 | tf_op jit(solution)/shard_map/ppermute | solution.py:24
  149.9 18.2 %collective-permute-done.19 = f32[8,256,128]{2,1,0:T(8,128)} collective-permute-done((f32[8,256,128]{2,1,0:T(8,128)}, f32[8,256,128]{2,1,0:T(8,128)}, u32[]{:S(2)}, u32[]{:S(2)}) %collective-permute-start.19) | collective-permute-done | bytes 1048608 | tf_op jit(solution)/shard_map/ppermute | solution.py:36
  173.4 11.0 %collective-permute-start.21 = (f32[1,128,128]{2,1,0:T(8,128)S(1)}, f32[1,128,128]{2,1,0:T(8,128)S(1)}, u32[]{:S(2)}, u32[]{:S(2)}) collective-permute-start(f32[1,128,128]{2,1,0:T(8,128)S(1)} %get-tuple-element.57), channel_id=1, source_target_pairs={{0,1},{1,2},{2,3},{3,4},{4,5},{5,6},{6,7},{7,8},{8,9},{9,10},{10,1... | collective-permute-start | bytes 196616 | tf_op jit(solution)/shard_map/ppermute | solution.py:24
  188.1 5.8 %collective-permute-start.23 = (f32[1,128,128]{2,1,0:T(8,128)S(1)}, f32[1,128,128]{2,1,0:T(8,128)S(1)}, u32[]{:S(2)}, u32[]{:S(2)}) collective-permute-start(f32[1,128,128]{2,1,0:T(8,128)S(1)} %get-tuple-element.55), channel_id=1, source_target_pairs={{0,1},{1,2},{2,3},{3,4},{4,5},{5,6},{6,7},{7,8},{8,9},{9,10},{10,1... | collective-permute-start | bytes 196616 | tf_op jit(solution)/shard_map/ppermute | solution.py:24
  201.8 18.6 %collective-permute-done.24 = f32[8,256,128]{2,1,0:T(8,128)} collective-permute-done((f32[8,256,128]{2,1,0:T(8,128)}, f32[8,256,128]{2,1,0:T(8,128)}, u32[]{:S(2)}, u32[]{:S(2)}) %collective-permute-start.24) | collective-permute-done | bytes 1048608 | tf_op jit(solution)/shard_map/ppermute | solution.py:36
  225.6 10.5 %collective-permute-start.26 = (f32[1,128,128]{2,1,0:T(8,128)S(1)}, f32[1,128,128]{2,1,0:T(8,128)S(1)}, u32[]{:S(2)}, u32[]{:S(2)}) collective-permute-start(f32[1,128,128]{2,1,0:T(8,128)S(1)} %get-tuple-element.53), channel_id=1, source_target_pairs={{0,1},{1,2},{2,3},{3,4},{4,5},{5,6},{6,7},{7,8},{8,9},{9,10},{10,1... | collective-permute-start | bytes 196616 | tf_op jit(solution)/shard_map/ppermute | solution.py:24
  239.8 5.8 %collective-permute-start.28 = (f32[1,128,128]{2,1,0:T(8,128)S(1)}, f32[1,128,128]{2,1,0:T(8,128)S(1)}, u32[]{:S(2)}, u32[]{:S(2)}) collective-permute-start(f32[1,128,128]{2,1,0:T(8,128)S(1)} %get-tuple-element.51), channel_id=1, source_target_pairs={{0,1},{1,2},{2,3},{3,4},{4,5},{5,6},{6,7},{7,8},{8,9},{9,10},{10,1... | collective-permute-start | bytes 196616 | tf_op jit(solution)/shard_map/ppermute | solution.py:24
  253.7 18.9 %collective-permute-done.29 = f32[8,256,128]{2,1,0:T(8,128)} collective-permute-done((f32[8,256,128]{2,1,0:T(8,128)}, f32[8,256,128]{2,1,0:T(8,128)}, u32[]{:S(2)}, u32[]{:S(2)}) %collective-permute-start.29) | collective-permute-done | bytes 1048608 | tf_op jit(solution)/shard_map/ppermute | solution.py:36
  278.0 10.2 %collective-permute-start.31 = (f32[1,128,128]{2,1,0:T(8,128)S(1)}, f32[1,128,128]{2,1,0:T(8,128)S(1)}, u32[]{:S(2)}, u32[]{:S(2)}) collective-permute-start(f32[1,128,128]{2,1,0:T(8,128)S(1)} %get-tuple-element.49), channel_id=1, source_target_pairs={{0,1},{1,2},{2,3},{3,4},{4,5},{5,6},{6,7},{7,8},{8,9},{9,10},{10,1... | collective-permute-start | bytes 196616 | tf_op jit(solution)/shard_map/ppermute | solution.py:24
  292.0 5.8 %collective-permute-start.33 = (f32[1,128,128]{2,1,0:T(8,128)S(1)}, f32[1,128,128]{2,1,0:T(8,128)S(1)}, u32[]{:S(2)}, u32[]{:S(2)}) collective-permute-start(f32[1,128,128]{2,1,0:T(8,128)S(1)} %get-tuple-element.47), channel_id=1, source_target_pairs={{0,1},{1,2},{2,3},{3,4},{4,5},{5,6},{6,7},{7,8},{8,9},{9,10},{10,1... | collective-permute-start | bytes 196616 | tf_op jit(solution)/shard_map/ppermute | solution.py:24
  301.0 5.4 %collective-permute-start.34 = (f32[8,256,128]{2,1,0:T(8,128)}, f32[8,256,128]{2,1,0:T(8,128)}, u32[]{:S(2)}, u32[]{:S(2)}) collective-permute-start(f32[8,256,128]{2,1,0:T(8,128)} %add.445), channel_id=1, source_target_pairs={{0,32},{32,64},{64,96},{96,128},{128,160},{160,192},{192,224},{1,3... | collective-permute-start | bytes 3145736 | tf_op jit(solution)/shard_map/ppermute | solution.py:36
  306.4 18.8 %collective-permute-done.34 = f32[8,256,128]{2,1,0:T(8,128)} collective-permute-done((f32[8,256,128]{2,1,0:T(8,128)}, f32[8,256,128]{2,1,0:T(8,128)}, u32[]{:S(2)}, u32[]{:S(2)}) %collective-permute-start.34) | collective-permute-done | bytes 1048608 | tf_op jit(solution)/shard_map/ppermute | solution.py:36
  330.4 10.3 %collective-permute-start.36 = (f32[1,128,128]{2,1,0:T(8,128)S(1)}, f32[1,128,128]{2,1,0:T(8,128)S(1)}, u32[]{:S(2)}, u32[]{:S(2)}) collective-permute-start(f32[1,128,128]{2,1,0:T(8,128)S(1)} %get-tuple-element.45), channel_id=1, source_target_pairs={{0,1},{1,2},{2,3},{3,4},{4,5},{5,6},{6,7},{7,8},{8,9},{9,10},{10,1... | collective-permute-start | bytes 196616 | tf_op jit(solution)/shard_map/ppermute | solution.py:24
  344.4 5.8 %collective-permute-start.38 = (f32[1,128,128]{2,1,0:T(8,128)S(1)}, f32[1,128,128]{2,1,0:T(8,128)S(1)}, u32[]{:S(2)}, u32[]{:S(2)}) collective-permute-start(f32[1,128,128]{2,1,0:T(8,128)S(1)} %get-tuple-element.43), channel_id=1, source_target_pairs={{0,1},{1,2},{2,3},{3,4},{4,5},{5,6},{6,7},{7,8},{8,9},{9,10},{10,1... | collective-permute-start | bytes 196616 | tf_op jit(solution)/shard_map/ppermute | solution.py:24
  353.4 5.4 %collective-permute-start.39 = (f32[8,256,128]{2,1,0:T(8,128)}, f32[8,256,128]{2,1,0:T(8,128)}, u32[]{:S(2)}, u32[]{:S(2)}) collective-permute-start(f32[8,256,128]{2,1,0:T(8,128)} %add.454), channel_id=1, source_target_pairs={{0,32},{32,64},{64,96},{96,128},{128,160},{160,192},{192,224},{1,3... | collective-permute-start | bytes 3145736 | tf_op jit(solution)/shard_map/ppermute | solution.py:36
  358.8 18.8 %collective-permute-done.39 = f32[8,256,128]{2,1,0:T(8,128)} collective-permute-done((f32[8,256,128]{2,1,0:T(8,128)}, f32[8,256,128]{2,1,0:T(8,128)}, u32[]{:S(2)}, u32[]{:S(2)}) %collective-permute-start.39) | collective-permute-done | bytes 1048608 | tf_op jit(solution)/shard_map/ppermute | solution.py:36
  382.8 10.3 %collective-permute-start.41 = (f32[1,128,128]{2,1,0:T(8,128)S(1)}, f32[1,128,128]{2,1,0:T(8,128)S(1)}, u32[]{:S(2)}, u32[]{:S(2)}) collective-permute-start(f32[1,128,128]{2,1,0:T(8,128)S(1)} %get-tuple-element.41), channel_id=1, source_target_pairs={{0,1},{1,2},{2,3},{3,4},{4,5},{5,6},{6,7},{7,8},{8,9},{9,10},{10,1... | collective-permute-start | bytes 196616 | tf_op jit(solution)/shard_map/ppermute | solution.py:24
  396.8 5.8 %collective-permute-start.43 = (f32[1,128,128]{2,1,0:T(8,128)S(1)}, f32[1,128,128]{2,1,0:T(8,128)S(1)}, u32[]{:S(2)}, u32[]{:S(2)}) collective-permute-start(f32[1,128,128]{2,1,0:T(8,128)S(1)} %get-tuple-element.39), channel_id=1, source_target_pairs={{0,1},{1,2},{2,3},{3,4},{4,5},{5,6},{6,7},{7,8},{8,9},{9,10},{10,1... | collective-permute-start | bytes 196616 | tf_op jit(solution)/shard_map/ppermute | solution.py:24
  404.8 5.4 %collective-permute-start.44 = (f32[8,256,128]{2,1,0:T(8,128)S(1)}, f32[8,256,128]{2,1,0:T(8,128)}, u32[]{:S(2)}, u32[]{:S(2)}) collective-permute-start(f32[8,256,128]{2,1,0:T(8,128)S(1)} %add.463), channel_id=1, source_target_pairs={{0,32},{32,64},{64,96},{96,128},{128,160},{160,192},{192,224},{1,3... | collective-permute-start | bytes 3145736 | tf_op jit(solution)/shard_map/ppermute | solution.py:36
  410.2 18.4 %collective-permute-done.44 = f32[8,256,128]{2,1,0:T(8,128)} collective-permute-done((f32[8,256,128]{2,1,0:T(8,128)S(1)}, f32[8,256,128]{2,1,0:T(8,128)}, u32[]{:S(2)}, u32[]{:S(2)}) %collective-permute-start.44) | collective-permute-done | bytes 1048608 | tf_op jit(solution)/shard_map/ppermute | solution.py:36
  434.8 10.3 %collective-permute-start.46 = (f32[1,128,128]{2,1,0:T(8,128)S(1)}, f32[1,128,128]{2,1,0:T(8,128)S(1)}, u32[]{:S(2)}, u32[]{:S(2)}) collective-permute-start(f32[1,128,128]{2,1,0:T(8,128)S(1)} %get-tuple-element.37), channel_id=1, source_target_pairs={{0,1},{1,2},{2,3},{3,4},{4,5},{5,6},{6,7},{7,8},{8,9},{9,10},{10,1... | collective-permute-start | bytes 196616 | tf_op jit(solution)/shard_map/ppermute | solution.py:24
  448.8 5.8 %collective-permute-start.48 = (f32[1,128,128]{2,1,0:T(8,128)S(1)}, f32[1,128,128]{2,1,0:T(8,128)S(1)}, u32[]{:S(2)}, u32[]{:S(2)}) collective-permute-start(f32[1,128,128]{2,1,0:T(8,128)S(1)} %get-tuple-element.35), channel_id=1, source_target_pairs={{0,1},{1,2},{2,3},{3,4},{4,5},{5,6},{6,7},{7,8},{8,9},{9,10},{10,1... | collective-permute-start | bytes 196616 | tf_op jit(solution)/shard_map/ppermute | solution.py:24
  459.0 29.5 %collective-permute-done.49 = f32[8,256,128]{2,1,0:T(8,128)S(1)} collective-permute-done((f32[8,256,128]{2,1,0:T(8,128)}, f32[8,256,128]{2,1,0:T(8,128)S(1)}, u32[]{:S(2)}, u32[]{:S(2)}) %collective-permute-start.49) | collective-permute-done | bytes 1048608 | tf_op jit(solution)/shard_map/ppermute | solution.py:36
  (257 shorter events, 160.3 us)
Async XLA Ops:
  3.0 21.7 %collective-permute-start = (f32[2,2,256,128]{3,2,1,0:T(8,128)}, f32[2,2,256,128]{3,2,1,0:T(8,128)}, u32[]{:S(2)}, u32[]{:S(2)}) collective-permute-start(f32[2,2,256,128]{3,2,1,0:T(8,128)} %get-tuple-element.21), channel_id=1, source_target_pairs={{0,1},{1,2},{2,3},{3,4},{4,5},{5,6},{6,7},{7,8},{8,9},{9,10},{10,1... | collective-permute-start | bytes 1572872 | tf_op jit(solution)/shard_map/ppermute | solution.py:24
  9.0 20.8 %collective-permute-start.1 = (f32[2,2,256,128]{3,2,1,0:T(8,128)}, f32[2,2,256,128]{3,2,1,0:T(8,128)}, u32[]{:S(2)}, u32[]{:S(2)}) collective-permute-start(f32[2,2,256,128]{3,2,1,0:T(8,128)} %get-tuple-element.22), channel_id=1, source_target_pairs={{1,0},{2,1},{3,2},{4,3},{5,4},{6,5},{7,6},{8,7},{9,8},{10,9},{11,1... | collective-permute-start | bytes 1572872 | tf_op jit(solution)/shard_map/ppermute | solution.py:26
  11.7 23.8 %collective-permute-start.6 = (f32[1,256,128]{2,1,0:T(8,128)}, f32[1,256,128]{2,1,0:T(8,128)}, u32[]{:S(2)}, u32[]{:S(2)}) collective-permute-start(f32[1,256,128]{2,1,0:T(8,128)} %get-tuple-element.34), channel_id=1, source_target_pairs={{1,0},{2,1},{3,2},{4,3},{5,4},{6,5},{7,6},{8,7},{9,8},{10,9},{11,1... | collective-permute-start | bytes 393224 | tf_op jit(solution)/shard_map/ppermute | solution.py:26
  13.6 21.9 %collective-permute-start.7 = (f32[1,256,128]{2,1,0:T(8,128)}, f32[1,256,128]{2,1,0:T(8,128)}, u32[]{:S(2)}, u32[]{:S(2)}) collective-permute-start(f32[1,256,128]{2,1,0:T(8,128)} %get-tuple-element.33), channel_id=1, source_target_pairs={{0,1},{1,2},{2,3},{3,4},{4,5},{5,6},{6,7},{7,8},{8,9},{9,10},{10,1... | collective-permute-start | bytes 393224 | tf_op jit(solution)/shard_map/ppermute | solution.py:24
  21.9 30.4 %collective-permute-start.2 = (f32[1,128,128]{2,1,0:T(8,128)}, f32[1,128,128]{2,1,0:T(8,128)}, u32[]{:S(2)}, u32[]{:S(2)}) collective-permute-start(f32[1,128,128]{2,1,0:T(8,128)} %get-tuple-element.66), channel_id=1, source_target_pairs={{1,0},{2,1},{3,2},{4,3},{5,4},{6,5},{7,6},{8,7},{9,8},{10,9},{11,1... | collective-permute-start | bytes 196616 | tf_op jit(solution)/shard_map/ppermute | solution.py:26
  24.6 27.7 %collective-permute-start.3 = (f32[1,128,128]{2,1,0:T(8,128)S(1)}, f32[1,128,128]{2,1,0:T(8,128)}, u32[]{:S(2)}, u32[]{:S(2)}) collective-permute-start(f32[1,128,128]{2,1,0:T(8,128)S(1)} %get-tuple-element.65), channel_id=1, source_target_pairs={{0,1},{1,2},{2,3},{3,4},{4,5},{5,6},{6,7},{7,8},{8,9},{9,10},{10,1... | collective-permute-start | bytes 196616 | tf_op jit(solution)/shard_map/ppermute | solution.py:24
  39.0 23.6 %collective-permute-start.8 = (f32[1,256,128]{2,1,0:T(8,128)}, f32[1,256,128]{2,1,0:T(8,128)}, u32[]{:S(2)}, u32[]{:S(2)}) collective-permute-start(f32[1,256,128]{2,1,0:T(8,128)} %get-tuple-element.32), channel_id=1, source_target_pairs={{1,0},{2,1},{3,2},{4,3},{5,4},{6,5},{7,6},{8,7},{9,8},{10,9},{11,1... | collective-permute-start | bytes 393224 | tf_op jit(solution)/shard_map/ppermute | solution.py:26
  40.9 21.7 %collective-permute-start.9 = (f32[1,256,128]{2,1,0:T(8,128)}, f32[1,256,128]{2,1,0:T(8,128)}, u32[]{:S(2)}, u32[]{:S(2)}) collective-permute-start(f32[1,256,128]{2,1,0:T(8,128)} %get-tuple-element.31), channel_id=1, source_target_pairs={{0,1},{1,2},{2,3},{3,4},{4,5},{5,6},{6,7},{7,8},{8,9},{9,10},{10,1... | collective-permute-start | bytes 393224 | tf_op jit(solution)/shard_map/ppermute | solution.py:24
  69.9 9.8 %collective-permute-start.11 = (f32[1,256,128]{2,1,0:T(8,128)S(1)}, f32[1,256,128]{2,1,0:T(8,128)S(1)}, u32[]{:S(2)}, u32[]{:S(2)}) collective-permute-start(f32[1,256,128]{2,1,0:T(8,128)S(1)} %get-tuple-element.29), channel_id=1, source_target_pairs={{0,1},{1,2},{2,3},{3,4},{4,5},{5,6},{6,7},{7,8},{8,9},{9,10},{10,1... | collective-permute-start | bytes 393224 | tf_op jit(solution)/shard_map/ppermute | solution.py:24
  82.9 10.2 %collective-permute-start.13 = (f32[1,256,128]{2,1,0:T(8,128)S(1)}, f32[1,256,128]{2,1,0:T(8,128)S(1)}, u32[]{:S(2)}, u32[]{:S(2)}) collective-permute-start(f32[1,256,128]{2,1,0:T(8,128)S(1)} %get-tuple-element.27), channel_id=1, source_target_pairs={{0,1},{1,2},{2,3},{3,4},{4,5},{5,6},{6,7},{7,8},{8,9},{9,10},{10,1... | collective-permute-start | bytes 393224 | tf_op jit(solution)/shard_map/ppermute | solution.py:24
  95.2 19.5 %collective-permute-start.14 = (f32[8,256,128]{2,1,0:T(8,128)}, f32[8,256,128]{2,1,0:T(8,128)}, u32[]{:S(2)}, u32[]{:S(2)}) collective-permute-start(f32[8,256,128]{2,1,0:T(8,128)} %get-tuple-element.5), channel_id=1, source_target_pairs={{0,32},{32,64},{64,96},{96,128},{128,160},{160,192},{192,224},{1,3... | collective-permute-start | bytes 3145736 | tf_op jit(solution)/shard_map/ppermute | solution.py:36
  118.8 13.0 %collective-permute-start.15 = (f32[1,128,128]{2,1,0:T(8,128)S(1)}, f32[1,128,128]{2,1,0:T(8,128)S(1)}, u32[]{:S(2)}, u32[]{:S(2)}) collective-permute-start(f32[1,128,128]{2,1,0:T(8,128)S(1)} %get-tuple-element.62), channel_id=1, source_target_pairs={{1,0},{2,1},{3,2},{4,3},{5,4},{6,5},{7,6},{8,7},{9,8},{10,9},{11,1... | collective-permute-start | bytes 196616 | tf_op jit(solution)/shard_map/ppermute | solution.py:26
  120.9 12.7 %collective-permute-start.16 = (f32[1,128,128]{2,1,0:T(8,128)S(1)}, f32[1,128,128]{2,1,0:T(8,128)S(1)}, u32[]{:S(2)}, u32[]{:S(2)}) collective-permute-start(f32[1,128,128]{2,1,0:T(8,128)S(1)} %get-tuple-element.61), channel_id=1, source_target_pairs={{0,1},{1,2},{2,3},{3,4},{4,5},{5,6},{6,7},{7,8},{8,9},{9,10},{10,1... | collective-permute-start | bytes 196616 | tf_op jit(solution)/shard_map/ppermute | solution.py:24
  145.3 22.8 %collective-permute-start.19 = (f32[8,256,128]{2,1,0:T(8,128)}, f32[8,256,128]{2,1,0:T(8,128)}, u32[]{:S(2)}, u32[]{:S(2)}) collective-permute-start(f32[8,256,128]{2,1,0:T(8,128)} %add.418), channel_id=1, source_target_pairs={{0,32},{32,64},{64,96},{96,128},{128,160},{160,192},{192,224},{1,3... | collective-permute-start | bytes 3145736 | tf_op jit(solution)/shard_map/ppermute | solution.py:36
  171.4 13.0 %collective-permute-start.20 = (f32[1,128,128]{2,1,0:T(8,128)S(1)}, f32[1,128,128]{2,1,0:T(8,128)S(1)}, u32[]{:S(2)}, u32[]{:S(2)}) collective-permute-start(f32[1,128,128]{2,1,0:T(8,128)S(1)} %get-tuple-element.58), channel_id=1, source_target_pairs={{1,0},{2,1},{3,2},{4,3},{5,4},{6,5},{7,6},{8,7},{9,8},{10,9},{11,1... | collective-permute-start | bytes 196616 | tf_op jit(solution)/shard_map/ppermute | solution.py:26
  173.4 12.3 %collective-permute-start.21 = (f32[1,128,128]{2,1,0:T(8,128)S(1)}, f32[1,128,128]{2,1,0:T(8,128)S(1)}, u32[]{:S(2)}, u32[]{:S(2)}) collective-permute-start(f32[1,128,128]{2,1,0:T(8,128)S(1)} %get-tuple-element.57), channel_id=1, source_target_pairs={{0,1},{1,2},{2,3},{3,4},{4,5},{5,6},{6,7},{7,8},{8,9},{9,10},{10,1... | collective-permute-start | bytes 196616 | tf_op jit(solution)/shard_map/ppermute | solution.py:24
  197.3 23.1 %collective-permute-start.24 = (f32[8,256,128]{2,1,0:T(8,128)}, f32[8,256,128]{2,1,0:T(8,128)}, u32[]{:S(2)}, u32[]{:S(2)}) collective-permute-start(f32[8,256,128]{2,1,0:T(8,128)} %add.427), channel_id=1, source_target_pairs={{0,32},{32,64},{64,96},{96,128},{128,160},{160,192},{192,224},{1,3... | collective-permute-start | bytes 3145736 | tf_op jit(solution)/shard_map/ppermute | solution.py:36
  223.7 12.5 %collective-permute-start.25 = (f32[1,128,128]{2,1,0:T(8,128)S(1)}, f32[1,128,128]{2,1,0:T(8,128)S(1)}, u32[]{:S(2)}, u32[]{:S(2)}) collective-permute-start(f32[1,128,128]{2,1,0:T(8,128)S(1)} %get-tuple-element.54), channel_id=1, source_target_pairs={{1,0},{2,1},{3,2},{4,3},{5,4},{6,5},{7,6},{8,7},{9,8},{10,9},{11,1... | collective-permute-start | bytes 196616 | tf_op jit(solution)/shard_map/ppermute | solution.py:26
  225.6 11.8 %collective-permute-start.26 = (f32[1,128,128]{2,1,0:T(8,128)S(1)}, f32[1,128,128]{2,1,0:T(8,128)S(1)}, u32[]{:S(2)}, u32[]{:S(2)}) collective-permute-start(f32[1,128,128]{2,1,0:T(8,128)S(1)} %get-tuple-element.53), channel_id=1, source_target_pairs={{0,1},{1,2},{2,3},{3,4},{4,5},{5,6},{6,7},{7,8},{8,9},{9,10},{10,1... | collective-permute-start | bytes 196616 | tf_op jit(solution)/shard_map/ppermute | solution.py:24
  248.8 23.7 %collective-permute-start.29 = (f32[8,256,128]{2,1,0:T(8,128)}, f32[8,256,128]{2,1,0:T(8,128)}, u32[]{:S(2)}, u32[]{:S(2)}) collective-permute-start(f32[8,256,128]{2,1,0:T(8,128)} %add.436), channel_id=1, source_target_pairs={{0,32},{32,64},{64,96},{96,128},{128,160},{160,192},{192,224},{1,3... | collective-permute-start | bytes 3145736 | tf_op jit(solution)/shard_map/ppermute | solution.py:36
  275.9 12.4 %collective-permute-start.30 = (f32[1,128,128]{2,1,0:T(8,128)S(1)}, f32[1,128,128]{2,1,0:T(8,128)S(1)}, u32[]{:S(2)}, u32[]{:S(2)}) collective-permute-start(f32[1,128,128]{2,1,0:T(8,128)S(1)} %get-tuple-element.50), channel_id=1, source_target_pairs={{1,0},{2,1},{3,2},{4,3},{5,4},{6,5},{7,6},{8,7},{9,8},{10,9},{11,1... | collective-permute-start | bytes 196616 | tf_op jit(solution)/shard_map/ppermute | solution.py:26
  278.0 11.5 %collective-permute-start.31 = (f32[1,128,128]{2,1,0:T(8,128)S(1)}, f32[1,128,128]{2,1,0:T(8,128)S(1)}, u32[]{:S(2)}, u32[]{:S(2)}) collective-permute-start(f32[1,128,128]{2,1,0:T(8,128)S(1)} %get-tuple-element.49), channel_id=1, source_target_pairs={{0,1},{1,2},{2,3},{3,4},{4,5},{5,6},{6,7},{7,8},{8,9},{9,10},{10,1... | collective-permute-start | bytes 196616 | tf_op jit(solution)/shard_map/ppermute | solution.py:24
  301.0 24.2 %collective-permute-start.34 = (f32[8,256,128]{2,1,0:T(8,128)}, f32[8,256,128]{2,1,0:T(8,128)}, u32[]{:S(2)}, u32[]{:S(2)}) collective-permute-start(f32[8,256,128]{2,1,0:T(8,128)} %add.445), channel_id=1, source_target_pairs={{0,32},{32,64},{64,96},{96,128},{128,160},{160,192},{192,224},{1,3... | collective-permute-start | bytes 3145736 | tf_op jit(solution)/shard_map/ppermute | solution.py:36
  328.4 12.3 %collective-permute-start.35 = (f32[1,128,128]{2,1,0:T(8,128)S(1)}, f32[1,128,128]{2,1,0:T(8,128)S(1)}, u32[]{:S(2)}, u32[]{:S(2)}) collective-permute-start(f32[1,128,128]{2,1,0:T(8,128)S(1)} %get-tuple-element.46), channel_id=1, source_target_pairs={{1,0},{2,1},{3,2},{4,3},{5,4},{6,5},{7,6},{8,7},{9,8},{10,9},{11,1... | collective-permute-start | bytes 196616 | tf_op jit(solution)/shard_map/ppermute | solution.py:26
  330.4 11.6 %collective-permute-start.36 = (f32[1,128,128]{2,1,0:T(8,128)S(1)}, f32[1,128,128]{2,1,0:T(8,128)S(1)}, u32[]{:S(2)}, u32[]{:S(2)}) collective-permute-start(f32[1,128,128]{2,1,0:T(8,128)S(1)} %get-tuple-element.45), channel_id=1, source_target_pairs={{0,1},{1,2},{2,3},{3,4},{4,5},{5,6},{6,7},{7,8},{8,9},{9,10},{10,1... | collective-permute-start | bytes 196616 | tf_op jit(solution)/shard_map/ppermute | solution.py:24
  353.4 24.2 %collective-permute-start.39 = (f32[8,256,128]{2,1,0:T(8,128)}, f32[8,256,128]{2,1,0:T(8,128)}, u32[]{:S(2)}, u32[]{:S(2)}) collective-permute-start(f32[8,256,128]{2,1,0:T(8,128)} %add.454), channel_id=1, source_target_pairs={{0,32},{32,64},{64,96},{96,128},{128,160},{160,192},{192,224},{1,3... | collective-permute-start | bytes 3145736 | tf_op jit(solution)/shard_map/ppermute | solution.py:36
  380.9 12.3 %collective-permute-start.40 = (f32[1,128,128]{2,1,0:T(8,128)S(1)}, f32[1,128,128]{2,1,0:T(8,128)S(1)}, u32[]{:S(2)}, u32[]{:S(2)}) collective-permute-start(f32[1,128,128]{2,1,0:T(8,128)S(1)} %get-tuple-element.42), channel_id=1, source_target_pairs={{1,0},{2,1},{3,2},{4,3},{5,4},{6,5},{7,6},{8,7},{9,8},{10,9},{11,1... | collective-permute-start | bytes 196616 | tf_op jit(solution)/shard_map/ppermute | solution.py:26
  382.8 11.6 %collective-permute-start.41 = (f32[1,128,128]{2,1,0:T(8,128)S(1)}, f32[1,128,128]{2,1,0:T(8,128)S(1)}, u32[]{:S(2)}, u32[]{:S(2)}) collective-permute-start(f32[1,128,128]{2,1,0:T(8,128)S(1)} %get-tuple-element.41), channel_id=1, source_target_pairs={{0,1},{1,2},{2,3},{3,4},{4,5},{5,6},{6,7},{7,8},{8,9},{9,10},{10,1... | collective-permute-start | bytes 196616 | tf_op jit(solution)/shard_map/ppermute | solution.py:24
  404.8 23.8 %collective-permute-start.44 = (f32[8,256,128]{2,1,0:T(8,128)S(1)}, f32[8,256,128]{2,1,0:T(8,128)}, u32[]{:S(2)}, u32[]{:S(2)}) collective-permute-start(f32[8,256,128]{2,1,0:T(8,128)S(1)} %add.463), channel_id=1, source_target_pairs={{0,32},{32,64},{64,96},{96,128},{128,160},{160,192},{192,224},{1,3... | collective-permute-start | bytes 3145736 | tf_op jit(solution)/shard_map/ppermute | solution.py:36
  432.7 12.4 %collective-permute-start.45 = (f32[1,128,128]{2,1,0:T(8,128)S(1)}, f32[1,128,128]{2,1,0:T(8,128)S(1)}, u32[]{:S(2)}, u32[]{:S(2)}) collective-permute-start(f32[1,128,128]{2,1,0:T(8,128)S(1)} %get-tuple-element.38), channel_id=1, source_target_pairs={{1,0},{2,1},{3,2},{4,3},{5,4},{6,5},{7,6},{8,7},{9,8},{10,9},{11,1... | collective-permute-start | bytes 196616 | tf_op jit(solution)/shard_map/ppermute | solution.py:26
  434.8 11.6 %collective-permute-start.46 = (f32[1,128,128]{2,1,0:T(8,128)S(1)}, f32[1,128,128]{2,1,0:T(8,128)S(1)}, u32[]{:S(2)}, u32[]{:S(2)}) collective-permute-start(f32[1,128,128]{2,1,0:T(8,128)S(1)} %get-tuple-element.37), channel_id=1, source_target_pairs={{0,1},{1,2},{2,3},{3,4},{4,5},{5,6},{6,7},{7,8},{8,9},{9,10},{10,1... | collective-permute-start | bytes 196616 | tf_op jit(solution)/shard_map/ppermute | solution.py:24
  457.7 30.8 %collective-permute-start.49 = (f32[8,256,128]{2,1,0:T(8,128)}, f32[8,256,128]{2,1,0:T(8,128)S(1)}, u32[]{:S(2)}, u32[]{:S(2)}) collective-permute-start(f32[8,256,128]{2,1,0:T(8,128)} %add.472), channel_id=1, source_target_pairs={{224,0},{225,1},{226,2},{227,3},{228,4},{229,5},{230,6},{231,7},{2... | collective-permute-start | bytes 3145736 | tf_op jit(solution)/shard_map/ppermute | solution.py:36
  (37 other events, 326.4 us)
where the time goes:
time: 497 us; the launch traced here: 490 us
  starting transfers between devices  228 us (46%)
  waiting for transfers between devices  186 us (37%)
  other arithmetic  62.9 us (13%)
  local copies, waits for them, and re-layouts  11 us (2%)
    ppermute x8, waiting for transfers between devices, shifted(): return lax.ppermute(x, axis, pairs)  158 us
    ppermute x21, starting transfers between devices, with_halo(): lax.ppermute(tail, axis, [(i, (i + 1) % count) for i in range(ends)])  153 us
    ppermute x21, starting transfers between devices, with_halo(): lax.ppermute(head, axis, [((i + 1) % count, i) for i in range(ends)])  40.8 us
    ppermute x8, starting transfers between devices, shifted(): return lax.ppermute(x, axis, pairs)  33.8 us
    ppermute x21, waiting for transfers between devices, with_halo(): lax.ppermute(tail, axis, [(i, (i + 1) % count) for i in range(ends)])  27.2 us
    reduce_sum x10, other arithmetic, restrict(): return jnp.mean(folded, axis=(-4, -2))  17.8 us
  transfers between devices with their start and end apart: 50, of which 27 were waited for; matrix products, arithmetic and copies ran while one was open for 5% of the time, Pallas kernels for 0%

commit v1 on v0

v1 whole, which is shorter than its diff:
```python
import jax
import jax.numpy as jnp
from jax import lax
from jax.experimental import pallas as pl
from jax.experimental.pallas import tpu as pltpu
from jax.sharding import Mesh, PartitionSpec as P

SIZES = (4, 2, 8, 2, 2)
AXES = ("y", "l", "z", "h", "c")
SLABS = 8
ROWS = 8
NY = 256
NZ = 128
HALF = ROWS // 2
CY = NY // 2
PAD = 8
CHUNK = 64
FINE = 0.15
COARSE = 0.3
TABLE = (1.0, 0.72, 0.52, 0.37, 0.26, 0.18, 0.13, 0.09)

BLOCKS = 16
YB = CY // BLOCKS
YM = 16
YW = YB + 2 * YM
XH = 14
XW = 12 + 2 * XH
XALL = 16 + 2 * XH
KEEP = (8, 8, 6, 4, 4, 4, 2, 8)
STARTS = tuple(sum(KEEP[:i]) for i in range(len(KEEP)))
NKEEP = sum(KEEP)

EK, EU, E1, EKC, EUC, E1C, EDGE = 0, 256, 512, 768, 896, 1024, 1152

F32 = jnp.float32


def up_lane(x):
    return pltpu.roll(x, NZ - 1, axis=x.ndim - 1)


def down_lane(x):
    return pltpu.roll(x, 1, axis=x.ndim - 1)


def lanes(shape):
    return lax.broadcasted_iota(jnp.int32, shape, len(shape) - 1)


def lookup(material):
    result = jnp.zeros(material.shape, F32)
    for number in range(8):
        result = jnp.where(material == number, F32(TABLE[number]), result)
    return result


def z_faces(k, weight):
    lane = lanes(k.shape)
    upper = jnp.where(lane == NZ - 1, 0.0, up_lane(k))
    lower = jnp.where(lane == 0, 0.0, down_lane(k))
    above = weight * (k + upper)
    below = weight * (k + lower)
    return jnp.where(lane == NZ - 1, 0.0, above), above + below


def coefficients(kp, r, a, n, wx, wy, wz, below, above):
    k = kp[r, PAD + a : PAD + a + n]
    cyp = wy * (k + kp[r, PAD + a + 1 : PAD + a + n + 1])
    cym = wy * (k + kp[r, PAD + a - 1 : PAD + a + n - 1])
    cz, zsum = z_faces(k, wz)
    diag = 1.0 - (cyp + cym + zsum)
    cx = None
    if below:
        diag = diag - wx * (k + kp[r - 1, PAD + a : PAD + a + n])
    if above:
        cx = wx * (k + kp[r + 1, PAD + a : PAD + a + n])
        diag = diag - cx
    return cx, cyp, cym, cz, diag


def base(u, r, a, n, cx, cyp, cym, cz, diag, below, above):
    here = u[r, PAD + a : PAD + a + n]
    s = slice(a, a + n)
    new = diag[r, s] * here
    new = new + cyp[r, s] * u[r, PAD + a + 1 : PAD + a + n + 1]
    new = new + cym[r, s] * u[r, PAD + a - 1 : PAD + a + n - 1]
    c = cz[r, s]
    new = new + c * up_lane(here) + down_lane(c * here)
    if below:
        new = new + cx[r - 1, s] * u[r - 1, PAD + a : PAD + a + n]
    if above:
        new = new + cx[r, s] * u[r + 1, PAD + a : PAD + a + n]
    return new


def each_row(count, visit):
    visit(0, False, True)

    def body(r, carry):
        visit(r, True, True)
        return carry

    lax.fori_loop(1, count - 1, body, 0)
    visit(count - 1, True, False)


def pieces(width):
    return [(a, CHUNK) for a in range(0, width, CHUNK)]


def clear_margin(ref, width):
    rows = ref.shape[0]
    ref[:, 0:PAD] = jnp.zeros((rows, PAD, NZ), F32)
    ref[:, PAD + width : PAD + width + PAD] = jnp.zeros((rows, PAD, NZ), F32)


def halve(ref, x, margin):
    total = None
    for p in range(2):
        for q in range(2):
            part = ref[2 * x + p, pl.ds(margin + q, CY, 2), :]
            total = part if total is None else total + part
    return 0.25 * total


def first_kernel(pos, u_in, mat, src, sc, so, cx, cyp, cym, cz, dg, ccx, ccyp, ccym, ccz, cdg, kc_out, kp, up, kcp, ucp, edge):
    clear_margin(kp, NY)
    clear_margin(up, NY)
    clear_margin(kcp, CY)
    clear_margin(ucp, CY)

    def fill(r, carry):
        for a, n in pieces(NY):
            kp[r, PAD + a : PAD + a + n] = lookup(mat[r, a : a + n])
            up[r, PAD + a : PAD + a + n] = u_in[0, r, a : a + n]
        return carry

    lax.fori_loop(0, ROWS, fill, 0)
    for x in range(HALF):
        kcp[x, PAD : PAD + CY] = halve(kp, x, PAD)
        ucp[x, PAD : PAD + CY] = halve(up, x, PAD)
        kc_out[x] = kcp[x, PAD : PAD + CY]

    def fine(r, below, above):
        for a, n in pieces(NY):
            s = slice(a, a + n)
            fx, cyp[r, s], cym[r, s], cz[r, s], dg[r, s] = coefficients(kp, r, a, n, 0.5 * FINE, 0.5 * FINE, 0.5 * FINE, below, above)
            if above:
                cx[r, s] = fx

    each_row(ROWS, fine)

    def coarse(r, below, above):
        for a, n in pieces(CY):
            s = slice(a, a + n)
            fx, ccyp[r, s], ccym[r, s], ccz[r, s], cdg[r, s] = coefficients(
                kcp, r, a, n, 0.125 * COARSE, 0.125 * COARSE, 0.5 * COARSE, below, above
            )
            if above:
                ccx[r, s] = fx

    each_row(HALF, coarse)
    for side, r, x in ((0, 0, 0), (1, ROWS - 1, HALF - 1)):
        for a, n in pieces(NY):
            edge[side, EK + a : EK + a + n] = kp[r, PAD + a : PAD + a + n]
            edge[side, EU + a : EU + a + n] = up[r, PAD + a : PAD + a + n]
            edge[side, E1 + a : E1 + a + n] = base(up, r, a, n, cx, cyp, cym, cz, dg, side == 1, side == 0) + FINE * src[r, a : a + n]
        for a, n in pieces(CY):
            edge[side, EKC + a : EKC + a + n] = kcp[x, PAD + a : PAD + a + n]
            edge[side, EUC + a : EUC + a + n] = ucp[x, PAD + a : PAD + a + n]
            edge[side, E1C + a : E1C + a + n] = base(ucp, x, a, n, ccx, ccyp, ccym, ccz, cdg, side == 1, side == 0)
    c = pos[4]
    sc[...] = edge[1 - c]
    so[...] = edge[c]


def two_sweeps(a_ref, b_ref, halo, later, face, live, rows, width, coefs, source):
    def one(src_ref, dst_ref, planes):
        def visit(r, below, above):
            for a, n in pieces(width):
                new = base(src_ref, r, a, n, *coefs, below, above)
                if source is not None:
                    new = new + FINE * source[r, a : a + n]
                here = src_ref[r, PAD + a : PAD + a + n]
                if not below:
                    new = new + face(0, a, n) * (planes(0, a, n) - here)
                if not above:
                    new = new + face(1, a, n) * (planes(1, a, n) - here)
                dst_ref[r, PAD + a : PAD + a + n] = new

        each_row(rows, visit)

    def second(side, a, n):
        r = 0 if side == 0 else rows - 1
        flux = face(side, a, n) * (a_ref[r, PAD + a : PAD + a + n] - halo(side, a, n))
        return live[side] * (later(side, a, n) + flux)

    def kept(store):
        def write(side):
            for a, n in pieces(width):
                store[side, a : a + n] = second(side, a, n)

        return write

    return one, kept


def run_two(a_ref, b_ref, store, halo, later, face, live, rows, width, coefs, source):
    one, kept = two_sweeps(a_ref, b_ref, halo, later, face, live, rows, width, coefs, source)
    one(a_ref, b_ref, halo)
    kept(store)(0)
    kept(store)(1)
    one(b_ref, a_ref, lambda side, a, n: store[side, a : a + n])


def lives(pos):
    place = (pos[2] * 2 + pos[3]) * 2 + pos[4]
    return jnp.where(place > 0, F32(1), F32(0)), jnp.where(place < 31, F32(1), F32(0))


def second_kernel(
    pos, u_in, src, sc, so, rc, ro, cx, cyp, cym, cz, dg, ccx, ccyp, ccym, ccz, cdg,
    u_out, faces, au, tc, to, ua, ub, ca, cb, own, got, store, edge,
):
    c = pos[4]
    live = lives(pos)
    for ref in (ua, ub):
        clear_margin(ref, NY)
    for ref in (ca, cb):
        clear_margin(ref, CY)
    own[1 - c] = sc[...]
    own[c] = so[...]
    got[1 - c] = rc[...]
    got[c] = ro[...]
    for side in range(2):
        got[side] = got[side] * live[side]

    def fill(r, carry):
        for a, n in pieces(NY):
            ua[r, PAD + a : PAD + a + n] = u_in[0, r, a : a + n]
        return carry

    lax.fori_loop(0, ROWS, fill, 0)
    for x in range(HALF):
        ca[x, PAD : PAD + CY] = halve(ua, x, PAD)
    for side in range(2):
        for a, n in pieces(NY):
            faces[side, a : a + n] = (0.5 * FINE) * (own[side, EK + a : EK + a + n] + got[side, EK + a : EK + a + n])

    def plane(offset):
        return lambda side, a, n: got[side, offset + a : offset + a + n]

    def coarse_face(side, a, n):
        return (0.125 * COARSE) * (own[side, EKC + a : EKC + a + n] + got[side, EKC + a : EKC + a + n])

    run_two(
        ua, ub, store, plane(EU), plane(E1), lambda side, a, n: faces[side, a : a + n],
        live, ROWS, NY, (cx, cyp, cym, cz, dg), src,
    )
    for side, r in ((0, 0), (1, ROWS - 1)):
        for a, n in pieces(NY):
            edge[side, a : a + n] = ua[r, PAD + a : PAD + a + n]
            edge[side, NY + a : NY + a + n] = base(ua, r, a, n, cx, cyp, cym, cz, dg, side == 1, side == 0) + FINE * src[r, a : a + n]
    tc[...] = edge[1 - c]
    to[...] = edge[c]
    u_out[...] = ua[...]
    run_two(
        ca, cb, store, plane(EUC), plane(E1C), coarse_face,
        live, HALF, CY, (ccx, ccyp, ccym, ccz, cdg), None,
    )
    for x in range(HALF):
        au[x] = ca[x, PAD : PAD + CY]


def third_kernel(pos, u_in, src, faces, rc, ro, au, kc, cx, cyp, cym, cz, dg, h_out, strips, ua, ub, got, store, wp):
    c = pos[4]
    slab = pos[0] * 2 + pos[1]
    live = lives(pos)
    ua[...] = u_in[...]
    clear_margin(ub, NY)
    got[1 - c] = rc[...]
    got[c] = ro[...]
    for side in range(2):
        got[side] = got[side] * live[side]
    run_two(
        ua, ub, store,
        lambda side, a, n: got[side, a : a + n],
        lambda side, a, n: got[side, NY + a : NY + a + n],
        lambda side, a, n: faces[side, a : a + n],
        live, ROWS, NY, (cx, cyp, cym, cz, dg), src,
    )
    keep = jnp.where(slab > 0, F32(1), F32(0))
    wp[:, 0:YM] = jnp.zeros((HALF, YM, NZ), F32)
    wp[:, YM + CY : YM + CY + YM] = jnp.zeros((HALF, YM, NZ), F32)
    last = slab == SLABS - 1
    for x in range(HALF):
        coarse = keep * au[x]
        total = None
        for p in range(2):
            for q in range(2):
                part = ua[2 * x + p, pl.ds(PAD + q, CY, 2), :] - coarse
                h_out[2 * x + p, pl.ds(q, CY, 2), :] = part
                total = part if total is None else total + part
        wp[x, YM : YM + CY] = jnp.where(last, kc[x], 0.25 * total)
    for b in range(BLOCKS):
        strips[b] = wp[:, b * YB : b * YB + YW]


def pack_kernel(pos, own, even, odd):
    up = 1 - lax.rem(pos[2], 2)
    for j in range(SLABS):
        n = KEEP[j]
        even[STARTS[j] : STARTS[j] + n] = own[j, pl.ds(up * (8 - n), n)]
        odd[STARTS[j] : STARTS[j] + n] = own[j, pl.ds((1 - up) * (8 - n), n)]


def chain_kernel(pos, own, part, even, odd, peven, podd, out, w, ea, eb, cx, cyp, cym, cz, dg, kp):
    c = pos[4]
    z = pos[2]
    block = (pos[0] * 2 + pos[1]) * 2 + pos[3]
    is_up = 1 - lax.rem(z, 2)
    low = jnp.where(z > 0, F32(1), F32(0))
    high = jnp.where(z < 7, F32(1), F32(0))
    w[...] = jnp.zeros(w.shape, F32)
    for j in range(SLABS):
        for i in range(8):
            row = XH + 8 * (i // 4) + i % 4
            w[j, row + 4 * c] = own[j, i]
            w[j, row + 4 * (1 - c)] = part[j, i]
    for (e_ref, o_ref, core) in ((even, odd, c), (peven, podd, 1 - c)):
        for j in range(SLABS):
            n = KEEP[j]
            for t in range(n):
                i_low = 8 - n + t
                r_low = XH + 8 * (i_low // 4) + i_low % 4 - 16
                r_high = XH + 8 * (t // 4) + t % 4 + 16
                src = STARTS[j] + t
                from_even = e_ref[src]
                from_odd = o_ref[src]
                below = jnp.where(is_up == 1, from_odd, from_even) * low
                above = jnp.where(is_up == 1, from_even, from_odd) * high
                row = r_low + 4 * core

                @pl.when(row >= 0)
                def _():
                    w[j, jnp.maximum(row, 0)] = below

                row2 = r_high + 4 * core

                @pl.when(row2 < XALL)
                def _():
                    w[j, jnp.minimum(row2, XALL - 1)] = above

    first = 4 * c
    kp[...] = jnp.zeros(kp.shape, F32)
    ea[...] = jnp.zeros(ea.shape, F32)
    eb[...] = jnp.zeros(eb.shape, F32)
    ycell = block * YB - YM + lax.broadcasted_iota(jnp.int32, (YW, NZ), 0)
    ymask = jnp.where((ycell >= 0) & (ycell < CY), F32(1), F32(0))

    def fill(r, carry):
        kp[r, PAD : PAD + YW] = w[7, first + r]
        ea[r, PAD : PAD + YW] = w[0, first + r]
        return carry

    lax.fori_loop(0, XW, fill, 0)
    wx = 0.125 * COARSE
    wz = 0.5 * COARSE

    def coef(r, carry):
        k = kp[r, PAD : PAD + YW]
        kup = kp[r + 1, PAD : PAD + YW]
        kdn = kp[jnp.maximum(r - 1, 0), PAD : PAD + YW]
        a = wx * (k + kp[r, PAD + 1 : PAD + YW + 1])
        b = wx * (k + kp[r, PAD - 1 : PAD + YW - 1])
        zc, zsum = z_faces(k, wz)
        above = wx * (k + kup)
        below = wx * (k + kdn)
        row = 16 * z + 4 * c - XH + r
        inside = jnp.where((row >= 0) & (row < CY), F32(1), F32(0))
        m = ymask * inside
        cyp[r] = a * m
        cym[r] = b * m
        cz[r] = zc * m
        cx[r, 0] = below * m
        cx[r, 1] = above * m
        dg[r] = (1.0 - (a + b + zsum + above + below)) * m
        return carry

    lax.fori_loop(0, XW, coef, 0)

    def sweep(src, dst, lo, hi, add=None):
        def body(r, carry):
            here = src[r, PAD : PAD + YW]
            new = dg[r] * here
            new = new + cyp[r] * src[r, PAD + 1 : PAD + YW + 1]
            new = new + cym[r] * src[r, PAD - 1 : PAD + YW - 1]
            zc = cz[r]
            new = new + zc * up_lane(here) + down_lane(zc * here)
            new = new + cx[r, 0] * src[r - 1, PAD : PAD + YW]
            new = new + cx[r, 1] * src[r + 1, PAD : PAD + YW]
            dst[r, PAD : PAD + YW] = new
            return carry

        lax.fori_loop(lo, hi, body, 0)

    out[2:4] = jnp.zeros((2, HALF, YB, NZ), F32)
    for k in range(1, 8):
        done = 2 * (k - 1)
        sweep(ea, eb, done + 1, XW - done - 1)
        sweep(eb, ea, done + 2, XW - done - 2)
        m = (k + 1) % SLABS
        for side in range(2):
            for i in range(HALF):
                out[2 * m + side, i] = ea[XH + 8 * side + i, PAD + YM : PAD + YM + YB]
        if k < 7:
            def add(r, carry):
                ea[r, PAD : PAD + YW] = ea[r, PAD : PAD + YW] + w[k, first + r]
                return carry

            lax.fori_loop(done + 2, XW - done - 2, add, 0)


def last_kernel(h_in, y_in, out):
    for x in range(HALF):
        fix = y_in[:, x].reshape(CY, NZ)
        for p in range(2):
            for q in range(2):
                out[0, 2 * x + p, pl.ds(q, CY, 2), :] = h_in[2 * x + p, pl.ds(q, CY, 2), :] + fix


def shape(*dims):
    return jax.ShapeDtypeStruct(dims, F32)


def call(kernel, outs, scratch, count, with_pos=True):
    vmem = pl.BlockSpec(memory_space=pltpu.VMEM)
    smem = pl.BlockSpec(memory_space=pltpu.SMEM)
    return pl.pallas_call(
        kernel,
        out_shape=outs,
        in_specs=([smem] if with_pos else []) + [vmem] * count,
        out_specs=jax.tree.map(lambda _: vmem, outs),
        scratch_shapes=[pltpu.VMEM(s, F32) for s in scratch],
    )


def pairs(n, odd):
    found = []
    for i in range(odd, n - 1, 2):
        found += [(i, i + 1), (i + 1, i)]
    if odd:
        found += [(0, n - 1), (n - 1, 0)]
    return found


SPACE = ("z", "h", "c")
PLANE = ("y", "l", "h")


def local(starts, material, source):
    pos = jnp.stack([lax.axis_index(a) for a in AXES]).astype(jnp.int32)
    fine = shape(ROWS, NY, NZ)
    crs = shape(HALF, CY, NZ)
    padded = (ROWS, NY + 2 * PAD, NZ)
    cpad = (HALF, CY + 2 * PAD, NZ)

    def swap_c(x):
        return lax.ppermute(x, "c", pairs(2, 0))

    def swap_o(x):
        return lax.ppermute(x, SPACE, pairs(32, 1))

    sc, so, cx, cyp, cym, cz, dg, ccx, ccyp, ccym, ccz, cdg, kc = call(
        first_kernel,
        (shape(EDGE, NZ), shape(EDGE, NZ), fine, fine, fine, fine, fine, crs, crs, crs, crs, crs, crs),
        (padded, padded, cpad, cpad, (2, EDGE, NZ)),
        3,
    )(pos, starts, material, source)
    ro = swap_o(so)
    rc = swap_c(sc)
    u2, faces, au, tc, to = call(
        second_kernel,
        (shape(*padded), shape(2, NY, NZ), crs, shape(2 * NY, NZ), shape(2 * NY, NZ)),
        (padded, padded, cpad, cpad, (2, EDGE, NZ), (2, EDGE, NZ), (2, NY, NZ), (2, 2 * NY, NZ)),
        16,
    )(pos, starts, source, sc, so, rc, ro, cx, cyp, cym, cz, dg, ccx, ccyp, ccym, ccz, cdg)
    ro2 = swap_o(to)
    rc2 = swap_c(tc)
    moved, strips = call(
        third_kernel,
        (fine, shape(BLOCKS, HALF, YW, NZ)),
        (padded, padded, (2, 2 * NY, NZ), (2, NY, NZ), (HALF, CY + 2 * YM, NZ)),
        12,
    )(pos, u2, source, faces, rc2, ro2, au, kc, cx, cyp, cym, cz, dg)
    own = lax.all_to_all(strips, PLANE, 0, 0, tiled=True)
    own, moved = lax.optimization_barrier((own, moved))
    own = own.reshape(SLABS, 8, YW, NZ)
    even, odd = call(pack_kernel, (shape(NKEEP, YW, NZ), shape(NKEEP, YW, NZ)), (), 1)(pos, own)
    moved = lax.ppermute(moved, ("y", "l"), [(i, (i + 1) % 8) for i in range(8)])
    even = lax.ppermute(even, "z", pairs(8, 0))
    odd = lax.ppermute(odd, "z", pairs(8, 1))
    part = swap_c(own)
    peven = swap_c(even)
    podd = swap_c(odd)
    dom = (XW + 1, YW + 2 * PAD, NZ)
    (fixes,) = call(
        chain_kernel,
        (shape(BLOCKS, HALF, YB, NZ),),
        (
            (SLABS, XALL, YW, NZ), dom, dom, (XW, 2, YW, NZ), (XW, YW, NZ), (XW, YW, NZ), (XW, YW, NZ), (XW, YW, NZ), dom,
        ),
        6,
    )(pos, own, part, even, odd, peven, podd)
    fixes = lax.all_to_all(fixes, PLANE, 0, 0, tiled=True)
    (result,) = call(last_kernel, (shape(1, ROWS, NY, NZ),), (), 2, with_pos=False)(moved, fixes)
    return result


def solution(mesh):
    refined = Mesh(mesh.devices.reshape(SIZES), AXES)
    in_specs = (P(("y", "l"), SPACE, None, None), P(SPACE, None, None), P(SPACE, None, None))
    out_specs = P(("y", "l"), SPACE, None, None)
    return jax.shard_map(local, mesh=refined, in_specs=in_specs, out_specs=out_specs, check_vma=False)
```

time: 497 us -> 167 us (0.34); the launches traced: 490 us -> 167 us
  starting transfers between devices: 228 us -> 28.7 us
  waiting for transfers between devices: 186 us -> 42.3 us
  Pallas kernels: 0 us -> 69 us
  other arithmetic: 62.9 us -> 0 us
  blocking collectives: 0 us -> 22.9 us
  local copies, waits for them, and re-layouts: 11 us -> 3.92 us
    ppermute x50 -> x10, starting transfers between devices: 228 us -> 23.9 us  [the longest x5 13.6 us: swap_c(): return lax.ppermute(x, 'c', pairs(2, 0))]
    ppermute x50 -> x10, waiting for transfers between devices: 186 us -> 34.9 us  [the longest x2 21.7 us: swap_o(): return lax.ppermute(x, SPACE, pairs(32, 1))]
    pallas_call x0 -> x6, Pallas kernels: none -> 69 us  [the longest x1 39.9 us: local(): call(chain_kernel, (shape(BLOCKS, HALF, YB, NZ),), ((SLABS, XALL, YW, NZ)...]
    all_to_all x0 -> x1, blocking collectives: none -> 22.9 us  [local(): own = lax.all_to_all(strips, PLANE, 0, 0, tiled=True)]
    reduce_sum x10 -> x0, other arithmetic: 17.8 us -> none  [restrict(): return jnp.mean(folded, axis=(-4, -2))]
    mul x60 -> x0, other arithmetic: 15.2 us -> none  [the longest x20 7.39 us: diffuse(): grad_z = face_z * (field_z[:, :, 1:] - field_z[:, :, :-1])]
    add x27 -> x0, other arithmetic: 13.3 us -> none  [the longest x7 7.72 us: local(): passing = prolong(coarse_run(chain_start)) + offset]
    select_n x7 -> x0, other arithmetic: 8.1 us -> none  [local(): chain_start = jnp.where(slab_index > round_num, arrived, chain_start)]
  transfers between devices with their start and end apart: 50 -> 11, of which waited for: 27 -> 8; matrix products, arithmetic and copies ran while one was open for 5% -> 0% of each run, Pallas kernels for 0% -> 24%
where the time goes in v1:
time: 167 us
  Pallas kernels  69 us (41%)
  waiting for transfers between devices  42.3 us (25%)
  starting transfers between devices  28.7 us (17%)
  blocking collectives  22.9 us (14%)
  local copies, waits for them, and re-layouts  3.92 us (2%)
    pallas_call x1, Pallas kernels, local(): call(chain_kernel, (shape(BLOCKS, HALF, YB, NZ),), ((SLABS, XALL, YW, NZ)...  39.9 us
    all_to_all x1, blocking collectives, local(): own = lax.all_to_all(strips, PLANE, 0, 0, tiled=True)  22.9 us
    ppermute x2, waiting for transfers between devices, swap_o(): return lax.ppermute(x, SPACE, pairs(32, 1))  21.7 us
    ppermute x5, starting transfers between devices, swap_c(): return lax.ppermute(x, 'c', pairs(2, 0))  13.6 us
    pallas_call x1, Pallas kernels, local(): call(second_kernel, (shape(*padded), shape(2, NY, NZ), crs, shape(2 * NY,...  9.18 us
    ppermute x1, waiting for transfers between devices, local(): even = lax.ppermute(even, 'z', pairs(8, 0))  8.61 us
    pallas_call x1, Pallas kernels, local(): call(third_kernel, (fine, shape(BLOCKS, HALF, YW, NZ)), (padded, padded,...  7.68 us
    all_to_all x1, waiting for transfers between devices, local(): fixes = lax.all_to_all(fixes, PLANE, 0, 0, tiled=True)  7.39 us
  transfers between devices with their start and end apart: 11, of which 8 were waited for; matrix products, arithmetic and copies ran while one was open for 0% of the time, Pallas kernels for 24%

profile of v1, /device:TPU:1, one launch (start us, length us, event | category | flops | bytes accessed | tf_op | source)
XLA Modules:
  0.0 166.8 jit_solution(4199175066617220116)
XLA Ops:
  0.0 0.7 stack.23.pos
  0.7 7.2 %shard_map.37 = (f32[1152,128]{1,0:T(8,128)}, f32[1152,128]{1,0:T(8,128)}, f32[8,256,128]{2,1,0:T(8,128)}, f32[8,256,128]{2,1,0:T(8,128)}, f32[8,256,128]{2,1,0:...) custom-call(s32[5]{0:T(128)} %stack.23.pos, ...), custom_call_target="tpu_custom_call" | custom-call | tf_op jit(solution)/shard_map/pallas_call | solution.py:474
  7.8 3.3 %collective-permute-start = (f32[1152,128]{1,0:T(8,128)}, f32[1152,128]{1,0:T(8,128)S(1)}, u32[]{:S(2)}, u32[]{:S(2)}) collective-permute-start(f32[1152,128]{1,0:T(8,128)} %get-tuple-element.29.sc), channel_id=1, source_target_pairs={{0,1},{1,0},{2,3},{3,2},{4,5},{5,4},{6,7},{7,6},{8,9},{9,8},{10,11... | collective-permute-start | bytes 1769480 | tf_op jit(solution)/shard_map/ppermute | solution.py:469
  11.1 1.0 collective-permute-start.1
  12.2 0.8 collective-permute-done.rc
  13.0 15.5 %collective-permute-done.1.ro = f32[1152,128]{1,0:T(8,128)S(1)} collective-permute-done((f32[1152,128]{1,0:T(8,128)}, f32[1152,128]{1,0:T(8,128)S(1)}, u32[]{:S(2)}, u32[]{:S(2)}) %collective-permute-start.1) | collective-permute-done | bytes 589856 | tf_op jit(solution)/shard_map/ppermute | solution.py:472
  28.5 0.8 copy-done.7
  29.3 9.2 %shard_map.38 = (f32[8,272,128]{2,1,0:T(8,128)}, f32[2,256,128]{2,1,0:T(8,128)}, f32[4,128,128]{2,1,0:T(8,128)}, f32[512,128]{1,0:T(8,128)}, f32[512,128]{1,0:T(8,128)}) custom-call(s32[5]{0:T(128)} %stack.23.pos, f32[1,8,256,128]{3,2,1,0:T(8,128)} %u_in.3, f32[8,256,128]{2,1,0:T(8,128)} %src.5, f32[1152,128]{1,0:T(8,128)} %get-tuple-element.29.sc, ...), custom_call_target="tpu_custom_call" | custom-call | tf_op jit(solution)/shard_map/pallas_call | solution.py:482
  38.5 0.0 collective-permute-start.2
  38.5 1.1 collective-permute-start.3
  39.6 0.6 collective-permute-done.2.rc
  40.3 6.2 %collective-permute-done.3.ro = f32[512,128]{1,0:T(8,128)S(1)} collective-permute-done((f32[512,128]{1,0:T(8,128)}, f32[512,128]{1,0:T(8,128)S(1)}, u32[]{:S(2)}, u32[]{:S(2)}) %collective-permute-start.3) | collective-permute-done | bytes 262176 | tf_op jit(solution)/shard_map/ppermute | solution.py:472
  46.4 0.7 copy-done.9
  47.2 7.7 %shard_map.39 = (f32[8,256,128]{2,1,0:T(8,128)}, f32[16,4,40,128]{3,2,1,0:T(8,128)}) custom-call(s32[5]{0:T(128)} %stack.23.pos, f32[8,272,128]{2,1,0:T(8,128)} %get-tuple-element.41.u_in, f32[8,256,128]{2,1,0:T(8,128)} %src.5, f32[2,256,128]{2,1,0:T(8,128)} %get-tuple-element.42.faces, f32[512,128]{1,0:T(8,128)} %copy-done.8, f32[512,128]{1,0:T(8,128)} %copy-done.9, ...), custom_call_target="tpu_custom_call" | custom-call | tf_op jit(solution)/shard_map/pallas_call | solution.py:490
  54.8 22.9 %all_to_all.10 = f32[16,4,40,128]{3,2,1,0:T(8,128)} all-to-all(f32[16,4,40,128]{3,2,1,0:T(8,128)} %get-tuple-element.47), channel_id=1, replica_groups=mesh['y'=4,'l'=2,'z'=8,'h'=2,'c'=2] {'y','l','h'}, dimensions={0} | all-to-all | bytes 2621440 | tf_op jit(solution)/shard_map/all_to_all | solution.py:496
  77.7 2.8 %shard_map.40 = (f32[44,40,128]{2,1,0:T(8,128)}, f32[44,40,128]{2,1,0:T(8,128)}) custom-call(s32[5]{0:T(128)} %stack.23.pos, f32[8,8,40,128]{3,2,1,0:T(8,128)} %bitcast.6), custom_call_target="tpu_custom_call" | custom-call | tf_op jit(solution)/shard_map/pallas_call | solution.py:499
  80.5 2.3 %collective-permute-start.6 = (f32[44,40,128]{2,1,0:T(8,128)}, f32[44,40,128]{2,1,0:T(8,128)S(1)}, u32[]{:S(2)}, u32[]{:S(2)}) collective-permute-start(f32[44,40,128]{2,1,0:T(8,128)} %get-tuple-element.51), channel_id=1, source_target_pairs={{0,4},{4,0},{8,12},{12,8},{16,20},{20,16},{24,28},{28,24},{1,5},{5... | collective-permute-start | bytes 2703368 | tf_op jit(solution)/shard_map/ppermute | solution.py:501
  82.8 5.6 %collective-permute-start.7 = (f32[44,40,128]{2,1,0:T(8,128)}, f32[44,40,128]{2,1,0:T(8,128)S(1)}, u32[]{:S(2)}, u32[]{:S(2)}) collective-permute-start(f32[44,40,128]{2,1,0:T(8,128)} %get-tuple-element.52), channel_id=1, source_target_pairs={{4,8},{8,4},{12,16},{16,12},{20,24},{24,20},{0,28},{28,0},{5,9},{9... | collective-permute-start | bytes 2703368 | tf_op jit(solution)/shard_map/ppermute | solution.py:502
  88.4 3.0 %collective-permute-start.5 = (f32[8,8,40,128]{3,2,1,0:T(8,128)S(1)}, f32[8,8,40,128]{3,2,1,0:T(8,128)S(1)}, u32[]{:S(2)}, u32[]{:S(2)}) collective-permute-start(f32[8,8,40,128]{3,2,1,0:T(8,128)S(1)} %bitcast.8), channel_id=1, source_target_pairs={{0,1},{1,0},{2,3},{3,2},{4,5},{5,4},{6,7},{7,6},{8,9},{9,8},{10,11... | collective-permute-start | bytes 3932168 | tf_op jit(solution)/shard_map/ppermute | solution.py:469
  91.4 8.6 %collective-permute-done.6.even = f32[44,40,128]{2,1,0:T(8,128)S(1)} collective-permute-done((f32[44,40,128]{2,1,0:T(8,128)}, f32[44,40,128]{2,1,0:T(8,128)S(1)}, u32[]{:S(2)}, u32[]{:S(2)}) %collective-permute-start.6) | collective-permute-done | bytes 901152 | tf_op jit(solution)/shard_map/ppermute | solution.py:501
  100.0 3.9 %collective-permute-start.8 = (f32[44,40,128]{2,1,0:T(8,128)S(1)}, f32[44,40,128]{2,1,0:T(8,128)S(1)}, u32[]{:S(2)}, u32[]{:S(2)}) collective-permute-start(f32[44,40,128]{2,1,0:T(8,128)S(1)} %collective-permute-done.6.even), channel_id=1, source_target_pairs={{0,1},{1,0},{2,3},{3,2},{4,5},{5,4},{6,7},{7,6},{8,9},{9,8},{10,11... | collective-permute-start | bytes 2703368 | tf_op jit(solution)/shard_map/ppermute | solution.py:469
  103.9 2.2 %collective-permute-done.7.odd = f32[44,40,128]{2,1,0:T(8,128)S(1)} collective-permute-done((f32[44,40,128]{2,1,0:T(8,128)}, f32[44,40,128]{2,1,0:T(8,128)S(1)}, u32[]{:S(2)}, u32[]{:S(2)}) %collective-permute-start.7) | collective-permute-done | bytes 901152 | tf_op jit(solution)/shard_map/ppermute | solution.py:502
  106.2 3.3 %collective-permute-start.9 = (f32[44,40,128]{2,1,0:T(8,128)S(1)}, f32[44,40,128]{2,1,0:T(8,128)}, u32[]{:S(2)}, u32[]{:S(2)}) collective-permute-start(f32[44,40,128]{2,1,0:T(8,128)S(1)} %collective-permute-done.7.odd), channel_id=1, source_target_pairs={{0,1},{1,0},{2,3},{3,2},{4,5},{5,4},{6,7},{7,6},{8,9},{9,8},{10,11... | collective-permute-start | bytes 2703368 | tf_op jit(solution)/shard_map/ppermute | solution.py:469
  109.5 0.3 collective-permute-start.4
  109.9 1.0 copy-done.5
  110.8 0.9 collective-permute-done.9.podd
  111.7 39.9 %shard_map.41 = f32[16,4,8,128]{3,2,1,0:T(8,128)} custom-call(s32[5]{0:T(128)} %stack.23.pos, f32[8,8,40,128]{3,2,1,0:T(8,128)} %bitcast.7, f32[8,8,40,128]{3,2,1,0:T(8,128)} %copy-done.1, f32[44,40,128]{2,1,0:T(8,128)} %copy-done.3, f32[44,40,128]{2,1,0:T(8,128)} %copy-done.4, f32[44,40,128]{2,1,0:T(8,128)} %copy-done.5, ...), custom_call_target="tpu_custom_call" | custom-call | tf_op jit(solution)/shard_map/pallas_call | solution.py:507
  151.6 4.8 %all-to-all-start.1 = ((f32[16,4,8,128]{3,2,1,0:T(8,128)}), f32[16,4,8,128]{3,2,1,0:T(8,128)S(1)}, u32[]{:S(2)}, u32[]{:S(2)}) async-start(f32[16,4,8,128]{3,2,1,0:T(8,128)} %shard_map.41), calls=%async_computation.1 | async-start | bytes 524288 | tf_op jit(solution)/shard_map/all_to_all | solution.py:515
  156.4 0.0 collective-permute-done.4.h_in
  156.4 7.4 %all-to-all-done.1.y_in = f32[16,4,8,128]{3,2,1,0:T(8,128)S(1)} async-done(((f32[16,4,8,128]{3,2,1,0:T(8,128)}), f32[16,4,8,128]{3,2,1,0:T(8,128)S(1)}, u32[]{:S(2)}, u32[]{:S(2)}) %all-to-all-start.1) | async-done | bytes 262176 | tf_op jit(solution)/shard_map/all_to_all | solution.py:515
  163.8 0.7 copy-done.2
  164.5 2.3 %shard_map.42 = f32[1,8,256,128]{3,2,1,0:T(8,128)} custom-call(f32[8,256,128]{2,1,0:T(8,128)} %collective-permute-done.4.h_in, f32[16,4,8,128]{3,2,1,0:T(8,128)} %copy-done.2), custom_call_target="tpu_custom_call" | custom-call | tf_op jit(solution)/shard_map/pallas_call | solution.py:516
  (18 shorter events, 0.0 us)
Async XLA Ops:
  7.8 5.1 %collective-permute-start = (f32[1152,128]{1,0:T(8,128)}, f32[1152,128]{1,0:T(8,128)S(1)}, u32[]{:S(2)}, u32[]{:S(2)}) collective-permute-start(f32[1152,128]{1,0:T(8,128)} %get-tuple-element.29.sc), channel_id=1, source_target_pairs={{0,1},{1,0},{2,3},{3,2},{4,5},{5,4},{6,7},{7,6},{8,9},{9,8},{10,11... | collective-permute-start | bytes 1769480 | tf_op jit(solution)/shard_map/ppermute | solution.py:469
  11.1 17.3 %collective-permute-start.1 = (f32[1152,128]{1,0:T(8,128)}, f32[1152,128]{1,0:T(8,128)S(1)}, u32[]{:S(2)}, u32[]{:S(2)}) collective-permute-start(f32[1152,128]{1,0:T(8,128)} %get-tuple-element.30.so), channel_id=1, source_target_pairs={{1,2},{2,1},{3,4},{4,3},{5,6},{6,5},{7,8},{8,7},{9,10},{10,9},{11,... | collective-permute-start | bytes 1769480 | tf_op jit(solution)/shard_map/ppermute | solution.py:472
  13.0 15.5 %copy-start.6 = (f32[1152,128]{1,0:T(8,128)}, f32[1152,128]{1,0:T(8,128)S(1)}, u32[]{:S(2)}) copy-start(f32[1152,128]{1,0:T(8,128)S(1)} %collective-permute-done.rc) | copy-start | bytes 1769476
  28.5 0.8 copy-start.7
  38.5 1.8 %collective-permute-start.2 = (f32[512,128]{1,0:T(8,128)}, f32[512,128]{1,0:T(8,128)S(1)}, u32[]{:S(2)}, u32[]{:S(2)}) collective-permute-start(f32[512,128]{1,0:T(8,128)} %get-tuple-element.43), channel_id=1, source_target_pairs={{0,1},{1,0},{2,3},{3,2},{4,5},{5,4},{6,7},{7,6},{8,9},{9,8},{10,11... | collective-permute-start | bytes 786440 | tf_op jit(solution)/shard_map/ppermute | solution.py:469
  38.5 7.9 %collective-permute-start.3 = (f32[512,128]{1,0:T(8,128)}, f32[512,128]{1,0:T(8,128)S(1)}, u32[]{:S(2)}, u32[]{:S(2)}) collective-permute-start(f32[512,128]{1,0:T(8,128)} %get-tuple-element.44), channel_id=1, source_target_pairs={{1,2},{2,1},{3,4},{4,3},{5,6},{6,5},{7,8},{8,7},{9,10},{10,9},{11,... | collective-permute-start | bytes 786440 | tf_op jit(solution)/shard_map/ppermute | solution.py:472
  40.3 6.2 %copy-start.8 = (f32[512,128]{1,0:T(8,128)}, f32[512,128]{1,0:T(8,128)S(1)}, u32[]{:S(2)}) copy-start(f32[512,128]{1,0:T(8,128)S(1)} %collective-permute-done.2.rc) | copy-start | bytes 786436
  46.4 0.7 copy-start.9
  77.7 10.7 %copy-start = (f32[16,4,40,128]{3,2,1,0:T(8,128)S(1)}, f32[16,4,40,128]{3,2,1,0:T(8,128)}, u32[]{:S(2)}) copy-start(f32[16,4,40,128]{3,2,1,0:T(8,128)} %all_to_all.10) | copy-start | bytes 3932164
  80.5 19.5 %collective-permute-start.6 = (f32[44,40,128]{2,1,0:T(8,128)}, f32[44,40,128]{2,1,0:T(8,128)S(1)}, u32[]{:S(2)}, u32[]{:S(2)}) collective-permute-start(f32[44,40,128]{2,1,0:T(8,128)} %get-tuple-element.51), channel_id=1, source_target_pairs={{0,4},{4,0},{8,12},{12,8},{16,20},{20,16},{24,28},{28,24},{1,5},{5... | collective-permute-start | bytes 2703368 | tf_op jit(solution)/shard_map/ppermute | solution.py:501
  82.8 23.4 %collective-permute-start.7 = (f32[44,40,128]{2,1,0:T(8,128)}, f32[44,40,128]{2,1,0:T(8,128)S(1)}, u32[]{:S(2)}, u32[]{:S(2)}) collective-permute-start(f32[44,40,128]{2,1,0:T(8,128)} %get-tuple-element.52), channel_id=1, source_target_pairs={{4,8},{8,4},{12,16},{16,12},{20,24},{24,20},{0,28},{28,0},{5,9},{9... | collective-permute-start | bytes 2703368 | tf_op jit(solution)/shard_map/ppermute | solution.py:502
  88.4 21.5 %collective-permute-start.5 = (f32[8,8,40,128]{3,2,1,0:T(8,128)S(1)}, f32[8,8,40,128]{3,2,1,0:T(8,128)S(1)}, u32[]{:S(2)}, u32[]{:S(2)}) collective-permute-start(f32[8,8,40,128]{3,2,1,0:T(8,128)S(1)} %bitcast.8), channel_id=1, source_target_pairs={{0,1},{1,0},{2,3},{3,2},{4,5},{5,4},{6,7},{7,6},{8,9},{9,8},{10,11... | collective-permute-start | bytes 3932168 | tf_op jit(solution)/shard_map/ppermute | solution.py:469
  100.0 11.7 %copy-start.3 = (f32[44,40,128]{2,1,0:T(8,128)}, f32[44,40,128]{2,1,0:T(8,128)S(1)}, u32[]{:S(2)}) copy-start(f32[44,40,128]{2,1,0:T(8,128)S(1)} %collective-permute-done.6.even) | copy-start | bytes 2703364
  100.0 9.9 %collective-permute-start.8 = (f32[44,40,128]{2,1,0:T(8,128)S(1)}, f32[44,40,128]{2,1,0:T(8,128)S(1)}, u32[]{:S(2)}, u32[]{:S(2)}) collective-permute-start(f32[44,40,128]{2,1,0:T(8,128)S(1)} %collective-permute-done.6.even), channel_id=1, source_target_pairs={{0,1},{1,0},{2,3},{3,2},{4,5},{5,4},{6,7},{7,6},{8,9},{9,8},{10,11... | collective-permute-start | bytes 2703368 | tf_op jit(solution)/shard_map/ppermute | solution.py:469
  106.2 3.7 %copy-start.4 = (f32[44,40,128]{2,1,0:T(8,128)}, f32[44,40,128]{2,1,0:T(8,128)S(1)}, u32[]{:S(2)}) copy-start(f32[44,40,128]{2,1,0:T(8,128)S(1)} %collective-permute-done.7.odd) | copy-start | bytes 2703364
  106.2 5.5 %collective-permute-start.9 = (f32[44,40,128]{2,1,0:T(8,128)S(1)}, f32[44,40,128]{2,1,0:T(8,128)}, u32[]{:S(2)}, u32[]{:S(2)}) collective-permute-start(f32[44,40,128]{2,1,0:T(8,128)S(1)} %collective-permute-done.7.odd), channel_id=1, source_target_pairs={{0,1},{1,0},{2,3},{3,2},{4,5},{5,4},{6,7},{7,6},{8,9},{9,8},{10,11... | collective-permute-start | bytes 2703368 | tf_op jit(solution)/shard_map/ppermute | solution.py:469
  109.5 46.9 %collective-permute-start.4 = (f32[8,256,128]{2,1,0:T(8,128)}, f32[8,256,128]{2,1,0:T(8,128)}, u32[]{:S(2)}, u32[]{:S(2)}) collective-permute-start(f32[8,256,128]{2,1,0:T(8,128)} %get-tuple-element.49), channel_id=1, source_target_pairs={{0,32},{32,64},{64,96},{96,128},{128,160},{160,192},{192,224},{224... | collective-permute-start | bytes 3145736 | tf_op jit(solution)/shard_map/ppermute | solution.py:500
  109.8 1.9 %copy-start.1 = (f32[8,8,40,128]{3,2,1,0:T(8,128)}, f32[8,8,40,128]{3,2,1,0:T(8,128)S(1)}, u32[]{:S(2)}) copy-start(f32[8,8,40,128]{3,2,1,0:T(8,128)S(1)} %collective-permute-done.5.part) | copy-start | bytes 3932164
  109.9 1.0 copy-start.5
  151.6 12.2 %all-to-all-start.1 = ((f32[16,4,8,128]{3,2,1,0:T(8,128)}), f32[16,4,8,128]{3,2,1,0:T(8,128)S(1)}, u32[]{:S(2)}, u32[]{:S(2)}) async-start(f32[16,4,8,128]{3,2,1,0:T(8,128)} %shard_map.41), calls=%async_computation.1 | async-start | bytes 524288 | tf_op jit(solution)/shard_map/all_to_all | solution.py:515
  163.8 0.7 copy-start.2

commit v2 on v1

v2 whole, which is shorter than its diff:
```python
import jax
import jax.numpy as jnp
from jax import lax
from jax.experimental import pallas as pl
from jax.experimental.pallas import tpu as pltpu
from jax.sharding import Mesh, PartitionSpec as P

SIZES = (4, 2, 8, 2, 2)
AXES = ("y", "l", "z", "h", "c")
SLABS = 8
ROWS = 8
NY = 256
NZ = 128
HALF = ROWS // 2
CY = NY // 2
PAD = 8
CHUNK = 64
FINE = 0.15
COARSE = 0.3
TABLE = (1.0, 0.72, 0.52, 0.37, 0.26, 0.18, 0.13, 0.09)

BLOCKS = 16
YB = CY // BLOCKS
YM = 16
YW = YB + 2 * YM
XH = 14
XW = 12 + 2 * XH
XALL = 48
KEEP = (8, 8, 6, 4, 4, 4, 2)
YCUT = (0, 0, 0, 8, 8, 8, 8)
WIDE = tuple(YW - 2 * cut for cut in YCUT)
STARTS = tuple(sum(KEEP[i] * WIDE[i] for i in range(j)) for j in range(8))
NSEND = STARTS[7]

EK, EU, E1, EKC, EUC, E1C, EDGE = 0, 256, 512, 768, 896, 1024, 1152

F32 = jnp.float32


def up_lane(x):
    return pltpu.roll(x, NZ - 1, axis=x.ndim - 1)


def down_lane(x):
    return pltpu.roll(x, 1, axis=x.ndim - 1)


def lanes(shape):
    return lax.broadcasted_iota(jnp.int32, shape, len(shape) - 1)


def lookup(material):
    result = jnp.zeros(material.shape, F32)
    for number in range(8):
        result = jnp.where(material == number, F32(TABLE[number]), result)
    return result


def z_faces(k, weight):
    lane = lanes(k.shape)
    upper = jnp.where(lane == NZ - 1, 0.0, up_lane(k))
    lower = jnp.where(lane == 0, 0.0, down_lane(k))
    above = weight * (k + upper)
    below = weight * (k + lower)
    return jnp.where(lane == NZ - 1, 0.0, above), above + below


def coefficients(kp, r, a, n, wx, wy, wz, below, above):
    k = kp[r, PAD + a : PAD + a + n]
    cyp = wy * (k + kp[r, PAD + a + 1 : PAD + a + n + 1])
    cym = wy * (k + kp[r, PAD + a - 1 : PAD + a + n - 1])
    cz, zsum = z_faces(k, wz)
    diag = 1.0 - (cyp + cym + zsum)
    cx = None
    if below:
        diag = diag - wx * (k + kp[r - 1, PAD + a : PAD + a + n])
    if above:
        cx = wx * (k + kp[r + 1, PAD + a : PAD + a + n])
        diag = diag - cx
    return cx, cyp, cym, cz, diag


def combine(u, r, a, n, cx_below, cx_above, cyp, cym, cz, diag):
    here = u[r, PAD + a : PAD + a + n]
    new = diag * here
    new = new + cyp * u[r, PAD + a + 1 : PAD + a + n + 1]
    new = new + cym * u[r, PAD + a - 1 : PAD + a + n - 1]
    new = new + cz * up_lane(here) + down_lane(cz * here)
    if cx_below is not None:
        new = new + cx_below * u[r - 1, PAD + a : PAD + a + n]
    if cx_above is not None:
        new = new + cx_above * u[r + 1, PAD + a : PAD + a + n]
    return new


def base(u, r, a, n, cx, cyp, cym, cz, diag, below, above):
    s = slice(a, a + n)
    return combine(
        u, r, a, n, cx[r - 1, s] if below else None, cx[r, s] if above else None, cyp[r, s], cym[r, s], cz[r, s], diag[r, s]
    )


def edge_sweep(kp, u, side, rows, a, n, wx, wy, wz):
    r = 0 if side == 0 else rows - 1
    cx, cyp, cym, cz, diag = coefficients(kp, r, a, n, wx, wy, wz, side == 1, side == 0)
    below = wx * (kp[r, PAD + a : PAD + a + n] + kp[r - 1, PAD + a : PAD + a + n]) if side == 1 else None
    return combine(u, r, a, n, below, cx, cyp, cym, cz, diag)


def each_row(count, visit):
    visit(0, False, True)

    def body(r, carry):
        visit(r, True, True)
        return carry

    lax.fori_loop(1, count - 1, body, 0)
    visit(count - 1, True, False)


def pieces(width):
    return [(a, CHUNK) for a in range(0, width, CHUNK)]


def clear_margin(ref, width):
    rows = ref.shape[0]
    ref[:, 0:PAD] = jnp.zeros((rows, PAD, NZ), F32)
    ref[:, PAD + width : PAD + width + PAD] = jnp.zeros((rows, PAD, NZ), F32)


def halve(ref, x, margin):
    total = None
    for p in range(2):
        for q in range(2):
            part = ref[2 * x + p, pl.ds(margin + q, CY, 2), :]
            total = part if total is None else total + part
    return 0.25 * total


FINE_W = (0.5 * FINE, 0.5 * FINE, 0.5 * FINE)
COARSE_W = (0.125 * COARSE, 0.125 * COARSE, 0.5 * COARSE)


def place(name):
    return lax.axis_index(name)


def block_of(h):
    return (place("y") * 2 + place("l")) * 2 + h


def lives():
    index = (place("z") * 2 + place("h")) * 2 + place("c")
    return jnp.where(index > 0, F32(1), F32(0)), jnp.where(index < 31, F32(1), F32(0))


def first_kernel(u_in, mat, src, sc, so, kp, up, kcp, ucp, edge, numbers, ends, u_sem, m_sem, s_sem):
    inside = pl.ds(PAD, NY)
    order = (0, 7, 1, 6, 2, 5, 3, 4)
    for side, r in ((0, 0), (1, ROWS - 1)):
        pltpu.make_async_copy(src.at[r], ends.at[side], s_sem.at[side]).start()
    for r in order:
        pltpu.make_async_copy(mat.at[r], numbers.at[r], m_sem.at[r]).start()
        pltpu.make_async_copy(u_in.at[0, r], up.at[r, inside], u_sem.at[r]).start()
    clear_margin(kp, NY)
    clear_margin(up, NY)
    clear_margin(kcp, CY)
    clear_margin(ucp, CY)
    for r in order:
        pltpu.make_async_copy(mat.at[r], numbers.at[r], m_sem.at[r]).wait()
        for a, n in pieces(NY):
            kp[r, PAD + a : PAD + a + n] = lookup(numbers[r, a : a + n])
    for r in range(ROWS):
        pltpu.make_async_copy(u_in.at[0, r], up.at[r, inside], u_sem.at[r]).wait()
    for side, r in ((0, 0), (1, ROWS - 1)):
        pltpu.make_async_copy(src.at[r], ends.at[side], s_sem.at[side]).wait()
    for x in range(HALF):
        kcp[x, PAD : PAD + CY] = halve(kp, x, PAD)
        ucp[x, PAD : PAD + CY] = halve(up, x, PAD)
    for side, r, x in ((0, 0, 0), (1, ROWS - 1, HALF - 1)):
        for a, n in pieces(NY):
            edge[side, EK + a : EK + a + n] = kp[r, PAD + a : PAD + a + n]
            edge[side, EU + a : EU + a + n] = up[r, PAD + a : PAD + a + n]
            edge[side, E1 + a : E1 + a + n] = edge_sweep(kp, up, side, ROWS, a, n, *FINE_W) + FINE * ends[side, a : a + n]
        for a, n in pieces(CY):
            edge[side, EKC + a : EKC + a + n] = kcp[x, PAD + a : PAD + a + n]
            edge[side, EUC + a : EUC + a + n] = ucp[x, PAD + a : PAD + a + n]
            edge[side, E1C + a : E1C + a + n] = edge_sweep(kcp, ucp, side, HALF, a, n, *COARSE_W)
    c = place("c")
    sc[...] = edge[1 - c]
    so[...] = edge[c]


def coef_kernel(kp, up, src, kcp, ucp, cx, cyp, cym, cz, dg, ccx, ccyp, ccym, ccz, cdg, b1, cb1, strip, strip_h, kw):
    clear_margin(b1, NY)
    clear_margin(cb1, CY)
    kw[:, 0:YM] = jnp.zeros((HALF, YM, NZ), F32)
    kw[:, YM + CY : YM + CY + YM] = jnp.zeros((HALF, YM, NZ), F32)
    kw[:, YM : YM + CY] = kcp[:, PAD : PAD + CY]
    h = place("h")
    strip[...] = kw[:, pl.ds(pl.multiple_of(block_of(h) * YB, 8), YW)]
    strip_h[...] = kw[:, pl.ds(pl.multiple_of(block_of(1 - h) * YB, 8), YW)]

    def make(k, u, n_all, weights, outs, target, source):
        fx, fyp, fym, fz, fd = outs

        def visit(r, below, above):
            for a, n in pieces(n_all):
                s = slice(a, a + n)
                wx = weights[0]
                above_c, yp, ym, zc, dd = coefficients(k, r, a, n, *weights, below, above)
                fyp[r, s], fym[r, s], fz[r, s], fd[r, s] = yp, ym, zc, dd
                if above:
                    fx[r, s] = above_c
                under = wx * (k[r, PAD + a : PAD + a + n] + k[r - 1, PAD + a : PAD + a + n]) if below else None
                new = combine(u, r, a, n, under, above_c, yp, ym, zc, dd)
                if source is not None:
                    new = new + FINE * source[r, s]
                target[r, PAD + a : PAD + a + n] = new

        each_row(u.shape[0], visit)

    make(kp, up, NY, FINE_W, (cx, cyp, cym, cz, dg), b1, src)
    make(kcp, ucp, CY, COARSE_W, (ccx, ccyp, ccym, ccz, cdg), cb1, None)


def fix_rows(target, old, swept, halo, face, rows, width):
    target[...] = swept[...]
    for side, r in ((0, 0), (1, rows - 1)):
        for a, n in pieces(width):
            s = slice(PAD + a, PAD + a + n)
            target[r, s] = swept[r, s] + face(side, a, n) * (halo(side, a, n) - old[r, s])


def halo_after(store, old, halo, later, face, live, rows, width):
    for side, r in ((0, 0), (1, rows - 1)):
        for a, n in pieces(width):
            flux = face(side, a, n) * (old[r, PAD + a : PAD + a + n] - halo(side, a, n))
            store[side, a : a + n] = live[side] * (later(side, a, n) + flux)


def full_sweep(dst, src_ref, store, face, rows, width, coefs, source):
    def visit(r, below, above):
        for a, n in pieces(width):
            new = base(src_ref, r, a, n, *coefs, below, above)
            if source is not None:
                new = new + FINE * source[r, a : a + n]
            here = src_ref[r, PAD + a : PAD + a + n]
            if not below:
                new = new + face(0, a, n) * (store[0, a : a + n] - here)
            if not above:
                new = new + face(1, a, n) * (store[1, a : a + n] - here)
            dst[r, PAD + a : PAD + a + n] = new

    each_row(rows, visit)


def reader(ref, offset=0):
    return lambda side, a, n: ref[side, offset + a : offset + a + n]


def second_kernel(
    src, sc, so, rc, ro, up, ucp, b1, cb1, strip, strip_h, cx, cyp, cym, cz, dg, u2, faces, c1, cfaces, cstore, tc, to, kown, own, got, store, edge, u1,
):
    c = place("c")
    h = place("h")
    kown[pl.ds(4 * h, HALF)] = strip[...]
    kown[pl.ds(4 * (1 - h), HALF)] = strip_h[...]
    live = lives()
    own[1 - c] = sc[...]
    own[c] = so[...]
    got[1 - c] = rc[...]
    got[c] = ro[...]
    for side in range(2):
        got[side] = got[side] * live[side]
        for a, n in pieces(NY):
            faces[side, a : a + n] = (0.5 * FINE) * (own[side, EK + a : EK + a + n] + got[side, EK + a : EK + a + n])
        for a, n in pieces(CY):
            cfaces[side, a : a + n] = (0.125 * COARSE) * (own[side, EKC + a : EKC + a + n] + got[side, EKC + a : EKC + a + n])
    clear_margin(u2, NY)
    halo_after(store, up, reader(got, EU), reader(got, E1), reader(faces), live, ROWS, NY)
    fix_rows(u1, up, b1, reader(got, EU), reader(faces), ROWS, NY)
    coefs = (cx, cyp, cym, cz, dg)
    full_sweep(u2, u1, store, reader(faces), ROWS, NY, coefs, src)
    for side, r in ((0, 0), (1, ROWS - 1)):
        for a, n in pieces(NY):
            edge[side, a : a + n] = u2[r, PAD + a : PAD + a + n]
            edge[side, NY + a : NY + a + n] = base(u2, r, a, n, *coefs, side == 1, side == 0) + FINE * src[r, a : a + n]
    tc[...] = edge[1 - c]
    to[...] = edge[c]
    halo_after(cstore, ucp, reader(got, EUC), reader(got, E1C), reader(cfaces), live, HALF, CY)
    fix_rows(c1, ucp, cb1, reader(got, EUC), reader(cfaces), HALF, CY)


def middle_kernel(u2, src, c1, cstore, cfaces, cx, cyp, cym, cz, dg, ccx, ccyp, ccym, ccz, cdg, b3, au):
    clear_margin(b3, NY)
    clear_margin(au, CY)

    def visit(r, below, above):
        for a, n in pieces(NY):
            b3[r, PAD + a : PAD + a + n] = base(u2, r, a, n, cx, cyp, cym, cz, dg, below, above) + FINE * src[r, a : a + n]

    each_row(ROWS, visit)
    full_sweep(au, c1, cstore, reader(cfaces), HALF, CY, (ccx, ccyp, ccym, ccz, cdg), None)


def third_kernel(
    u2, src, faces, rc, ro, b3, au, kown, keven, kodd, cx, cyp, cym, cz, dg, h_out, strips, kall, got, store, u3, f, wp,
):
    kall[0:8] = kown[...]
    kall[8:16] = keven[...]
    kall[16:24] = kodd[...]
    c = place("c")
    live = lives()
    got[1 - c] = rc[...]
    got[c] = ro[...]
    for side in range(2):
        got[side] = got[side] * live[side]
    halo_after(store, u2, reader(got), reader(got, NY), reader(faces), live, ROWS, NY)
    fix_rows(u3, u2, b3, reader(got), reader(faces), ROWS, NY)
    full_sweep(f, u3, store, reader(faces), ROWS, NY, (cx, cyp, cym, cz, dg), src)
    keep = jnp.where(place("y") + place("l") > 0, F32(1), F32(0))
    wp[:, 0:YM] = jnp.zeros((HALF, YM, NZ), F32)
    wp[:, YM + CY : YM + CY + YM] = jnp.zeros((HALF, YM, NZ), F32)
    for x in range(HALF):
        coarse = keep * au[x, PAD : PAD + CY]
        total = None
        for p in range(2):
            for q in range(2):
                part = f[2 * x + p, pl.ds(PAD + q, CY, 2), :] - coarse
                h_out[2 * x + p, pl.ds(q, CY, 2), :] = part
                total = part if total is None else total + part
        wp[x, YM : YM + CY] = 0.25 * total
    for b in range(BLOCKS):
        strips[b] = wp[:, b * YB : b * YB + YW]


def pack_kernel(own, even, odd):
    up = 1 - lax.rem(place("z"), 2)
    for j in range(7):
        n, cut, wide = KEEP[j], YCUT[j], WIDE[j]
        for t in range(n):
            at = STARTS[j] + t * wide
            even[at : at + wide] = own[j, up * (8 - n) + t, cut : cut + wide]
            odd[at : at + wide] = own[j, (1 - up) * (8 - n) + t, cut : cut + wide]


def position(i):
    return 8 * (i // 4) + i % 4


def patch_kernel(kall, pkall, cxp, cyp, cym, cz, dg, kp):
    c = place("c")
    z = place("z")
    is_up = 1 - lax.rem(z, 2)
    low = jnp.where(z > 0, F32(1), F32(0))
    high = jnp.where(z < 7, F32(1), F32(0))
    first = 4 * c + 16 - XH
    kp[:, 0:PAD] = jnp.zeros((XALL, PAD, NZ), F32)
    kp[:, PAD + YW : PAD + YW + PAD] = jnp.zeros((XALL, PAD, NZ), F32)
    for core, k_ref in ((c, kall), (1 - c, pkall)):
        shift = 16 + 4 * core
        for i in range(8):
            kp[shift + position(i), PAD : PAD + YW] = k_ref[i]

            kp[shift + position(i) - 16, PAD : PAD + YW] = k_ref[8 * (1 + is_up) + i] * low
            kp[shift + position(i) + 16, PAD : PAD + YW] = k_ref[8 * (2 - is_up) + i] * high

    ycell = block_of(place("h")) * YB - YM + lax.broadcasted_iota(jnp.int32, (YW, NZ), 0)
    ymask = jnp.where((ycell >= 0) & (ycell < CY), F32(1), F32(0))
    wx, _, wz = COARSE_W

    def coef(g, carry):
        for t in range(4):
            r = 4 * g + t
            q = first + r
            k = kp[q, PAD : PAD + YW]
            a = wx * (k + kp[q, PAD + 1 : PAD + YW + 1])
            b = wx * (k + kp[q, PAD - 1 : PAD + YW - 1])
            zc, zsum = z_faces(k, wz)
            above = wx * (k + kp[q + 1, PAD : PAD + YW])
            below = wx * (k + kp[q - 1, PAD : PAD + YW])
            row = 16 * z + 4 * c - XH + r
            m = ymask * jnp.where((row >= 0) & (row < CY), F32(1), F32(0))
            m_above = ymask * jnp.where((row >= 0) & (row < CY - 1), F32(1), F32(0))
            cyp[r] = a * m
            cym[r] = b * m
            cz[r] = zc * m
            cxp[r] = above * m_above
            dg[r] = (1.0 - (a + b + zsum + above + below)) * m
        return carry

    lax.fori_loop(0, XW // 4, coef, 0)


def chain_kernel(own, part, even, odd, peven, podd, cxp, cyp, cym, cz, dg, out, w, ea, eb):
    c = place("c")
    z = place("z")
    is_up = lax.rem(z, 2) == 0
    low = jnp.where(z > 0, F32(1), F32(0))
    high = jnp.where(z < 7, F32(1), F32(0))
    first = 4 * c + 16 - XH

    for core, mine, e_ref, o_ref in ((c, own, even, odd), (1 - c, part, peven, podd)):
        shift = 16 + 4 * core
        for j in range(7):
            for i in range(8):
                w[j, shift + position(i)] = mine[j, i]

        def fill(from_below, from_above):
            for j in range(7):
                n, cut, wide = KEEP[j], YCUT[j], WIDE[j]
                for t in range(n):
                    at = STARTS[j] + t * wide
                    w[j, shift + position(8 - n + t) - 16, cut : cut + wide] = from_below[at : at + wide] * low
                    w[j, shift + position(t) + 16, cut : cut + wide] = from_above[at : at + wide] * high

        @pl.when(is_up)
        def _():
            fill(o_ref, e_ref)

        @pl.when(jnp.logical_not(is_up))
        def _():
            fill(e_ref, o_ref)

    for r in range(XW):
        ea[r, PAD : PAD + YW] = w[0, first + r]

    def halved(lo, hi, visit):
        half = (hi - lo) // 2

        def body(g, carry):
            for t in range(half):
                visit(lo + g * half + t)
            return carry

        lax.fori_loop(0, 2, body, 0)

    def sweep(src, dst, number, added):
        cut = 0 if number <= 5 else 8
        s = slice(cut, YW - cut)
        n = YW - 2 * cut

        def visit(r):
            here = src[r, PAD + cut : PAD + cut + n]
            zc = cz[r, s]
            new = dg[r, s] * here + cyp[r, s] * src[r, PAD + cut + 1 : PAD + cut + n + 1]
            new = new + cym[r, s] * src[r, PAD + cut - 1 : PAD + cut + n - 1]
            new = new + (cxp[r - 1, s] * src[r - 1, PAD + cut : PAD + cut + n] + cxp[r, s] * src[r + 1, PAD + cut : PAD + cut + n])
            dst[r, PAD + cut : PAD + cut + n] = new + (zc * up_lane(here) + down_lane(zc * here))

        halved(number, XW - number, visit)

    out[2:4] = jnp.zeros((2, HALF, YB, NZ), F32)
    for k in range(1, 8):
        sweep(ea, eb, 2 * k - 1, None)
        sweep(eb, ea, 2 * k, None)
        m = (k + 1) % SLABS
        for side in range(2):
            for i in range(HALF):
                out[2 * m + side, i] = ea[XH + 8 * side + i, PAD + YM : PAD + YM + YB]
        if k < 7:
            cut = YCUT[k]
            s = slice(PAD + cut, PAD + YW - cut)

            def add(r):
                ea[r, s] = ea[r, s] + w[k, first + r, cut : YW - cut]

            halved(2 * k, XW - 2 * k, add)


def last_kernel(h_in, y_in, out):
    for x in range(HALF):
        fix = y_in[:, x].reshape(CY, NZ)
        for p in range(2):
            for q in range(2):
                out[0, 2 * x + p, pl.ds(q, CY, 2), :] = h_in[2 * x + p, pl.ds(q, CY, 2), :] + fix


def call(kernel, outs, scratch, *operands, limit=10, specs=None):
    vmem = pl.BlockSpec(memory_space=pltpu.VMEM)
    return pl.pallas_call(
        kernel,
        out_shape=[jax.ShapeDtypeStruct(s, F32) for s in outs],
        in_specs=specs or [vmem] * len(operands),
        out_specs=[vmem] * len(outs),
        scratch_shapes=[s if callable(getattr(s, "get_ref_aval", None)) else pltpu.VMEM(s, F32) for s in scratch],
        compiler_params=pltpu.CompilerParams(vmem_limit_bytes=limit * 1024 * 1024),
    )(*operands)


def pairs(n, odd):
    found = []
    for i in range(odd, n - 1, 2):
        found += [(i, i + 1), (i + 1, i)]
    if odd:
        found += [(0, n - 1), (n - 1, 0)]
    return found


SPACE = ("z", "h", "c")
PLANE = ("y", "l", "h")


def local(starts, material, source):
    fine = (ROWS, NY, NZ)
    crs = (HALF, CY, NZ)
    padded = (ROWS, NY + 2 * PAD, NZ)
    cpad = (HALF, CY + 2 * PAD, NZ)
    strip_shape = (HALF, YW, NZ)

    def swap_c(x):
        return lax.ppermute(x, "c", pairs(2, 0))

    def swap_o(x):
        return lax.ppermute(x, SPACE, pairs(32, 1))

    dma = pltpu.SemaphoreType.DMA
    sc, so, kp, up, kcp, ucp = call(
        first_kernel,
        ((EDGE, NZ), (EDGE, NZ), padded, padded, cpad, cpad),
        ((2, EDGE, NZ), pltpu.VMEM(fine, jnp.int32), (2, NY, NZ), dma((ROWS,)), dma((ROWS,)), dma((2,))),
        *(pltpu.with_memory_space_constraint(x, pltpu.HBM) for x in (starts, material, source)),
        specs=[pl.BlockSpec(memory_space=pltpu.HBM)] * 3,
    )
    rc = swap_c(sc)
    ro = swap_o(so)
    *coefs, b1, cb1, strip, strip_h = call(
        coef_kernel, (fine,) * 5 + (crs,) * 5 + (padded, cpad, strip_shape, strip_shape), ((HALF, CY + 2 * YM, NZ),),
        kp, up, source, kcp, ucp,
    )
    strip_h = lax.ppermute(strip_h, "h", pairs(2, 0))
    u2, faces, c1, cfaces, cstore, tc, to, kown = call(
        second_kernel,
        (padded, (2, NY, NZ), cpad, (2, CY, NZ), (2, CY, NZ), (2 * NY, NZ), (2 * NY, NZ), (8, YW, NZ)),
        ((2, EDGE, NZ), (2, EDGE, NZ), (2, NY, NZ), (2, 2 * NY, NZ), padded),
        source, sc, so, rc, ro, up, ucp, b1, cb1, strip, strip_h, *coefs[:5],
    )
    rc2 = swap_c(tc)
    ro2 = swap_o(to)
    keven = lax.ppermute(kown, "z", pairs(8, 0))
    kodd = lax.ppermute(kown, "z", pairs(8, 1))
    b3, au = call(middle_kernel, (padded, cpad), (), u2, source, c1, cstore, cfaces, *coefs)
    moved, strips, kall = call(
        third_kernel,
        (fine, (BLOCKS, HALF, YW, NZ), (24, YW, NZ)),
        ((2, 2 * NY, NZ), (2, NY, NZ), padded, padded, (HALF, CY + 2 * YM, NZ)),
        u2, source, faces, rc2, ro2, b3, au, kown, keven, kodd, *coefs[:5],
    )
    own = lax.all_to_all(strips, PLANE, 0, 0, tiled=True)
    own, moved = lax.optimization_barrier((own, moved))
    own = own.reshape(SLABS, 8, YW, NZ)
    even, odd = call(pack_kernel, ((NSEND, NZ), (NSEND, NZ)), (), own)
    even = lax.ppermute(even, "z", pairs(8, 0))
    odd = lax.ppermute(odd, "z", pairs(8, 1))
    part = swap_c(own)
    moved = lax.ppermute(moved, ("y", "l"), [(i, (i + 1) % 8) for i in range(8)])
    peven = swap_c(even)
    podd = swap_c(odd)
    dom = (XW + 1, YW + 2 * PAD, NZ)
    flat = (XW, YW, NZ)
    patch = call(patch_kernel, (flat,) * 5, ((XALL, YW + 2 * PAD, NZ),), kall, swap_c(kall))
    (fixes,) = call(
        chain_kernel, ((BLOCKS, HALF, YB, NZ),), ((7, XALL, YW, NZ), dom, dom),
        own, part, even, odd, peven, podd, *patch, limit=18,
    )
    fixes = lax.all_to_all(fixes, PLANE, 0, 0, tiled=True)
    (result,) = call(last_kernel, ((1, ROWS, NY, NZ),), (), moved, fixes)
    return result


def solution(mesh):
    refined = Mesh(mesh.devices.reshape(SIZES), AXES)
    in_specs = (P(("y", "l"), SPACE, None, None), P(SPACE, None, None), P(SPACE, None, None))
    out_specs = P(("y", "l"), SPACE, None, None)
    return jax.shard_map(local, mesh=refined, in_specs=in_specs, out_specs=out_specs, check_vma=False)
```

time: 167 us -> 109 us (0.65)
  Pallas kernels: 69 us -> 20.7 us
  local copies, waits for them, and re-layouts: 3.92 us -> 0.01 us
  waiting for transfers between devices: 42.3 us -> 38.6 us
  starting transfers between devices: 28.7 us -> 25.4 us
    pallas_call x6 -> x9, Pallas kernels: 69 us -> 20.7 us  [call(): pl.pallas_call(kernel, out_shape=[jax.ShapeDtypeStruct(s, F32) for s in o...]
    ppermute x2, waiting for transfers between devices: 21.7 us -> 2.08 us  [swap_o(): return lax.ppermute(x, SPACE, pairs(32, 1))]
    ppermute x0 -> x3, waiting for transfers between devices: none -> 13.7 us  [the longest x1 10.3 us: local(): strip_h = lax.ppermute(strip_h, 'h', pairs(2, 0))]
    ppermute x0 -> x3, starting transfers between devices: none -> 7.24 us  [the longest x1 5.57 us: local(): kodd = lax.ppermute(kown, 'z', pairs(8, 1))]
    ppermute x5 -> x6, starting transfers between devices: 13.6 us -> 9.05 us  [swap_c(): return lax.ppermute(x, 'c', pairs(2, 0))]
    unnamed x20 -> x2, local copies, waits for them, and re-layouts: 3.25 us -> 0.01 us
    ppermute x1, waiting for transfers between devices: 8.61 us -> 11.3 us  [local(): even = lax.ppermute(even, 'z', pairs(8, 0))]
    ppermute x1, starting transfers between devices: 2.3 us -> 0.09 us  [local(): even = lax.ppermute(even, 'z', pairs(8, 0))]
  transfers between devices with their start and end apart: 11 -> 15, of which waited for: 8 -> 8; matrix products, arithmetic and copies ran while one was open for 0% -> 0% of each run, Pallas kernels for 24% -> 12%
where the time goes in v2:
time: 109 us
  waiting for transfers between devices  38.6 us (35%)
  starting transfers between devices  25.4 us (23%)
  blocking collectives  24 us (22%)
  Pallas kernels  20.7 us (19%)
    all_to_all x1, blocking collectives, local(): own = lax.all_to_all(strips, PLANE, 0, 0, tiled=True)  24 us
    pallas_call x9, Pallas kernels, call(): pl.pallas_call(kernel, out_shape=[jax.ShapeDtypeStruct(s, F32) for s in o...  20.7 us
    ppermute x1, waiting for transfers between devices, local(): even = lax.ppermute(even, 'z', pairs(8, 0))  11.3 us
    ppermute x1, waiting for transfers between devices, local(): strip_h = lax.ppermute(strip_h, 'h', pairs(2, 0))  10.3 us
    ppermute x6, starting transfers between devices, swap_c(): return lax.ppermute(x, 'c', pairs(2, 0))  9.05 us
    all_to_all x1, waiting for transfers between devices, local(): fixes = lax.all_to_all(fixes, PLANE, 0, 0, tiled=True)  7.34 us
    ppermute x1, starting transfers between devices, local(): kodd = lax.ppermute(kown, 'z', pairs(8, 1))  5.57 us
    ppermute x1, starting transfers between devices, local(): odd = lax.ppermute(odd, 'z', pairs(8, 1))  4 us
  transfers between devices with their start and end apart: 15, of which 8 were waited for; matrix products, arithmetic and copies ran while one was open for 0% of the time, Pallas kernels for 12%

profile of v2, /device:TPU:1, one launch (start us, length us, event | category | flops | bytes accessed | tf_op | source)
XLA Modules:
  0.0 108.8 jit_solution(4679910296895312877)
XLA Ops:
  0.0 3.0 %shard_map.37 = (f32[1152,128]{1,0:T(8,128)S(1)}, f32[1152,128]{1,0:T(8,128)S(1)}, f32[8,272,128]{2,1,0:T(8,128)S(1)}, f32[8,272,128]{2,1,0:T(8,128)S(1)}, f32[4...) custom-call(f32[1,8,256,128]{3,2,1,0:T(8,128)} %u_in.1, s32[8,256,128]{2,1,0:T(8,128)} %mat.1, f32[8,256,128]{2,1,0:T(8,128)} %src.9), custom_call_target="tpu_custom_call" | custom-call | tf_op jit(solution)/shard_map/pallas_call | solution.py:482
  3.0 3.3 %collective-permute-start = (f32[1152,128]{1,0:T(8,128)S(1)}, f32[1152,128]{1,0:T(8,128)S(1)}, u32[]{:S(2)}, u32[]{:S(2)}) collective-permute-start(f32[1152,128]{1,0:T(8,128)S(1)} %get-tuple-element.47.sc), channel_id=1, source_target_pairs={{0,1},{1,0},{2,3},{3,2},{4,5},{5,4},{6,7},{7,6},{8,9},{9,8},{10,11... | collective-permute-start | bytes 1769480 | tf_op jit(solution)/shard_map/ppermute | solution.py:513
  6.3 1.0 collective-permute-start.1
  7.3 2.9 %shard_map.38 = (f32[8,256,128]{2,1,0:T(8,128)S(1)}, f32[8,256,128]{2,1,0:T(8,128)S(1)}, f32[8,256,128]{2,1,0:T(8,128)S(1)}, f32[8,256,128]{2,1,0:T(8,128)S(1)},...) custom-call(f32[8,272,128]{2,1,0:T(8,128)S(1)} %get-tuple-element.51, ...), custom_call_target="tpu_custom_call" | custom-call | tf_op jit(solution)/shard_map/pallas_call | solution.py:482
  10.2 1.7 %collective-permute-start.2 = (f32[4,40,128]{2,1,0:T(8,128)S(1)}, f32[4,40,128]{2,1,0:T(8,128)S(1)}, u32[]{:S(2)}, u32[]{:S(2)}) collective-permute-start(f32[4,40,128]{2,1,0:T(8,128)S(1)} %get-tuple-element.56), channel_id=1, source_target_pairs={{0,2},{2,0},{1,3},{3,1},{4,6},{6,4},{5,7},{7,5},{8,10},{10,8},{9,1... | collective-permute-start | bytes 245768 | tf_op jit(solution)/shard_map/ppermute | solution.py:532
  11.9 10.3 %collective-permute-done.2.strip_h = f32[4,40,128]{2,1,0:T(8,128)S(1)} collective-permute-done((f32[4,40,128]{2,1,0:T(8,128)S(1)}, f32[4,40,128]{2,1,0:T(8,128)S(1)}, u32[]{:S(2)}, u32[]{:S(2)}) %collective-permute-start.2) | collective-permute-done | bytes 81952 | tf_op jit(solution)/shard_map/ppermute | solution.py:532
  22.2 2.1 %collective-permute-done.1.ro = f32[1152,128]{1,0:T(8,128)S(1)} collective-permute-done((f32[1152,128]{1,0:T(8,128)S(1)}, f32[1152,128]{1,0:T(8,128)S(1)}, u32[]{:S(2)}, u32[]{:S(2)}) %collective-permute-start.1) | collective-permute-done | bytes 589856 | tf_op jit(solution)/shard_map/ppermute | solution.py:516
  24.3 2.0 %shard_map.39 = (f32[8,272,128]{2,1,0:T(8,128)S(1)}, f32[2,256,128]{2,1,0:T(8,128)S(1)}, f32[4,144,128]{2,1,0:T(8,128)S(1)}, f32[2,128,128]{2,1,0:T(8,128)S(1)},...) custom-call(f32[8,256,128]{2,1,0:T(8,128)S(1)} %copy-done, ...), custom_call_target="tpu_custom_call" | custom-call | tf_op jit(solution)/shard_map/pallas_call | solution.py:482
  26.3 1.7 %collective-permute-start.3 = (f32[512,128]{1,0:T(8,128)S(1)}, f32[512,128]{1,0:T(8,128)S(1)}, u32[]{:S(2)}, u32[]{:S(2)}) collective-permute-start(f32[512,128]{1,0:T(8,128)S(1)} %get-tuple-element.64), channel_id=1, source_target_pairs={{0,1},{1,0},{2,3},{3,2},{4,5},{5,4},{6,7},{7,6},{8,9},{9,8},{10,11... | collective-permute-start | bytes 786440 | tf_op jit(solution)/shard_map/ppermute | solution.py:513
  27.9 0.1 collective-permute-start.4
  28.1 5.6 %collective-permute-start.6 = (f32[8,40,128]{2,1,0:T(8,128)S(1)}, f32[8,40,128]{2,1,0:T(8,128)S(1)}, u32[]{:S(2)}, u32[]{:S(2)}) collective-permute-start(f32[8,40,128]{2,1,0:T(8,128)S(1)} %get-tuple-element.76.kown), channel_id=1, source_target_pairs={{4,8},{8,4},{12,16},{16,12},{20,24},{24,20},{0,28},{28,0},{5,9},{9... | collective-permute-start | bytes 491528 | tf_op jit(solution)/shard_map/ppermute | solution.py:542
  33.7 1.6 %shard_map.40 = (f32[8,272,128]{2,1,0:T(8,128)S(1)}, f32[4,144,128]{2,1,0:T(8,128)S(1)}) custom-call(f32[8,272,128]{2,1,0:T(8,128)S(1)} %get-tuple-element.62.u2, f32[8,256,128]{2,1,0:T(8,128)S(1)} %copy-done, f32[4,144,128]{2,1,0:T(8,128)S(1)} %get-tuple-element.66.c1, f32[2,128,128]{2,1,0:T(8,128)S(1)} %get-tuple-element.67.cstore, ...), custom_call_target="tpu_custom_call" | custom-call | tf_op jit(solution)/shard_map/pallas_call | solution.py:482
  35.2 2.4 %collective-permute-done.6.kodd = f32[8,40,128]{2,1,0:T(8,128)S(1)} collective-permute-done((f32[8,40,128]{2,1,0:T(8,128)S(1)}, f32[8,40,128]{2,1,0:T(8,128)S(1)}, u32[]{:S(2)}, u32[]{:S(2)}) %collective-permute-start.6) | collective-permute-done | bytes 163872 | tf_op jit(solution)/shard_map/ppermute | solution.py:542
  37.7 0.9 collective-permute-done.5.keven
  38.6 1.6 %shard_map.41 = (f32[8,256,128]{2,1,0:T(8,128)S(1)}, f32[16,4,40,128]{3,2,1,0:T(8,128)S(1)}, f32[24,40,128]{2,1,0:T(8,128)S(1)}) custom-call(f32[8,272,128]{2,1,0:T(8,128)S(1)} %get-tuple-element.62.u2, f32[8,256,128]{2,1,0:T(8,128)S(1)} %copy-done, f32[2,256,128]{2,1,0:T(8,128)S(1)} %get-tuple-element.63.faces, f32[512,128]{1,0:T(8,128)S(1)} %collective-permute-done.3.rc, ...), custom_call_target="tpu_custom_call" | custom-call | tf_op jit(solution)/shard_map/pallas_call | solution.py:482
  40.2 24.0 %all_to_all.10 = f32[16,4,40,128]{3,2,1,0:T(8,128)S(1)} all-to-all(f32[16,4,40,128]{3,2,1,0:T(8,128)S(1)} %get-tuple-element.77), channel_id=1, replica_groups=mesh['y'=4,'l'=2,'z'=8,'h'=2,'c'=2] {'y','l','h'}, dimensions={0} | all-to-all | bytes 2621440 | tf_op jit(solution)/shard_map/all_to_all | solution.py:550
  64.2 2.5 %collective-permute-start.8 = (f32[8,8,40,128]{3,2,1,0:T(8,128)S(1)}, f32[8,8,40,128]{3,2,1,0:T(8,128)S(1)}, u32[]{:S(2)}, u32[]{:S(2)}) collective-permute-start(f32[8,8,40,128]{3,2,1,0:T(8,128)S(1)} %bitcast.1), channel_id=1, source_target_pairs={{0,1},{1,0},{2,3},{3,2},{4,5},{5,4},{6,7},{7,6},{8,9},{9,8},{10,11... | collective-permute-start | bytes 3932168 | tf_op jit(solution)/shard_map/ppermute | solution.py:513
  66.8 0.1 shard_map.42
  66.8 0.1 collective-permute-start.9
  66.9 4.0 %collective-permute-start.10 = (f32[1216,128]{1,0:T(8,128)S(1)}, f32[1216,128]{1,0:T(8,128)S(1)}, u32[]{:S(2)}, u32[]{:S(2)}) collective-permute-start(f32[1216,128]{1,0:T(8,128)S(1)} %get-tuple-element.82), channel_id=1, source_target_pairs={{4,8},{8,4},{12,16},{16,12},{20,24},{24,20},{0,28},{28,0},{5,9},{9... | collective-permute-start | bytes 1867784 | tf_op jit(solution)/shard_map/ppermute | solution.py:555
  70.9 0.3 collective-permute-start.7
  71.2 11.3 %collective-permute-done.9.even = f32[1216,128]{1,0:T(8,128)S(1)} collective-permute-done((f32[1216,128]{1,0:T(8,128)S(1)}, f32[1216,128]{1,0:T(8,128)S(1)}, u32[]{:S(2)}, u32[]{:S(2)}) %collective-permute-start.9) | collective-permute-done | bytes 622624 | tf_op jit(solution)/shard_map/ppermute | solution.py:554
  82.5 0.9 collective-permute-start.11
  83.4 1.9 %collective-permute-done.10.odd = f32[1216,128]{1,0:T(8,128)S(1)} collective-permute-done((f32[1216,128]{1,0:T(8,128)S(1)}, f32[1216,128]{1,0:T(8,128)S(1)}, u32[]{:S(2)}, u32[]{:S(2)}) %collective-permute-start.10) | collective-permute-done | bytes 622624 | tf_op jit(solution)/shard_map/ppermute | solution.py:555
  85.3 0.7 collective-permute-start.12
  85.9 0.0 collective-permute-start.13
  85.9 2.4 %collective-permute-done.13.pkall = f32[24,40,128]{2,1,0:T(8,128)S(1)} collective-permute-done((f32[24,40,128]{2,1,0:T(8,128)S(1)}, f32[24,40,128]{2,1,0:T(8,128)S(1)}, u32[]{:S(2)}, u32[]{:S(2)}) %collective-permute-start.13) | collective-permute-done | bytes 491552 | tf_op jit(solution)/shard_map/ppermute | solution.py:513
  88.3 1.3 %shard_map.43 = (f32[40,40,128]{2,1,0:T(8,128)S(1)}, f32[40,40,128]{2,1,0:T(8,128)S(1)}, f32[40,40,128]{2,1,0:T(8,128)S(1)}, f32[40,40,128]{2,1,0:T(8,128)S(1)}, f32[40,40,128]{2,1,0:T(8,128)S(1)}) custom-call(f32[24,40,128]{2,1,0:T(8,128)S(1)} %get-tuple-element.83.kall, f32[24,40,128]{2,1,0:T(8,128)S(1)} %collective-permute-done.13.pkall), custom_call_target="tpu_custom_call" | custom-call | tf_op jit(solution)/shard_map/pallas_call | solution.py:482
  89.7 7.2 %shard_map.44 = f32[16,4,8,128]{3,2,1,0:T(8,128)} custom-call(f32[8,8,40,128]{3,2,1,0:T(8,128)S(1)} %bitcast.3, f32[8,8,40,128]{3,2,1,0:T(8,128)S(1)} %collective-permute-done.8.part, f32[1216,128]{1,0:T(8,128)S(1)} %collective-permute-done.9.even, f32[1216,128]{1,0:T(8,128)S(1)} %collective-permute-done.10.odd, ...), custom_call_target="tpu_custom_call" | custom-call | tf_op jit(solution)/shard_map/pallas_call | solution.py:482
  96.8 3.5 %all-to-all-start.1 = ((f32[16,4,8,128]{3,2,1,0:T(8,128)}), f32[16,4,8,128]{3,2,1,0:T(8,128)S(1)}, u32[]{:S(2)}, u32[]{:S(2)}) async-start(f32[16,4,8,128]{3,2,1,0:T(8,128)} %shard_map.44), calls=%async_computation.1 | async-start | bytes 524288 | tf_op jit(solution)/shard_map/all_to_all | solution.py:567
  100.4 7.3 %all-to-all-done.1.y_in = f32[16,4,8,128]{3,2,1,0:T(8,128)S(1)} async-done(((f32[16,4,8,128]{3,2,1,0:T(8,128)}), f32[16,4,8,128]{3,2,1,0:T(8,128)S(1)}, u32[]{:S(2)}, u32[]{:S(2)}) %all-to-all-start.1) | async-done | bytes 262176 | tf_op jit(solution)/shard_map/all_to_all | solution.py:567
  107.7 1.1 shard_map.45
  (10 shorter events, 0.0 us)
Async XLA Ops:
  0.0 7.3 %copy-start = (f32[8,256,128]{2,1,0:T(8,128)S(1)}, f32[8,256,128]{2,1,0:T(8,128)}, u32[]{:S(2)}) copy-start(f32[8,256,128]{2,1,0:T(8,128)} %src.9) | copy-start | bytes 3145732
  3.0 19.2 %collective-permute-start = (f32[1152,128]{1,0:T(8,128)S(1)}, f32[1152,128]{1,0:T(8,128)S(1)}, u32[]{:S(2)}, u32[]{:S(2)}) collective-permute-start(f32[1152,128]{1,0:T(8,128)S(1)} %get-tuple-element.47.sc), channel_id=1, source_target_pairs={{0,1},{1,0},{2,3},{3,2},{4,5},{5,4},{6,7},{7,6},{8,9},{9,8},{10,11... | collective-permute-start | bytes 1769480 | tf_op jit(solution)/shard_map/ppermute | solution.py:513
  6.3 18.0 %collective-permute-start.1 = (f32[1152,128]{1,0:T(8,128)S(1)}, f32[1152,128]{1,0:T(8,128)S(1)}, u32[]{:S(2)}, u32[]{:S(2)}) collective-permute-start(f32[1152,128]{1,0:T(8,128)S(1)} %get-tuple-element.48.so), channel_id=1, source_target_pairs={{1,2},{2,1},{3,4},{4,3},{5,6},{6,5},{7,8},{8,7},{9,10},{10,9},{11,... | collective-permute-start | bytes 1769480 | tf_op jit(solution)/shard_map/ppermute | solution.py:516
  10.2 12.0 %collective-permute-start.2 = (f32[4,40,128]{2,1,0:T(8,128)S(1)}, f32[4,40,128]{2,1,0:T(8,128)S(1)}, u32[]{:S(2)}, u32[]{:S(2)}) collective-permute-start(f32[4,40,128]{2,1,0:T(8,128)S(1)} %get-tuple-element.56), channel_id=1, source_target_pairs={{0,2},{2,0},{1,3},{3,1},{4,6},{6,4},{5,7},{7,5},{8,10},{10,8},{9,1... | collective-permute-start | bytes 245768 | tf_op jit(solution)/shard_map/ppermute | solution.py:532
  26.3 12.3 %collective-permute-start.3 = (f32[512,128]{1,0:T(8,128)S(1)}, f32[512,128]{1,0:T(8,128)S(1)}, u32[]{:S(2)}, u32[]{:S(2)}) collective-permute-start(f32[512,128]{1,0:T(8,128)S(1)} %get-tuple-element.64), channel_id=1, source_target_pairs={{0,1},{1,0},{2,3},{3,2},{4,5},{5,4},{6,7},{7,6},{8,9},{9,8},{10,11... | collective-permute-start | bytes 786440 | tf_op jit(solution)/shard_map/ppermute | solution.py:513
  27.9 10.7 %collective-permute-start.4 = (f32[512,128]{1,0:T(8,128)S(1)}, f32[512,128]{1,0:T(8,128)S(1)}, u32[]{:S(2)}, u32[]{:S(2)}) collective-permute-start(f32[512,128]{1,0:T(8,128)S(1)} %get-tuple-element.65), channel_id=1, source_target_pairs={{1,2},{2,1},{3,4},{4,3},{5,6},{6,5},{7,8},{8,7},{9,10},{10,9},{11,... | collective-permute-start | bytes 786440 | tf_op jit(solution)/shard_map/ppermute | solution.py:516
  28.1 9.6 %collective-permute-start.6 = (f32[8,40,128]{2,1,0:T(8,128)S(1)}, f32[8,40,128]{2,1,0:T(8,128)S(1)}, u32[]{:S(2)}, u32[]{:S(2)}) collective-permute-start(f32[8,40,128]{2,1,0:T(8,128)S(1)} %get-tuple-element.76.kown), channel_id=1, source_target_pairs={{4,8},{8,4},{12,16},{16,12},{20,24},{24,20},{0,28},{28,0},{5,9},{9... | collective-permute-start | bytes 491528 | tf_op jit(solution)/shard_map/ppermute | solution.py:542
  33.7 4.9 %collective-permute-start.5 = (f32[8,40,128]{2,1,0:T(8,128)S(1)}, f32[8,40,128]{2,1,0:T(8,128)S(1)}, u32[]{:S(2)}, u32[]{:S(2)}) collective-permute-start(f32[8,40,128]{2,1,0:T(8,128)S(1)} %get-tuple-element.76.kown), channel_id=1, source_target_pairs={{0,4},{4,0},{8,12},{12,8},{16,20},{20,16},{24,28},{28,24},{1,5},{5... | collective-permute-start | bytes 491528 | tf_op jit(solution)/shard_map/ppermute | solution.py:541
  64.2 25.4 %collective-permute-start.8 = (f32[8,8,40,128]{3,2,1,0:T(8,128)S(1)}, f32[8,8,40,128]{3,2,1,0:T(8,128)S(1)}, u32[]{:S(2)}, u32[]{:S(2)}) collective-permute-start(f32[8,8,40,128]{3,2,1,0:T(8,128)S(1)} %bitcast.1), channel_id=1, source_target_pairs={{0,1},{1,0},{2,3},{3,2},{4,5},{5,4},{6,7},{7,6},{8,9},{9,8},{10,11... | collective-permute-start | bytes 3932168 | tf_op jit(solution)/shard_map/ppermute | solution.py:513
  66.8 15.7 %collective-permute-start.9 = (f32[1216,128]{1,0:T(8,128)S(1)}, f32[1216,128]{1,0:T(8,128)S(1)}, u32[]{:S(2)}, u32[]{:S(2)}) collective-permute-start(f32[1216,128]{1,0:T(8,128)S(1)} %get-tuple-element.81), channel_id=1, source_target_pairs={{0,4},{4,0},{8,12},{12,8},{16,20},{20,16},{24,28},{28,24},{1,5},{5... | collective-permute-start | bytes 1867784 | tf_op jit(solution)/shard_map/ppermute | solution.py:554
  66.9 18.3 %collective-permute-start.10 = (f32[1216,128]{1,0:T(8,128)S(1)}, f32[1216,128]{1,0:T(8,128)S(1)}, u32[]{:S(2)}, u32[]{:S(2)}) collective-permute-start(f32[1216,128]{1,0:T(8,128)S(1)} %get-tuple-element.82), channel_id=1, source_target_pairs={{4,8},{8,4},{12,16},{16,12},{20,24},{24,20},{0,28},{28,0},{5,9},{9... | collective-permute-start | bytes 1867784 | tf_op jit(solution)/shard_map/ppermute | solution.py:555
  70.9 29.4 %collective-permute-start.7 = (f32[8,256,128]{2,1,0:T(8,128)S(1)}, f32[8,256,128]{2,1,0:T(8,128)S(1)}, u32[]{:S(2)}, u32[]{:S(2)}) collective-permute-start(f32[8,256,128]{2,1,0:T(8,128)S(1)} %get-tuple-element.79), channel_id=1, source_target_pairs={{0,32},{32,64},{64,96},{96,128},{128,160},{160,192},{192,224},{224... | collective-permute-start | bytes 3145736 | tf_op jit(solution)/shard_map/ppermute | solution.py:557
  82.5 7.1 %collective-permute-start.11 = (f32[1216,128]{1,0:T(8,128)S(1)}, f32[1216,128]{1,0:T(8,128)S(1)}, u32[]{:S(2)}, u32[]{:S(2)}) collective-permute-start(f32[1216,128]{1,0:T(8,128)S(1)} %collective-permute-done.9.even), channel_id=1, source_target_pairs={{0,1},{1,0},{2,3},{3,2},{4,5},{5,4},{6,7},{7,6},{8,9},{9,8},{10,11... | collective-permute-start | bytes 1867784 | tf_op jit(solution)/shard_map/ppermute | solution.py:513
  85.3 4.4 %collective-permute-start.12 = (f32[1216,128]{1,0:T(8,128)S(1)}, f32[1216,128]{1,0:T(8,128)S(1)}, u32[]{:S(2)}, u32[]{:S(2)}) collective-permute-start(f32[1216,128]{1,0:T(8,128)S(1)} %collective-permute-done.10.odd), channel_id=1, source_target_pairs={{0,1},{1,0},{2,3},{3,2},{4,5},{5,4},{6,7},{7,6},{8,9},{9,8},{10,11... | collective-permute-start | bytes 1867784 | tf_op jit(solution)/shard_map/ppermute | solution.py:513
  85.9 2.4 %collective-permute-start.13 = (f32[24,40,128]{2,1,0:T(8,128)S(1)}, f32[24,40,128]{2,1,0:T(8,128)S(1)}, u32[]{:S(2)}, u32[]{:S(2)}) collective-permute-start(f32[24,40,128]{2,1,0:T(8,128)S(1)} %get-tuple-element.83.kall), channel_id=1, source_target_pairs={{0,1},{1,0},{2,3},{3,2},{4,5},{5,4},{6,7},{7,6},{8,9},{9,8},{10,11... | collective-permute-start | bytes 1474568 | tf_op jit(solution)/shard_map/ppermute | solution.py:513
  96.8 10.9 %all-to-all-start.1 = ((f32[16,4,8,128]{3,2,1,0:T(8,128)}), f32[16,4,8,128]{3,2,1,0:T(8,128)S(1)}, u32[]{:S(2)}, u32[]{:S(2)}) async-start(f32[16,4,8,128]{3,2,1,0:T(8,128)} %shard_map.44), calls=%async_computation.1 | async-start | bytes 524288 | tf_op jit(solution)/shard_map/all_to_all | solution.py:567

commit v3 on v2

--- a/solution.py
+++ b/solution.py
@@ -4,6 +4,7 @@
 from jax.experimental import pallas as pl
 from jax.experimental.pallas import tpu as pltpu
 from jax.sharding import Mesh, PartitionSpec as P
+
 
 SIZES = (4, 2, 8, 2, 2)
 AXES = ("y", "l", "z", "h", "c")
@@ -21,18 +22,22 @@
 
 BLOCKS = 16
 YB = CY // BLOCKS
-YM = 16
+YM = 14
+WM = 16
 YW = YB + 2 * YM
 XH = 14
 XW = 12 + 2 * XH
 XALL = 48
 KEEP = (8, 8, 6, 4, 4, 4, 2)
-YCUT = (0, 0, 0, 8, 8, 8, 8)
+YCUT = (0, 2, 4, 6, 8, 10, 12)
 WIDE = tuple(YW - 2 * cut for cut in YCUT)
 STARTS = tuple(sum(KEEP[i] * WIDE[i] for i in range(j)) for j in range(8))
 NSEND = STARTS[7]
-
-EK, EU, E1, EKC, EUC, E1C, EDGE = 0, 256, 512, 768, 896, 1024, 1152
+KW = YB + 2 * WM
+OFF = WM - YM
+
+EK, EU, E1, EDGE = 0, 256, 512, 768
+EKC, EUC, E1C, CEDGE = 0, 128, 256, 384
 
 F32 = jnp.float32
 
@@ -154,7 +159,7 @@
     return jnp.where(index > 0, F32(1), F32(0)), jnp.where(index < 31, F32(1), F32(0))
 
 
-def first_kernel(u_in, mat, src, sc, so, kp, up, kcp, ucp, edge, numbers, ends, u_sem, m_sem, s_sem):
+def first_kernel(u_in, mat, src, sc, so, kp, up, edge, numbers, ends, u_sem, m_sem, s_sem):
     inside = pl.ds(PAD, NY)
     order = (0, 7, 1, 6, 2, 5, 3, 4)
     for side, r in ((0, 0), (1, ROWS - 1)):
@@ -164,8 +169,6 @@
         pltpu.make_async_copy(u_in.at[0, r], up.at[r, inside], u_sem.at[r]).start()
     clear_margin(kp, NY)
     clear_margin(up, NY)
-    clear_margin(kcp, CY)
-    clear_margin(ucp, CY)
     for r in order:
         pltpu.make_async_copy(mat.at[r], numbers.at[r], m_sem.at[r]).wait()
         for a, n in pieces(NY):
@@ -174,32 +177,32 @@
         pltpu.make_async_copy(u_in.at[0, r], up.at[r, inside], u_sem.at[r]).wait()
     for side, r in ((0, 0), (1, ROWS - 1)):
         pltpu.make_async_copy(src.at[r], ends.at[side], s_sem.at[side]).wait()
-    for x in range(HALF):
-        kcp[x, PAD : PAD + CY] = halve(kp, x, PAD)
-        ucp[x, PAD : PAD + CY] = halve(up, x, PAD)
-    for side, r, x in ((0, 0, 0), (1, ROWS - 1, HALF - 1)):
+    for side, r in ((0, 0), (1, ROWS - 1)):
         for a, n in pieces(NY):
             edge[side, EK + a : EK + a + n] = kp[r, PAD + a : PAD + a + n]
             edge[side, EU + a : EU + a + n] = up[r, PAD + a : PAD + a + n]
             edge[side, E1 + a : E1 + a + n] = edge_sweep(kp, up, side, ROWS, a, n, *FINE_W) + FINE * ends[side, a : a + n]
-        for a, n in pieces(CY):
-            edge[side, EKC + a : EKC + a + n] = kcp[x, PAD + a : PAD + a + n]
-            edge[side, EUC + a : EUC + a + n] = ucp[x, PAD + a : PAD + a + n]
-            edge[side, E1C + a : E1C + a + n] = edge_sweep(kcp, ucp, side, HALF, a, n, *COARSE_W)
     c = place("c")
     sc[...] = edge[1 - c]
     so[...] = edge[c]
 
 
-def coef_kernel(kp, up, src, kcp, ucp, cx, cyp, cym, cz, dg, ccx, ccyp, ccym, ccz, cdg, b1, cb1, strip, strip_h, kw):
+def coef_kernel(
+    kp, up, src, cx, cyp, cym, cz, dg, ccx, ccyp, ccym, ccz, cdg, b1, cb1, ucp, csc, cso, strip, strip_h, kw, kcp, edge,
+):
+    clear_margin(kcp, CY)
+    clear_margin(ucp, CY)
+    for x in range(HALF):
+        kcp[x, PAD : PAD + CY] = halve(kp, x, PAD)
+        ucp[x, PAD : PAD + CY] = halve(up, x, PAD)
     clear_margin(b1, NY)
     clear_margin(cb1, CY)
-    kw[:, 0:YM] = jnp.zeros((HALF, YM, NZ), F32)
-    kw[:, YM + CY : YM + CY + YM] = jnp.zeros((HALF, YM, NZ), F32)
-    kw[:, YM : YM + CY] = kcp[:, PAD : PAD + CY]
+    kw[:, 0:WM] = jnp.zeros((HALF, WM, NZ), F32)
+    kw[:, WM + CY : WM + CY + WM] = jnp.zeros((HALF, WM, NZ), F32)
+    kw[:, WM : WM + CY] = kcp[:, PAD : PAD + CY]
     h = place("h")
-    strip[...] = kw[:, pl.ds(pl.multiple_of(block_of(h) * YB, 8), YW)]
-    strip_h[...] = kw[:, pl.ds(pl.multiple_of(block_of(1 - h) * YB, 8), YW)]
+    strip[...] = kw[:, pl.ds(pl.multiple_of(block_of(h) * YB, 8), KW)]
+    strip_h[...] = kw[:, pl.ds(pl.multiple_of(block_of(1 - h) * YB, 8), KW)]
 
     def make(k, u, n_all, weights, outs, target, source):
         fx, fyp, fym, fz, fd = outs
@@ -222,6 +225,13 @@
 
     make(kp, up, NY, FINE_W, (cx, cyp, cym, cz, dg), b1, src)
     make(kcp, ucp, CY, COARSE_W, (ccx, ccyp, ccym, ccz, cdg), cb1, None)
+    c = place("c")
+    for side, x in ((0, 0), (1, HALF - 1)):
+        edge[side, EKC : EKC + CY] = kcp[x, PAD : PAD + CY]
+        edge[side, EUC : EUC + CY] = ucp[x, PAD : PAD + CY]
+        edge[side, E1C : E1C + CY] = cb1[x, PAD : PAD + CY]
+    csc[...] = edge[1 - c]
+    cso[...] = edge[c]
 
 
 def fix_rows(target, old, swept, halo, face, rows, width):
@@ -260,7 +270,7 @@
 
 
 def second_kernel(
-    src, sc, so, rc, ro, up, ucp, b1, cb1, strip, strip_h, cx, cyp, cym, cz, dg, u2, faces, c1, cfaces, cstore, tc, to, kown, own, got, store, edge, u1,
+    src, sc, so, rc, ro, up, b1, strip, strip_h, cx, cyp, cym, cz, dg, u2, faces, tc, to, kown, own, got, store, edge, u1,
 ):
     c = place("c")
     h = place("h")
@@ -275,8 +285,6 @@
         got[side] = got[side] * live[side]
         for a, n in pieces(NY):
             faces[side, a : a + n] = (0.5 * FINE) * (own[side, EK + a : EK + a + n] + got[side, EK + a : EK + a + n])
-        for a, n in pieces(CY):
-            cfaces[side, a : a + n] = (0.125 * COARSE) * (own[side, EKC + a : EKC + a + n] + got[side, EKC + a : EKC + a + n])
     clear_margin(u2, NY)
     halo_after(store, up, reader(got, EU), reader(got, E1), reader(faces), live, ROWS, NY)
     fix_rows(u1, up, b1, reader(got, EU), reader(faces), ROWS, NY)
@@ -288,11 +296,23 @@
             edge[side, NY + a : NY + a + n] = base(u2, r, a, n, *coefs, side == 1, side == 0) + FINE * src[r, a : a + n]
     tc[...] = edge[1 - c]
     to[...] = edge[c]
+
+
+def middle_kernel(
+    u2, src, csc, cso, crc, cro, ucp, cb1, cx, cyp, cym, cz, dg, ccx, ccyp, ccym, ccz, cdg, b3, au, own, got, cfaces, cstore, c1,
+):
+    c = place("c")
+    live = lives()
+    own[1 - c] = csc[...]
+    own[c] = cso[...]
+    got[1 - c] = crc[...]
+    got[c] = cro[...]
+    for side in range(2):
+        got[side] = got[side] * live[side]
+        for a, n in pieces(CY):
+            cfaces[side, a : a + n] = (0.125 * COARSE) * (own[side, EKC + a : EKC + a + n] + got[side, EKC + a : EKC + a + n])
     halo_after(cstore, ucp, reader(got, EUC), reader(got, E1C), reader(cfaces), live, HALF, CY)
     fix_rows(c1, ucp, cb1, reader(got, EUC), reader(cfaces), HALF, CY)
-
-
-def middle_kernel(u2, src, c1, cstore, cfaces, cx, cyp, cym, cz, dg, ccx, ccyp, ccym, ccz, cdg, b3, au):
     clear_margin(b3, NY)
     clear_margin(au, CY)
 
@@ -320,8 +340,8 @@
     fix_rows(u3, u2, b3, reader(got), reader(faces), ROWS, NY)
     full_sweep(f, u3, store, reader(faces), ROWS, NY, (cx, cyp, cym, cz, dg), src)
     keep = jnp.where(place("y") + place("l") > 0, F32(1), F32(0))
-    wp[:, 0:YM] = jnp.zeros((HALF, YM, NZ), F32)
-    wp[:, YM + CY : YM + CY + YM] = jnp.zeros((HALF, YM, NZ), F32)
+    wp[:, 0:WM] = jnp.zeros((HALF, WM, NZ), F32)
+    wp[:, WM + CY : WM + CY + WM] = jnp.zeros((HALF, WM, NZ), F32)
     for x in range(HALF):
         coarse = keep * au[x, PAD : PAD + CY]
         total = None
@@ -330,9 +350,10 @@
                 part = f[2 * x + p, pl.ds(PAD + q, CY, 2), :] - coarse
                 h_out[2 * x + p, pl.ds(q, CY, 2), :] = part
                 total = part if total is None else total + part
-        wp[x, YM : YM + CY] = 0.25 * total
+        wp[x, WM : WM + CY] = 0.25 * total
     for b in range(BLOCKS):
-        strips[b] = wp[:, b * YB : b * YB + YW]
+        for x in range(HALF):
+            strips[b, x * YW : (x + 1) * YW] = wp[x, b * YB + WM - YM : b * YB + WM - YM + YW]
 
 
 def pack_kernel(own, even, odd):
@@ -341,8 +362,10 @@
         n, cut, wide = KEEP[j], YCUT[j], WIDE[j]
         for t in range(n):
             at = STARTS[j] + t * wide
-            even[at : at + wide] = own[j, up * (8 - n) + t, cut : cut + wide]
-            odd[at : at + wide] = own[j, (1 - up) * (8 - n) + t, cut : cut + wide]
+            high = own[j, (8 - n + t) * YW + cut : (8 - n + t) * YW + cut + wide]
+            low = own[j, t * YW + cut : t * YW + cut + wide]
+            even[at : at + wide] = jnp.where(up == 1, high, low)
+            odd[at : at + wide] = jnp.where(up == 1, low, high)
 
 
 def position(i):
@@ -357,16 +380,16 @@
     high = jnp.where(z < 7, F32(1), F32(0))
     first = 4 * c + 16 - XH
     kp[:, 0:PAD] = jnp.zeros((XALL, PAD, NZ), F32)
-    kp[:, PAD + YW : PAD + YW + PAD] = jnp.zeros((XALL, PAD, NZ), F32)
+    kp[:, PAD + KW : PAD + KW + PAD] = jnp.zeros((XALL, PAD, NZ), F32)
     for core, k_ref in ((c, kall), (1 - c, pkall)):
         shift = 16 + 4 * core
         for i in range(8):
-            kp[shift + position(i), PAD : PAD + YW] = k_ref[i]
-
-            kp[shift + position(i) - 16, PAD : PAD + YW] = k_ref[8 * (1 + is_up) + i] * low
-            kp[shift + position(i) + 16, PAD : PAD + YW] = k_ref[8 * (2 - is_up) + i] * high
-
-    ycell = block_of(place("h")) * YB - YM + lax.broadcasted_iota(jnp.int32, (YW, NZ), 0)
+            kp[shift + position(i), PAD : PAD + KW] = k_ref[i]
+
+            kp[shift + position(i) - 16, PAD : PAD + KW] = k_ref[8 * (1 + is_up) + i] * low
+            kp[shift + position(i) + 16, PAD : PAD + KW] = k_ref[8 * (2 - is_up) + i] * high
+
+    ycell = block_of(place("h")) * YB - WM + lax.broadcasted_iota(jnp.int32, (KW, NZ), 0)
     ymask = jnp.where((ycell >= 0) & (ycell < CY), F32(1), F32(0))
     wx, _, wz = COARSE_W
 
@@ -374,12 +397,12 @@
         for t in range(4):
             r = 4 * g + t
             q = first + r
-            k = kp[q, PAD : PAD + YW]
-            a = wx * (k + kp[q, PAD + 1 : PAD + YW + 1])
-            b = wx * (k + kp[q, PAD - 1 : PAD + YW - 1])
+            k = kp[q, PAD : PAD + KW]
+            a = wx * (k + kp[q, PAD + 1 : PAD + KW + 1])
+            b = wx * (k + kp[q, PAD - 1 : PAD + KW - 1])
             zc, zsum = z_faces(k, wz)
-            above = wx * (k + kp[q + 1, PAD : PAD + YW])
-            below = wx * (k + kp[q - 1, PAD : PAD + YW])
+            above = wx * (k + kp[q + 1, PAD : PAD + KW])
+            below = wx * (k + kp[q - 1, PAD : PAD + KW])
             row = 16 * z + 4 * c - XH + r
             m = ymask * jnp.where((row >= 0) & (row < CY), F32(1), F32(0))
             m_above = ymask * jnp.where((row >= 0) & (row < CY - 1), F32(1), F32(0))
@@ -405,15 +428,15 @@
         shift = 16 + 4 * core
         for j in range(7):
             for i in range(8):
-                w[j, shift + position(i)] = mine[j, i]
+                w[j, shift + position(i), OFF : OFF + YW] = mine[j, i * YW : (i + 1) * YW]
 
         def fill(from_below, from_above):
             for j in range(7):
                 n, cut, wide = KEEP[j], YCUT[j], WIDE[j]
                 for t in range(n):
                     at = STARTS[j] + t * wide
-                    w[j, shift + position(8 - n + t) - 16, cut : cut + wide] = from_below[at : at + wide] * low
-                    w[j, shift + position(t) + 16, cut : cut + wide] = from_above[at : at + wide] * high
+                    w[j, shift + position(8 - n + t) - 16, OFF + cut : OFF + cut + wide] = from_below[at : at + wide] * low
+                    w[j, shift + position(t) + 16, OFF + cut : OFF + cut + wide] = from_above[at : at + wide] * high
 
         @pl.when(is_up)
         def _():
@@ -424,7 +447,7 @@
             fill(e_ref, o_ref)
 
     for r in range(XW):
-        ea[r, PAD : PAD + YW] = w[0, first + r]
+        ea[r, PAD : PAD + KW] = w[0, first + r]
 
     def halved(lo, hi, visit):
         half = (hi - lo) // 2
@@ -436,10 +459,10 @@
 
         lax.fori_loop(0, 2, body, 0)
 
-    def sweep(src, dst, number, added):
+    def sweep(src, dst, number):
         cut = 0 if number <= 5 else 8
-        s = slice(cut, YW - cut)
-        n = YW - 2 * cut
+        s = slice(cut, KW - cut)
+        n = KW - 2 * cut
 
         def visit(r):
             here = src[r, PAD + cut : PAD + cut + n]
@@ -453,18 +476,18 @@
 
     out[2:4] = jnp.zeros((2, HALF, YB, NZ), F32)
     for k in range(1, 8):
-        sweep(ea, eb, 2 * k - 1, None)
-        sweep(eb, ea, 2 * k, None)
+        sweep(ea, eb, 2 * k - 1)
+        sweep(eb, ea, 2 * k)
         m = (k + 1) % SLABS
         for side in range(2):
             for i in range(HALF):
-                out[2 * m + side, i] = ea[XH + 8 * side + i, PAD + YM : PAD + YM + YB]
+                out[2 * m + side, i] = ea[XH + 8 * side + i, PAD + WM : PAD + WM + YB]
         if k < 7:
-            cut = YCUT[k]
-            s = slice(PAD + cut, PAD + YW - cut)
+            cut = 8 if k >= 3 else 0
+            s = slice(PAD + cut, PAD + KW - cut)
 
             def add(r):
-                ea[r, s] = ea[r, s] + w[k, first + r, cut : YW - cut]
+                ea[r, s] = ea[r, s] + w[k, first + r, cut : KW - cut]
 
             halved(2 * k, XW - 2 * k, add)
 
@@ -477,7 +500,7 @@
                 out[0, 2 * x + p, pl.ds(q, CY, 2), :] = h_in[2 * x + p, pl.ds(q, CY, 2), :] + fix
 
 
-def call(kernel, outs, scratch, *operands, limit=10, specs=None):
+def call(kernel, outs, scratch, *operands, limit=6, specs=None):
     vmem = pl.BlockSpec(memory_space=pltpu.VMEM)
     return pl.pallas_call(
         kernel,
@@ -502,12 +525,12 @@
 PLANE = ("y", "l", "h")
 
 
-def local(starts, material, source):
+def steps(starts, material, source):
     fine = (ROWS, NY, NZ)
     crs = (HALF, CY, NZ)
     padded = (ROWS, NY + 2 * PAD, NZ)
     cpad = (HALF, CY + 2 * PAD, NZ)
-    strip_shape = (HALF, YW, NZ)
+    strip_shape = (HALF, KW, NZ)
 
     def swap_c(x):
         return lax.ppermute(x, "c", pairs(2, 0))
@@ -516,53 +539,62 @@
         return lax.ppermute(x, SPACE, pairs(32, 1))
 
     dma = pltpu.SemaphoreType.DMA
-    sc, so, kp, up, kcp, ucp = call(
+    sc, so, kp, up = call(
         first_kernel,
-        ((EDGE, NZ), (EDGE, NZ), padded, padded, cpad, cpad),
+        ((EDGE, NZ), (EDGE, NZ), padded, padded),
         ((2, EDGE, NZ), pltpu.VMEM(fine, jnp.int32), (2, NY, NZ), dma((ROWS,)), dma((ROWS,)), dma((2,))),
         *(pltpu.with_memory_space_constraint(x, pltpu.HBM) for x in (starts, material, source)),
         specs=[pl.BlockSpec(memory_space=pltpu.HBM)] * 3,
     )
     rc = swap_c(sc)
     ro = swap_o(so)
-    *coefs, b1, cb1, strip, strip_h = call(
-        coef_kernel, (fine,) * 5 + (crs,) * 5 + (padded, cpad, strip_shape, strip_shape), ((HALF, CY + 2 * YM, NZ),),
-        kp, up, source, kcp, ucp,
+    edges = (CEDGE, NZ)
+    *coefs, b1, cb1, ucp, csc, cso, strip, strip_h = call(
+        coef_kernel, (fine,) * 5 + (crs,) * 5 + (padded, cpad, cpad, edges, edges, strip_shape, strip_shape),
+        ((HALF, CY + 2 * WM, NZ), cpad, (2, CEDGE, NZ)),
+        kp, up, source,
     )
     strip_h = lax.ppermute(strip_h, "h", pairs(2, 0))
-    u2, faces, c1, cfaces, cstore, tc, to, kown = call(
+    strip_h, csc, cso = lax.optimization_barrier((strip_h, csc, cso))
+    cro = swap_o(cso)
+    crc = swap_c(csc)
+    u2, faces, tc, to, kown = call(
         second_kernel,
-        (padded, (2, NY, NZ), cpad, (2, CY, NZ), (2, CY, NZ), (2 * NY, NZ), (2 * NY, NZ), (8, YW, NZ)),
+        (padded, (2, NY, NZ), (2 * NY, NZ), (2 * NY, NZ), (8, KW, NZ)),
         ((2, EDGE, NZ), (2, EDGE, NZ), (2, NY, NZ), (2, 2 * NY, NZ), padded),
-        source, sc, so, rc, ro, up, ucp, b1, cb1, strip, strip_h, *coefs[:5],
+        source, sc, so, rc, ro, up, b1, strip, strip_h, *coefs[:5],
     )
     rc2 = swap_c(tc)
     ro2 = swap_o(to)
     keven = lax.ppermute(kown, "z", pairs(8, 0))
     kodd = lax.ppermute(kown, "z", pairs(8, 1))
-    b3, au = call(middle_kernel, (padded, cpad), (), u2, source, c1, cstore, cfaces, *coefs)
+    b3, au = call(
+        middle_kernel, (padded, cpad), ((2, CEDGE, NZ), (2, CEDGE, NZ), (2, CY, NZ), (2, CY, NZ), cpad),
+        u2, source, csc, cso, crc, cro, ucp, cb1, *coefs,
+    )
     moved, strips, kall = call(
         third_kernel,
-        (fine, (BLOCKS, HALF, YW, NZ), (24, YW, NZ)),
-        ((2, 2 * NY, NZ), (2, NY, NZ), padded, padded, (HALF, CY + 2 * YM, NZ)),
+        (fine, (BLOCKS, HALF * YW, NZ), (24, KW, NZ)),
+        ((2, 2 * NY, NZ), (2, NY, NZ), padded, padded, (HALF, CY + 2 * WM, NZ)),
         u2, source, faces, rc2, ro2, b3, au, kown, keven, kodd, *coefs[:5],
     )
     own = lax.all_to_all(strips, PLANE, 0, 0, tiled=True)
-    own, moved = lax.optimization_barrier((own, moved))
-    own = own.reshape(SLABS, 8, YW, NZ)
+    own, moved, kall = lax.optimization_barrier((own, moved, kall))
+    own = own.reshape(SLABS, 8 * YW, NZ)
     even, odd = call(pack_kernel, ((NSEND, NZ), (NSEND, NZ)), (), own)
     even = lax.ppermute(even, "z", pairs(8, 0))
     odd = lax.ppermute(odd, "z", pairs(8, 1))
     part = swap_c(own)
+    pkall = swap_c(kall)
     moved = lax.ppermute(moved, ("y", "l"), [(i, (i + 1) % 8) for i in range(8)])
     peven = swap_c(even)
     podd = swap_c(odd)
-    dom = (XW + 1, YW + 2 * PAD, NZ)
-    flat = (XW, YW, NZ)
-    patch = call(patch_kernel, (flat,) * 5, ((XALL, YW + 2 * PAD, NZ),), kall, swap_c(kall))
+    dom = (XW + 1, KW + 2 * PAD, NZ)
+    flat = (XW, KW, NZ)
+    patch = call(patch_kernel, (flat,) * 5, ((XALL, KW + 2 * PAD, NZ),), kall, pkall)
     (fixes,) = call(
-        chain_kernel, ((BLOCKS, HALF, YB, NZ),), ((7, XALL, YW, NZ), dom, dom),
-        own, part, even, odd, peven, podd, *patch, limit=18,
+        chain_kernel, ((BLOCKS, HALF, YB, NZ),), ((7, XALL, KW, NZ), dom, dom),
+        own, part, even, odd, peven, podd, *patch, limit=12,
     )
     fixes = lax.all_to_all(fixes, PLANE, 0, 0, tiled=True)
     (result,) = call(last_kernel, ((1, ROWS, NY, NZ),), (), moved, fixes)
@@ -573,4 +605,4 @@
     refined = Mesh(mesh.devices.reshape(SIZES), AXES)
     in_specs = (P(("y", "l"), SPACE, None, None), P(SPACE, None, None), P(SPACE, None, None))
     out_specs = P(("y", "l"), SPACE, None, None)
-    return jax.shard_map(local, mesh=refined, in_specs=in_specs, out_specs=out_specs, check_vma=False)
+    return jax.shard_map(steps, mesh=refined, in_specs=in_specs, out_specs=out_specs, check_vma=False)

time: 109 us -> 106 us (0.972)
  waiting for transfers between devices: 38.6 us -> 35.2 us
  starting transfers between devices: 25.4 us -> 27.7 us
  blocking collectives: 24 us -> 21.9 us
    ppermute x6, waiting for transfers between devices: 26.8 us -> 18 us  [the longest x1 7.69 us: steps(): even = lax.ppermute(even, 'z', pairs(8, 0))]
    ppermute x2 -> x3, waiting for transfers between devices: 2.08 us -> 7.63 us  [swap_o(): return lax.ppermute(x, SPACE, pairs(32, 1))]
    ppermute x2 -> x3, starting transfers between devices: 1.17 us -> 4.35 us  [swap_o(): return lax.ppermute(x, SPACE, pairs(32, 1))]
    all_to_all x1, blocking collectives: 24 us -> 21.9 us  [steps(): own = lax.all_to_all(strips, PLANE, 0, 0, tiled=True)]
    ppermute x6, starting transfers between devices: 11.6 us -> 10.5 us  [the longest x1 4.67 us: steps(): odd = lax.ppermute(odd, 'z', pairs(8, 1))]
    ppermute x6 -> x7, starting transfers between devices: 9.05 us -> 9.37 us  [swap_c(): return lax.ppermute(x, 'c', pairs(2, 0))]
    ppermute x6 -> x7, waiting for transfers between devices: 2.39 us -> 2.22 us  [swap_c(): return lax.ppermute(x, 'c', pairs(2, 0))]
  transfers between devices with their start and end apart: 15 -> 17, of which waited for: 8 -> 6; matrix products, arithmetic and copies ran while one was open for 0% -> 0% of each run, Pallas kernels for 12% -> 14%
where the time goes in v3:
time: 106 us; the launch traced here: 105 us
  waiting for transfers between devices  35.2 us (33%)
  starting transfers between devices  27.7 us (26%)
  blocking collectives  21.9 us (21%)
  Pallas kernels  20.4 us (19%)
    all_to_all x1, blocking collectives, steps(): own = lax.all_to_all(strips, PLANE, 0, 0, tiled=True)  21.9 us
    pallas_call x9, Pallas kernels, call(): pl.pallas_call(kernel, out_shape=[jax.ShapeDtypeStruct(s, F32) for s in o...  20.4 us
    ppermute x7, starting transfers between devices, swap_c(): return lax.ppermute(x, 'c', pairs(2, 0))  9.37 us
    ppermute x1, waiting for transfers between devices, steps(): even = lax.ppermute(even, 'z', pairs(8, 0))  7.69 us
    ppermute x3, waiting for transfers between devices, swap_o(): return lax.ppermute(x, SPACE, pairs(32, 1))  7.63 us
    ppermute x1, waiting for transfers between devices, steps(): strip_h = lax.ppermute(strip_h, 'h', pairs(2, 0))  7.62 us
    all_to_all x1, waiting for transfers between devices, steps(): fixes = lax.all_to_all(fixes, PLANE, 0, 0, tiled=True)  7.39 us
    ppermute x1, starting transfers between devices, steps(): odd = lax.ppermute(odd, 'z', pairs(8, 1))  4.67 us
  transfers between devices with their start and end apart: 17, of which 6 were waited for; matrix products, arithmetic and copies ran while one was open for 0% of the time, Pallas kernels for 14%

profile of v3, /device:TPU:1, one launch (start us, length us, event | category | flops | bytes accessed | tf_op | source)
XLA Modules:
  0.0 105.4 jit_solution(4996778186577228557)
XLA Ops:
  0.0 2.6 %shard_map.37 = (f32[768,128]{1,0:T(8,128)S(1)}, f32[768,128]{1,0:T(8,128)S(1)}, f32[8,272,128]{2,1,0:T(8,128)S(1)}, f32[8,272,128]{2,1,0:T(8,128)S(1)}) custom-call(f32[1,8,256,128]{3,2,1,0:T(8,128)} %u_in.1, s32[8,256,128]{2,1,0:T(8,128)} %mat.1, f32[8,256,128]{2,1,0:T(8,128)} %src.9), custom_call_target="tpu_custom_call" | custom-call | tf_op jit(solution)/shard_map/pallas_call | solution.py:505
  2.6 3.3 %collective-permute-start = (f32[768,128]{1,0:T(8,128)S(1)}, f32[768,128]{1,0:T(8,128)S(1)}, u32[]{:S(2)}, u32[]{:S(2)}) collective-permute-start(f32[768,128]{1,0:T(8,128)S(1)} %get-tuple-element.49.sc), channel_id=1, source_target_pairs={{0,1},{1,0},{2,3},{3,2},{4,5},{5,4},{6,7},{7,6},{8,9},{9,8},{10,11... | collective-permute-start | bytes 1179656 | tf_op jit(solution)/shard_map/ppermute | solution.py:536
  5.9 1.0 collective-permute-start.1
  6.9 3.0 %shard_map.38 = (f32[8,256,128]{2,1,0:T(8,128)S(1)}, f32[8,256,128]{2,1,0:T(8,128)S(1)}, f32[8,256,128]{2,1,0:T(8,128)S(1)}, f32[8,256,128]{2,1,0:T(8,128)S(1)},...) custom-call(f32[8,272,128]{2,1,0:T(8,128)S(1)} %get-tuple-element.52, ...), custom_call_target="tpu_custom_call" | custom-call | tf_op jit(solution)/shard_map/pallas_call | solution.py:505
  10.0 1.7 %collective-permute-start.2 = (f32[4,40,128]{2,1,0:T(8,128)S(1)}, f32[4,40,128]{2,1,0:T(8,128)S(1)}, u32[]{:S(2)}, u32[]{:S(2)}) collective-permute-start(f32[4,40,128]{2,1,0:T(8,128)S(1)} %get-tuple-element.55), channel_id=1, source_target_pairs={{0,2},{2,0},{1,3},{3,1},{4,6},{6,4},{5,7},{7,5},{8,10},{10,8},{9,1... | collective-permute-start | bytes 245768 | tf_op jit(solution)/shard_map/ppermute | solution.py:557
  11.6 7.6 %collective-permute-done.2.strip_h = f32[4,40,128]{2,1,0:T(8,128)S(1)} collective-permute-done((f32[4,40,128]{2,1,0:T(8,128)S(1)}, f32[4,40,128]{2,1,0:T(8,128)S(1)}, u32[]{:S(2)}, u32[]{:S(2)}) %collective-permute-start.2) | collective-permute-done | bytes 81952 | tf_op jit(solution)/shard_map/ppermute | solution.py:557
  19.3 2.5 %collective-permute-start.5 = (f32[384,128]{1,0:T(8,128)S(1)}, f32[384,128]{1,0:T(8,128)S(1)}, u32[]{:S(2)}, u32[]{:S(2)}) collective-permute-start(f32[384,128]{1,0:T(8,128)S(1)} %get-tuple-element.68.csc), channel_id=1, source_target_pairs={{0,1},{1,0},{2,3},{3,2},{4,5},{5,4},{6,7},{7,6},{8,9},{9,8},{10,11... | collective-permute-start | bytes 589832 | tf_op jit(solution)/shard_map/ppermute | solution.py:536
  21.7 1.8 %shard_map.39 = (f32[8,272,128]{2,1,0:T(8,128)S(1)}, f32[2,256,128]{2,1,0:T(8,128)S(1)}, f32[512,128]{1,0:T(8,128)S(1)}, f32[512,128]{1,0:T(8,128)S(1)}, f32[8,40,128]{2,1,0:T(8,128)S(1)}) custom-call(f32[8,256,128]{2,1,0:T(8,128)S(1)} %copy-done, f32[768,128]{1,0:T(8,128)S(1)} %get-tuple-element.49.sc, f32[768,128]{1,0:T(8,128)S(1)} %get-tuple-element.50.so, ...), custom_call_target="tpu_custom_call" | custom-call | tf_op jit(solution)/shard_map/pallas_call | solution.py:505
  23.5 0.1 collective-permute-start.3
  23.7 0.4 collective-permute-start.4
  24.1 2.9 %collective-permute-start.6 = (f32[384,128]{1,0:T(8,128)S(1)}, f32[384,128]{1,0:T(8,128)S(1)}, u32[]{:S(2)}, u32[]{:S(2)}) collective-permute-start(f32[384,128]{1,0:T(8,128)S(1)} %get-tuple-element.69.cso), channel_id=1, source_target_pairs={{1,2},{2,1},{3,4},{4,3},{5,6},{6,5},{7,8},{8,7},{9,10},{10,9},{11,... | collective-permute-start | bytes 589832 | tf_op jit(solution)/shard_map/ppermute | solution.py:539
  27.0 3.4 %collective-permute-start.8 = (f32[8,40,128]{2,1,0:T(8,128)S(1)}, f32[8,40,128]{2,1,0:T(8,128)S(1)}, u32[]{:S(2)}, u32[]{:S(2)}) collective-permute-start(f32[8,40,128]{2,1,0:T(8,128)S(1)} %get-tuple-element.79.kown), channel_id=1, source_target_pairs={{4,8},{8,4},{12,16},{16,12},{20,24},{24,20},{0,28},{28,0},{5,9},{9... | collective-permute-start | bytes 491528 | tf_op jit(solution)/shard_map/ppermute | solution.py:570
  30.4 7.6 %collective-permute-done.6.cro = f32[384,128]{1,0:T(8,128)S(1)} collective-permute-done((f32[384,128]{1,0:T(8,128)S(1)}, f32[384,128]{1,0:T(8,128)S(1)}, u32[]{:S(2)}, u32[]{:S(2)}) %collective-permute-start.6) | collective-permute-done | bytes 196640 | tf_op jit(solution)/shard_map/ppermute | solution.py:539
  38.1 1.7 %shard_map.40 = (f32[8,272,128]{2,1,0:T(8,128)S(1)}, f32[4,144,128]{2,1,0:T(8,128)S(1)}) custom-call(f32[8,272,128]{2,1,0:T(8,128)S(1)} %get-tuple-element.64.u2, f32[8,256,128]{2,1,0:T(8,128)S(1)} %copy-done, f32[384,128]{1,0:T(8,128)S(1)} %get-tuple-element.68.csc, f32[384,128]{1,0:T(8,128)S(1)} %get-tuple-element.69.cso, ...), custom_call_target="tpu_custom_call" | custom-call | tf_op jit(solution)/shard_map/pallas_call | solution.py:505
  39.8 1.6 %shard_map.41 = (f32[8,256,128]{2,1,0:T(8,128)S(1)}, f32[16,144,128]{2,1,0:T(8,128)S(1)}, f32[24,40,128]{2,1,0:T(8,128)S(1)}) custom-call(f32[8,272,128]{2,1,0:T(8,128)S(1)} %get-tuple-element.64.u2, f32[8,256,128]{2,1,0:T(8,128)S(1)} %copy-done, f32[2,256,128]{2,1,0:T(8,128)S(1)} %get-tuple-element.65.faces, f32[512,128]{1,0:T(8,128)S(1)} %collective-permute-done.3.rc, ...), custom_call_target="tpu_custom_call" | custom-call | tf_op jit(solution)/shard_map/pallas_call | solution.py:505
  41.4 21.9 %all_to_all.10 = f32[16,144,128]{2,1,0:T(8,128)S(1)} all-to-all(f32[16,144,128]{2,1,0:T(8,128)S(1)} %get-tuple-element.80), channel_id=1, replica_groups=mesh['y'=4,'l'=2,'z'=8,'h'=2,'c'=2] {'y','l','h'}, dimensions={0} | all-to-all | bytes 2359296 | tf_op jit(solution)/shard_map/all_to_all | solution.py:581
  63.4 1.8 %collective-permute-start.10 = (f32[8,288,128]{2,1,0:T(8,128)S(1)}, f32[8,288,128]{2,1,0:T(8,128)S(1)}, u32[]{:S(2)}, u32[]{:S(2)}) collective-permute-start(f32[8,288,128]{2,1,0:T(8,128)S(1)} %bitcast.1), channel_id=1, source_target_pairs={{0,1},{1,0},{2,3},{3,2},{4,5},{5,4},{6,7},{7,6},{8,9},{9,8},{10,11... | collective-permute-start | bytes 3538952 | tf_op jit(solution)/shard_map/ppermute | solution.py:536
  65.2 0.1 shard_map.42
  65.2 0.4 collective-permute-start.11
  65.6 4.7 %collective-permute-start.12 = (f32[976,128]{1,0:T(8,128)S(1)}, f32[976,128]{1,0:T(8,128)S(1)}, u32[]{:S(2)}, u32[]{:S(2)}) collective-permute-start(f32[976,128]{1,0:T(8,128)S(1)} %get-tuple-element.86), channel_id=1, source_target_pairs={{4,8},{8,4},{12,16},{16,12},{20,24},{24,20},{0,28},{28,0},{5,9},{9... | collective-permute-start | bytes 1499144 | tf_op jit(solution)/shard_map/ppermute | solution.py:586
  70.3 0.3 collective-permute-start.9
  70.6 7.7 %collective-permute-done.11.even = f32[976,128]{1,0:T(8,128)S(1)} collective-permute-done((f32[976,128]{1,0:T(8,128)S(1)}, f32[976,128]{1,0:T(8,128)S(1)}, u32[]{:S(2)}, u32[]{:S(2)}) %collective-permute-start.11) | collective-permute-done | bytes 499744 | tf_op jit(solution)/shard_map/ppermute | solution.py:585
  78.3 0.9 collective-permute-start.13
  79.1 2.7 %collective-permute-done.12.odd = f32[976,128]{1,0:T(8,128)S(1)} collective-permute-done((f32[976,128]{1,0:T(8,128)S(1)}, f32[976,128]{1,0:T(8,128)S(1)}, u32[]{:S(2)}, u32[]{:S(2)}) %collective-permute-start.12) | collective-permute-done | bytes 499744 | tf_op jit(solution)/shard_map/ppermute | solution.py:586
  81.8 0.9 collective-permute-start.14
  82.6 0.0 collective-permute-start.15
  82.7 2.2 %collective-permute-done.15.pkall = f32[24,40,128]{2,1,0:T(8,128)S(1)} collective-permute-done((f32[24,40,128]{2,1,0:T(8,128)S(1)}, f32[24,40,128]{2,1,0:T(8,128)S(1)}, u32[]{:S(2)}, u32[]{:S(2)}) %collective-permute-start.15) | collective-permute-done | bytes 491552 | tf_op jit(solution)/shard_map/ppermute | solution.py:536
  84.9 1.3 %shard_map.43 = (f32[40,40,128]{2,1,0:T(8,128)S(1)}, f32[40,40,128]{2,1,0:T(8,128)S(1)}, f32[40,40,128]{2,1,0:T(8,128)S(1)}, f32[40,40,128]{2,1,0:T(8,128)S(1)}, f32[40,40,128]{2,1,0:T(8,128)S(1)}) custom-call(f32[24,40,128]{2,1,0:T(8,128)S(1)} %get-tuple-element.87.kall, f32[24,40,128]{2,1,0:T(8,128)S(1)} %collective-permute-done.15.pkall), custom_call_target="tpu_custom_call" | custom-call | tf_op jit(solution)/shard_map/pallas_call | solution.py:505
  86.2 7.2 %shard_map.44 = f32[16,4,8,128]{3,2,1,0:T(8,128)} custom-call(f32[8,288,128]{2,1,0:T(8,128)S(1)} %bitcast.3, f32[8,288,128]{2,1,0:T(8,128)S(1)} %collective-permute-done.10.part, f32[976,128]{1,0:T(8,128)S(1)} %collective-permute-done.11.even, f32[976,128]{1,0:T(8,128)S(1)} %collective-permute-done.12.odd, f32[976,128]{1,0:T(8,128)S(1)} %collective-permute-done.13.peven, ...), custom_call_target="tpu_custom_call" | custom-call | tf_op jit(solution)/shard_map/pallas_call | solution.py:505
  93.4 3.5 %all-to-all-start.1 = ((f32[16,4,8,128]{3,2,1,0:T(8,128)}), f32[16,4,8,128]{3,2,1,0:T(8,128)S(1)}, u32[]{:S(2)}, u32[]{:S(2)}) async-start(f32[16,4,8,128]{3,2,1,0:T(8,128)} %shard_map.44), calls=%async_computation.1 | async-start | bytes 524288 | tf_op jit(solution)/shard_map/all_to_all | solution.py:599
  96.9 7.4 %all-to-all-done.1.y_in = f32[16,4,8,128]{3,2,1,0:T(8,128)S(1)} async-done(((f32[16,4,8,128]{3,2,1,0:T(8,128)}), f32[16,4,8,128]{3,2,1,0:T(8,128)S(1)}, u32[]{:S(2)}, u32[]{:S(2)}) %all-to-all-start.1) | async-done | bytes 262176 | tf_op jit(solution)/shard_map/all_to_all | solution.py:599
  104.3 1.1 %shard_map.45 = f32[1,8,256,128]{3,2,1,0:T(8,128)} custom-call(f32[8,256,128]{2,1,0:T(8,128)S(1)} %collective-permute-done.9.h_in, f32[16,4,8,128]{3,2,1,0:T(8,128)S(1)} %all-to-all-done.1.y_in), custom_call_target="tpu_custom_call" | custom-call | tf_op jit(solution)/shard_map/pallas_call | solution.py:505
  (14 shorter events, 0.0 us)
Async XLA Ops:
  0.0 6.9 %copy-start = (f32[8,256,128]{2,1,0:T(8,128)S(1)}, f32[8,256,128]{2,1,0:T(8,128)}, u32[]{:S(2)}) copy-start(f32[8,256,128]{2,1,0:T(8,128)} %src.9) | copy-start | bytes 3145732
  2.6 19.1 %collective-permute-start = (f32[768,128]{1,0:T(8,128)S(1)}, f32[768,128]{1,0:T(8,128)S(1)}, u32[]{:S(2)}, u32[]{:S(2)}) collective-permute-start(f32[768,128]{1,0:T(8,128)S(1)} %get-tuple-element.49.sc), channel_id=1, source_target_pairs={{0,1},{1,0},{2,3},{3,2},{4,5},{5,4},{6,7},{7,6},{8,9},{9,8},{10,11... | collective-permute-start | bytes 1179656 | tf_op jit(solution)/shard_map/ppermute | solution.py:536
  5.9 15.8 %collective-permute-start.1 = (f32[768,128]{1,0:T(8,128)S(1)}, f32[768,128]{1,0:T(8,128)S(1)}, u32[]{:S(2)}, u32[]{:S(2)}) collective-permute-start(f32[768,128]{1,0:T(8,128)S(1)} %get-tuple-element.50.so), channel_id=1, source_target_pairs={{1,2},{2,1},{3,4},{4,3},{5,6},{6,5},{7,8},{8,7},{9,10},{10,9},{11,... | collective-permute-start | bytes 1179656 | tf_op jit(solution)/shard_map/ppermute | solution.py:539
  10.0 9.3 %collective-permute-start.2 = (f32[4,40,128]{2,1,0:T(8,128)S(1)}, f32[4,40,128]{2,1,0:T(8,128)S(1)}, u32[]{:S(2)}, u32[]{:S(2)}) collective-permute-start(f32[4,40,128]{2,1,0:T(8,128)S(1)} %get-tuple-element.55), channel_id=1, source_target_pairs={{0,2},{2,0},{1,3},{3,1},{4,6},{6,4},{5,7},{7,5},{8,10},{10,8},{9,1... | collective-permute-start | bytes 245768 | tf_op jit(solution)/shard_map/ppermute | solution.py:557
  19.3 11.2 %collective-permute-start.5 = (f32[384,128]{1,0:T(8,128)S(1)}, f32[384,128]{1,0:T(8,128)S(1)}, u32[]{:S(2)}, u32[]{:S(2)}) collective-permute-start(f32[384,128]{1,0:T(8,128)S(1)} %get-tuple-element.68.csc), channel_id=1, source_target_pairs={{0,1},{1,0},{2,3},{3,2},{4,5},{5,4},{6,7},{7,6},{8,9},{9,8},{10,11... | collective-permute-start | bytes 589832 | tf_op jit(solution)/shard_map/ppermute | solution.py:536
  23.5 16.2 %collective-permute-start.3 = (f32[512,128]{1,0:T(8,128)S(1)}, f32[512,128]{1,0:T(8,128)S(1)}, u32[]{:S(2)}, u32[]{:S(2)}) collective-permute-start(f32[512,128]{1,0:T(8,128)S(1)} %get-tuple-element.66), channel_id=1, source_target_pairs={{0,1},{1,0},{2,3},{3,2},{4,5},{5,4},{6,7},{7,6},{8,9},{9,8},{10,11... | collective-permute-start | bytes 786440 | tf_op jit(solution)/shard_map/ppermute | solution.py:536
  23.7 16.1 %collective-permute-start.4 = (f32[512,128]{1,0:T(8,128)S(1)}, f32[512,128]{1,0:T(8,128)S(1)}, u32[]{:S(2)}, u32[]{:S(2)}) collective-permute-start(f32[512,128]{1,0:T(8,128)S(1)} %get-tuple-element.67), channel_id=1, source_target_pairs={{1,2},{2,1},{3,4},{4,3},{5,6},{6,5},{7,8},{8,7},{9,10},{10,9},{11,... | collective-permute-start | bytes 786440 | tf_op jit(solution)/shard_map/ppermute | solution.py:539
  24.1 14.0 %collective-permute-start.6 = (f32[384,128]{1,0:T(8,128)S(1)}, f32[384,128]{1,0:T(8,128)S(1)}, u32[]{:S(2)}, u32[]{:S(2)}) collective-permute-start(f32[384,128]{1,0:T(8,128)S(1)} %get-tuple-element.69.cso), channel_id=1, source_target_pairs={{1,2},{2,1},{3,4},{4,3},{5,6},{6,5},{7,8},{8,7},{9,10},{10,9},{11,... | collective-permute-start | bytes 589832 | tf_op jit(solution)/shard_map/ppermute | solution.py:539
  27.0 12.8 %collective-permute-start.8 = (f32[8,40,128]{2,1,0:T(8,128)S(1)}, f32[8,40,128]{2,1,0:T(8,128)S(1)}, u32[]{:S(2)}, u32[]{:S(2)}) collective-permute-start(f32[8,40,128]{2,1,0:T(8,128)S(1)} %get-tuple-element.79.kown), channel_id=1, source_target_pairs={{4,8},{8,4},{12,16},{16,12},{20,24},{24,20},{0,28},{28,0},{5,9},{9... | collective-permute-start | bytes 491528 | tf_op jit(solution)/shard_map/ppermute | solution.py:570
  30.4 9.3 %collective-permute-start.7 = (f32[8,40,128]{2,1,0:T(8,128)S(1)}, f32[8,40,128]{2,1,0:T(8,128)S(1)}, u32[]{:S(2)}, u32[]{:S(2)}) collective-permute-start(f32[8,40,128]{2,1,0:T(8,128)S(1)} %get-tuple-element.79.kown), channel_id=1, source_target_pairs={{0,4},{4,0},{8,12},{12,8},{16,20},{20,16},{24,28},{28,24},{1,5},{5... | collective-permute-start | bytes 491528 | tf_op jit(solution)/shard_map/ppermute | solution.py:569
  63.4 22.8 %collective-permute-start.10 = (f32[8,288,128]{2,1,0:T(8,128)S(1)}, f32[8,288,128]{2,1,0:T(8,128)S(1)}, u32[]{:S(2)}, u32[]{:S(2)}) collective-permute-start(f32[8,288,128]{2,1,0:T(8,128)S(1)} %bitcast.1), channel_id=1, source_target_pairs={{0,1},{1,0},{2,3},{3,2},{4,5},{5,4},{6,7},{7,6},{8,9},{9,8},{10,11... | collective-permute-start | bytes 3538952 | tf_op jit(solution)/shard_map/ppermute | solution.py:536
  65.2 13.0 %collective-permute-start.11 = (f32[976,128]{1,0:T(8,128)S(1)}, f32[976,128]{1,0:T(8,128)S(1)}, u32[]{:S(2)}, u32[]{:S(2)}) collective-permute-start(f32[976,128]{1,0:T(8,128)S(1)} %get-tuple-element.85), channel_id=1, source_target_pairs={{0,4},{4,0},{8,12},{12,8},{16,20},{20,16},{24,28},{28,24},{1,5},{5... | collective-permute-start | bytes 1499144 | tf_op jit(solution)/shard_map/ppermute | solution.py:585
  65.6 16.2 %collective-permute-start.12 = (f32[976,128]{1,0:T(8,128)S(1)}, f32[976,128]{1,0:T(8,128)S(1)}, u32[]{:S(2)}, u32[]{:S(2)}) collective-permute-start(f32[976,128]{1,0:T(8,128)S(1)} %get-tuple-element.86), channel_id=1, source_target_pairs={{4,8},{8,4},{12,16},{16,12},{20,24},{24,20},{0,28},{28,0},{5,9},{9... | collective-permute-start | bytes 1499144 | tf_op jit(solution)/shard_map/ppermute | solution.py:586
  70.3 26.6 %collective-permute-start.9 = (f32[8,256,128]{2,1,0:T(8,128)S(1)}, f32[8,256,128]{2,1,0:T(8,128)S(1)}, u32[]{:S(2)}, u32[]{:S(2)}) collective-permute-start(f32[8,256,128]{2,1,0:T(8,128)S(1)} %get-tuple-element.83), channel_id=1, source_target_pairs={{0,32},{32,64},{64,96},{96,128},{128,160},{160,192},{192,224},{224... | collective-permute-start | bytes 3145736 | tf_op jit(solution)/shard_map/ppermute | solution.py:589
  78.3 7.9 %collective-permute-start.13 = (f32[976,128]{1,0:T(8,128)S(1)}, f32[976,128]{1,0:T(8,128)S(1)}, u32[]{:S(2)}, u32[]{:S(2)}) collective-permute-start(f32[976,128]{1,0:T(8,128)S(1)} %collective-permute-done.11.even), channel_id=1, source_target_pairs={{0,1},{1,0},{2,3},{3,2},{4,5},{5,4},{6,7},{7,6},{8,9},{9,8},{10,11... | collective-permute-start | bytes 1499144 | tf_op jit(solution)/shard_map/ppermute | solution.py:536
  81.8 4.4 %collective-permute-start.14 = (f32[976,128]{1,0:T(8,128)S(1)}, f32[976,128]{1,0:T(8,128)S(1)}, u32[]{:S(2)}, u32[]{:S(2)}) collective-permute-start(f32[976,128]{1,0:T(8,128)S(1)} %collective-permute-done.12.odd), channel_id=1, source_target_pairs={{0,1},{1,0},{2,3},{3,2},{4,5},{5,4},{6,7},{7,6},{8,9},{9,8},{10,11... | collective-permute-start | bytes 1499144 | tf_op jit(solution)/shard_map/ppermute | solution.py:536
  82.6 2.2 %collective-permute-start.15 = (f32[24,40,128]{2,1,0:T(8,128)S(1)}, f32[24,40,128]{2,1,0:T(8,128)S(1)}, u32[]{:S(2)}, u32[]{:S(2)}) collective-permute-start(f32[24,40,128]{2,1,0:T(8,128)S(1)} %get-tuple-element.87.kall), channel_id=1, source_target_pairs={{0,1},{1,0},{2,3},{3,2},{4,5},{5,4},{6,7},{7,6},{8,9},{9,8},{10,11... | collective-permute-start | bytes 1474568 | tf_op jit(solution)/shard_map/ppermute | solution.py:536
  93.4 10.9 %all-to-all-start.1 = ((f32[16,4,8,128]{3,2,1,0:T(8,128)}), f32[16,4,8,128]{3,2,1,0:T(8,128)S(1)}, u32[]{:S(2)}, u32[]{:S(2)}) async-start(f32[16,4,8,128]{3,2,1,0:T(8,128)} %shard_map.44), calls=%async_computation.1 | async-start | bytes 524288 | tf_op jit(solution)/shard_map/all_to_all | solution.py:599

commit v4 on v3

--- a/solution.py
+++ b/solution.py
@@ -188,7 +188,7 @@
 
 
 def coef_kernel(
-    kp, up, src, cx, cyp, cym, cz, dg, ccx, ccyp, ccym, ccz, cdg, b1, cb1, ucp, csc, cso, strip, strip_h, kw, kcp, edge,
+    kp, up, src, cx, cyp, cym, cz, dg, ccx, ccyp, ccym, ccz, cdg, b1, b2, cb1, ucp, csc, cso, strip, strip_h, kw, kcp, edge,
 ):
     clear_margin(kcp, CY)
     clear_margin(ucp, CY)
@@ -196,6 +196,7 @@
         kcp[x, PAD : PAD + CY] = halve(kp, x, PAD)
         ucp[x, PAD : PAD + CY] = halve(up, x, PAD)
     clear_margin(b1, NY)
+    clear_margin(b2, NY)
     clear_margin(cb1, CY)
     kw[:, 0:WM] = jnp.zeros((HALF, WM, NZ), F32)
     kw[:, WM + CY : WM + CY + WM] = jnp.zeros((HALF, WM, NZ), F32)
@@ -224,6 +225,7 @@
         each_row(u.shape[0], visit)
 
     make(kp, up, NY, FINE_W, (cx, cyp, cym, cz, dg), b1, src)
+    inner_rows(b2, b1, (cx, cyp, cym, cz, dg), src)
     make(kcp, ucp, CY, COARSE_W, (ccx, ccyp, ccym, ccz, cdg), cb1, None)
     c = place("c")
     for side, x in ((0, 0), (1, HALF - 1)):
@@ -234,12 +236,33 @@
     cso[...] = edge[c]
 
 
-def fix_rows(target, old, swept, halo, face, rows, width):
-    target[...] = swept[...]
+def inner_rows(dst, src_ref, coefs, source):
+    def body(r, carry):
+        for a, n in pieces(NY):
+            dst[r, PAD + a : PAD + a + n] = base(src_ref, r, a, n, *coefs, True, True) + FINE * source[r, a : a + n]
+        return carry
+
+    lax.fori_loop(2, ROWS - 2, body, 0)
+
+
+def outer_rows(dst, src_ref, store, face, coefs, source):
+    for r in (1, ROWS - 2, 0, ROWS - 1):
+        below, above = r > 0, r < ROWS - 1
+        for a, n in pieces(NY):
+            new = base(src_ref, r, a, n, *coefs, below, above) + FINE * source[r, a : a + n]
+            here = src_ref[r, PAD + a : PAD + a + n]
+            if not below:
+                new = new + face(0, a, n) * (store[0, a : a + n] - here)
+            if not above:
+                new = new + face(1, a, n) * (store[1, a : a + n] - here)
+            dst[r, PAD + a : PAD + a + n] = new
+
+
+def fix_rows(target, old, halo, face, rows, width):
     for side, r in ((0, 0), (1, rows - 1)):
         for a, n in pieces(width):
             s = slice(PAD + a, PAD + a + n)
-            target[r, s] = swept[r, s] + face(side, a, n) * (halo(side, a, n) - old[r, s])
+            target[r, s] = target[r, s] + face(side, a, n) * (halo(side, a, n) - old[r, s])
 
 
 def halo_after(store, old, halo, later, face, live, rows, width):
@@ -270,7 +293,7 @@
 
 
 def second_kernel(
-    src, sc, so, rc, ro, up, b1, strip, strip_h, cx, cyp, cym, cz, dg, u2, faces, tc, to, kown, own, got, store, edge, u1,
+    src, sc, so, rc, ro, up, b1, b2, strip, strip_h, cx, cyp, cym, cz, dg, u1, u2, faces, tc, to, kown, own, got, store, edge,
 ):
     c = place("c")
     h = place("h")
@@ -285,11 +308,10 @@
         got[side] = got[side] * live[side]
         for a, n in pieces(NY):
             faces[side, a : a + n] = (0.5 * FINE) * (own[side, EK + a : EK + a + n] + got[side, EK + a : EK + a + n])
-    clear_margin(u2, NY)
     halo_after(store, up, reader(got, EU), reader(got, E1), reader(faces), live, ROWS, NY)
-    fix_rows(u1, up, b1, reader(got, EU), reader(faces), ROWS, NY)
+    fix_rows(u1, up, reader(got, EU), reader(faces), ROWS, NY)
     coefs = (cx, cyp, cym, cz, dg)
-    full_sweep(u2, u1, store, reader(faces), ROWS, NY, coefs, src)
+    outer_rows(u2, u1, store, reader(faces), coefs, src)
     for side, r in ((0, 0), (1, ROWS - 1)):
         for a, n in pieces(NY):
             edge[side, a : a + n] = u2[r, PAD + a : PAD + a + n]
@@ -299,7 +321,7 @@
 
 
 def middle_kernel(
-    u2, src, csc, cso, crc, cro, ucp, cb1, cx, cyp, cym, cz, dg, ccx, ccyp, ccym, ccz, cdg, b3, au, own, got, cfaces, cstore, c1,
+    u2, src, csc, cso, crc, cro, ucp, cb1, cx, cyp, cym, cz, dg, ccx, ccyp, ccym, ccz, cdg, b3, b4, au, own, got, cfaces, cstore, c1,
 ):
     c = place("c")
     live = lives()
@@ -312,8 +334,10 @@
         for a, n in pieces(CY):
             cfaces[side, a : a + n] = (0.125 * COARSE) * (own[side, EKC + a : EKC + a + n] + got[side, EKC + a : EKC + a + n])
     halo_after(cstore, ucp, reader(got, EUC), reader(got, E1C), reader(cfaces), live, HALF, CY)
-    fix_rows(c1, ucp, cb1, reader(got, EUC), reader(cfaces), HALF, CY)
+    c1[...] = cb1[...]
+    fix_rows(c1, ucp, reader(got, EUC), reader(cfaces), HALF, CY)
     clear_margin(b3, NY)
+    clear_margin(b4, NY)
     clear_margin(au, CY)
 
     def visit(r, below, above):
@@ -321,15 +345,13 @@
             b3[r, PAD + a : PAD + a + n] = base(u2, r, a, n, cx, cyp, cym, cz, dg, below, above) + FINE * src[r, a : a + n]
 
     each_row(ROWS, visit)
+    inner_rows(b4, b3, (cx, cyp, cym, cz, dg), src)
     full_sweep(au, c1, cstore, reader(cfaces), HALF, CY, (ccx, ccyp, ccym, ccz, cdg), None)
 
 
 def third_kernel(
-    u2, src, faces, rc, ro, b3, au, kown, keven, kodd, cx, cyp, cym, cz, dg, h_out, strips, kall, got, store, u3, f, wp,
+    u2, src, faces, rc, ro, b3, b4, au, cx, cyp, cym, cz, dg, u3, f, h_out, strips, got, store, wp,
 ):
-    kall[0:8] = kown[...]
-    kall[8:16] = keven[...]
-    kall[16:24] = kodd[...]
     c = place("c")
     live = lives()
     got[1 - c] = rc[...]
@@ -337,8 +359,8 @@
     for side in range(2):
         got[side] = got[side] * live[side]
     halo_after(store, u2, reader(got), reader(got, NY), reader(faces), live, ROWS, NY)
-    fix_rows(u3, u2, b3, reader(got), reader(faces), ROWS, NY)
-    full_sweep(f, u3, store, reader(faces), ROWS, NY, (cx, cyp, cym, cz, dg), src)
+    fix_rows(u3, u2, reader(got), reader(faces), ROWS, NY)
+    outer_rows(f, u3, store, reader(faces), (cx, cyp, cym, cz, dg), src)
     keep = jnp.where(place("y") + place("l") > 0, F32(1), F32(0))
     wp[:, 0:WM] = jnp.zeros((HALF, WM, NZ), F32)
     wp[:, WM + CY : WM + CY + WM] = jnp.zeros((HALF, WM, NZ), F32)
@@ -356,7 +378,10 @@
             strips[b, x * YW : (x + 1) * YW] = wp[x, b * YB + WM - YM : b * YB + WM - YM + YW]
 
 
-def pack_kernel(own, even, odd):
+def pack_kernel(own, kown, keven, kodd, even, odd, kall):
+    kall[0:8] = kown[...]
+    kall[8:16] = keven[...]
+    kall[16:24] = kodd[...]
     up = 1 - lax.rem(place("z"), 2)
     for j in range(7):
         n, cut, wide = KEEP[j], YCUT[j], WIDE[j]
@@ -449,15 +474,9 @@
     for r in range(XW):
         ea[r, PAD : PAD + KW] = w[0, first + r]
 
-    def halved(lo, hi, visit):
-        half = (hi - lo) // 2
-
-        def body(g, carry):
-            for t in range(half):
-                visit(lo + g * half + t)
-            return carry
-
-        lax.fori_loop(0, 2, body, 0)
+    def each(lo, hi, visit):
+        for r in range(lo, hi):
+            visit(r)
 
     def sweep(src, dst, number):
         cut = 0 if number <= 5 else 8
@@ -472,7 +491,7 @@
             new = new + (cxp[r - 1, s] * src[r - 1, PAD + cut : PAD + cut + n] + cxp[r, s] * src[r + 1, PAD + cut : PAD + cut + n])
             dst[r, PAD + cut : PAD + cut + n] = new + (zc * up_lane(here) + down_lane(zc * here))
 
-        halved(number, XW - number, visit)
+        each(number, XW - number, visit)
 
     out[2:4] = jnp.zeros((2, HALF, YB, NZ), F32)
     for k in range(1, 8):
@@ -489,7 +508,7 @@
             def add(r):
                 ea[r, s] = ea[r, s] + w[k, first + r, cut : KW - cut]
 
-            halved(2 * k, XW - 2 * k, add)
+            each(2 * k, XW - 2 * k, add)
 
 
 def last_kernel(h_in, y_in, out):
@@ -500,7 +519,7 @@
                 out[0, 2 * x + p, pl.ds(q, CY, 2), :] = h_in[2 * x + p, pl.ds(q, CY, 2), :] + fix
 
 
-def call(kernel, outs, scratch, *operands, limit=6, specs=None):
+def call(kernel, outs, scratch, *operands, limit=6, specs=None, alias=()):
     vmem = pl.BlockSpec(memory_space=pltpu.VMEM)
     return pl.pallas_call(
         kernel,
@@ -508,6 +527,7 @@
         in_specs=specs or [vmem] * len(operands),
         out_specs=[vmem] * len(outs),
         scratch_shapes=[s if callable(getattr(s, "get_ref_aval", None)) else pltpu.VMEM(s, F32) for s in scratch],
+        input_output_aliases=dict(alias),
         compiler_params=pltpu.CompilerParams(vmem_limit_bytes=limit * 1024 * 1024),
     )(*operands)
 
@@ -546,42 +566,42 @@
         *(pltpu.with_memory_space_constraint(x, pltpu.HBM) for x in (starts, material, source)),
         specs=[pl.BlockSpec(memory_space=pltpu.HBM)] * 3,
     )
+    ro = swap_o(so)
     rc = swap_c(sc)
-    ro = swap_o(so)
     edges = (CEDGE, NZ)
-    *coefs, b1, cb1, ucp, csc, cso, strip, strip_h = call(
-        coef_kernel, (fine,) * 5 + (crs,) * 5 + (padded, cpad, cpad, edges, edges, strip_shape, strip_shape),
+    *coefs, b1, b2, cb1, ucp, csc, cso, strip, strip_h = call(
+        coef_kernel, (fine,) * 5 + (crs,) * 5 + (padded, padded, cpad, cpad, edges, edges, strip_shape, strip_shape),
         ((HALF, CY + 2 * WM, NZ), cpad, (2, CEDGE, NZ)),
         kp, up, source,
     )
     strip_h = lax.ppermute(strip_h, "h", pairs(2, 0))
-    strip_h, csc, cso = lax.optimization_barrier((strip_h, csc, cso))
+    crc = swap_c(csc)
+    strip_h, cso = lax.optimization_barrier((strip_h, cso))
     cro = swap_o(cso)
-    crc = swap_c(csc)
-    u2, faces, tc, to, kown = call(
+    _, u2, faces, tc, to, kown = call(
         second_kernel,
-        (padded, (2, NY, NZ), (2 * NY, NZ), (2 * NY, NZ), (8, KW, NZ)),
-        ((2, EDGE, NZ), (2, EDGE, NZ), (2, NY, NZ), (2, 2 * NY, NZ), padded),
-        source, sc, so, rc, ro, up, b1, strip, strip_h, *coefs[:5],
+        (padded, padded, (2, NY, NZ), (2 * NY, NZ), (2 * NY, NZ), (8, KW, NZ)),
+        ((2, EDGE, NZ), (2, EDGE, NZ), (2, NY, NZ), (2, 2 * NY, NZ)),
+        source, sc, so, rc, ro, up, b1, b2, strip, strip_h, *coefs[:5], alias=((6, 0), (7, 1)),
     )
+    ro2 = swap_o(to)
     rc2 = swap_c(tc)
-    ro2 = swap_o(to)
     keven = lax.ppermute(kown, "z", pairs(8, 0))
     kodd = lax.ppermute(kown, "z", pairs(8, 1))
-    b3, au = call(
-        middle_kernel, (padded, cpad), ((2, CEDGE, NZ), (2, CEDGE, NZ), (2, CY, NZ), (2, CY, NZ), cpad),
+    b3, b4, au = call(
+        middle_kernel, (padded, padded, cpad), ((2, CEDGE, NZ), (2, CEDGE, NZ), (2, CY, NZ), (2, CY, NZ), cpad),
         u2, source, csc, cso, crc, cro, ucp, cb1, *coefs,
     )
-    moved, strips, kall = call(
+    _, _, moved, strips = call(
         third_kernel,
-        (fine, (BLOCKS, HALF * YW, NZ), (24, KW, NZ)),
-        ((2, 2 * NY, NZ), (2, NY, NZ), padded, padded, (HALF, CY + 2 * WM, NZ)),
-        u2, source, faces, rc2, ro2, b3, au, kown, keven, kodd, *coefs[:5],
+        (padded, padded, fine, (BLOCKS, HALF * YW, NZ)),
+        ((2, 2 * NY, NZ), (2, NY, NZ), (HALF, CY + 2 * WM, NZ)),
+        u2, source, faces, rc2, ro2, b3, b4, au, *coefs[:5], alias=((5, 0), (6, 1)),
     )
     own = lax.all_to_all(strips, PLANE, 0, 0, tiled=True)
-    own, moved, kall = lax.optimization_barrier((own, moved, kall))
+    own, moved = lax.optimization_barrier((own, moved))
     own = own.reshape(SLABS, 8 * YW, NZ)
-    even, odd = call(pack_kernel, ((NSEND, NZ), (NSEND, NZ)), (), own)
+    even, odd, kall = call(pack_kernel, ((NSEND, NZ), (NSEND, NZ), (24, KW, NZ)), (), own, kown, keven, kodd)
     even = lax.ppermute(even, "z", pairs(8, 0))
     odd = lax.ppermute(odd, "z", pairs(8, 1))
     part = swap_c(own)

time: 106 us -> 109 us (1.028)
  waiting for transfers between devices: 35.2 us -> 42.1 us
  Pallas kernels: 20.4 us -> 17.1 us
    ppermute x7, starting transfers between devices: 9.37 us -> 15.5 us  [swap_c(): return lax.ppermute(x, 'c', pairs(2, 0))]
    ppermute x1, waiting for transfers between devices: 0.01 us -> 4.57 us  [steps(): kodd = lax.ppermute(kown, 'z', pairs(8, 1))]
    pallas_call x9, Pallas kernels: 20.4 us -> 17.1 us  [call(): pl.pallas_call(kernel, out_shape=[jax.ShapeDtypeStruct(s, F32) for s in o...]
    ppermute x3, starting transfers between devices: 4.35 us -> 1.03 us  [swap_o(): return lax.ppermute(x, SPACE, pairs(32, 1))]
    ppermute x1, starting transfers between devices: 4.67 us -> 1.49 us  [steps(): odd = lax.ppermute(odd, 'z', pairs(8, 1))]
    ppermute x1, waiting for transfers between devices: 2.65 us -> 0.01 us  [steps(): odd = lax.ppermute(odd, 'z', pairs(8, 1))]
    ppermute x1, waiting for transfers between devices: 7.69 us -> 9.76 us  [steps(): even = lax.ppermute(even, 'z', pairs(8, 0))]
    ppermute x3, waiting for transfers between devices: 7.63 us -> 9.24 us  [swap_o(): return lax.ppermute(x, SPACE, pairs(32, 1))]
  transfers between devices with their start and end apart: 17 -> 17, of which waited for: 6 -> 10; matrix products, arithmetic and copies ran while one was open for 0% -> 0% of each run, Pallas kernels for 14% -> 11%
where the time goes in v4:
time: 109 us
  waiting for transfers between devices  42.1 us (39%)
  starting transfers between devices  27.5 us (25%)
  blocking collectives  22.2 us (20%)
  Pallas kernels  17.1 us (16%)
    all_to_all x1, blocking collectives, steps(): own = lax.all_to_all(strips, PLANE, 0, 0, tiled=True)  22.2 us
    pallas_call x9, Pallas kernels, call(): pl.pallas_call(kernel, out_shape=[jax.ShapeDtypeStruct(s, F32) for s in o...  17.1 us
    ppermute x7, starting transfers between devices, swap_c(): return lax.ppermute(x, 'c', pairs(2, 0))  15.5 us
    ppermute x1, waiting for transfers between devices, steps(): even = lax.ppermute(even, 'z', pairs(8, 0))  9.76 us
    ppermute x3, waiting for transfers between devices, swap_o(): return lax.ppermute(x, SPACE, pairs(32, 1))  9.24 us
    ppermute x1, waiting for transfers between devices, steps(): strip_h = lax.ppermute(strip_h, 'h', pairs(2, 0))  6.98 us
    all_to_all x1, waiting for transfers between devices, steps(): fixes = lax.all_to_all(fixes, PLANE, 0, 0, tiled=True)  6.7 us
    ppermute x1, waiting for transfers between devices, steps(): kodd = lax.ppermute(kown, 'z', pairs(8, 1))  4.57 us
  transfers between devices with their start and end apart: 17, of which 10 were waited for; matrix products, arithmetic and copies ran while one was open for 0% of the time, Pallas kernels for 11%

profile of v4, /device:TPU:1, one launch (start us, length us, event | category | flops | bytes accessed | tf_op | source)
XLA Modules:
  0.0 109.0 jit_solution(703952035321499898)
XLA Ops:
  0.0 2.6 %shard_map.37 = (f32[768,128]{1,0:T(8,128)S(1)}, f32[768,128]{1,0:T(8,128)S(1)}, f32[8,272,128]{2,1,0:T(8,128)S(1)}, f32[8,272,128]{2,1,0:T(8,128)S(1)}) custom-call(f32[1,8,256,128]{3,2,1,0:T(8,128)} %u_in.1, s32[8,256,128]{2,1,0:T(8,128)} %mat.1, f32[8,256,128]{2,1,0:T(8,128)} %src.9), custom_call_target="tpu_custom_call" | custom-call | tf_op jit(solution)/shard_map/pallas_call | solution.py:524
  2.6 3.3 %collective-permute-start = (f32[768,128]{1,0:T(8,128)S(1)}, f32[768,128]{1,0:T(8,128)S(1)}, u32[]{:S(2)}, u32[]{:S(2)}) collective-permute-start(f32[768,128]{1,0:T(8,128)S(1)} %get-tuple-element.49.sc), channel_id=1, source_target_pairs={{0,1},{1,0},{2,3},{3,2},{4,5},{5,4},{6,7},{7,6},{8,9},{9,8},{10,11... | collective-permute-start | bytes 1179656 | tf_op jit(solution)/shard_map/ppermute | solution.py:556
  5.9 1.0 collective-permute-start.1
  6.9 3.7 %shard_map.38 = (f32[8,256,128]{2,1,0:T(8,128)S(1)}, f32[8,256,128]{2,1,0:T(8,128)S(1)}, f32[8,256,128]{2,1,0:T(8,128)S(1)}, f32[8,256,128]{2,1,0:T(8,128)S(1)},...) custom-call(f32[8,272,128]{2,1,0:T(8,128)S(1)} %get-tuple-element.52, ...), custom_call_target="tpu_custom_call" | custom-call | tf_op jit(solution)/shard_map/pallas_call | solution.py:524
  10.6 1.7 %collective-permute-start.2 = (f32[4,40,128]{2,1,0:T(8,128)S(1)}, f32[4,40,128]{2,1,0:T(8,128)S(1)}, u32[]{:S(2)}, u32[]{:S(2)}) collective-permute-start(f32[4,40,128]{2,1,0:T(8,128)S(1)} %get-tuple-element.56), channel_id=1, source_target_pairs={{0,2},{2,0},{1,3},{3,1},{4,6},{6,4},{5,7},{7,5},{8,10},{10,8},{9,1... | collective-permute-start | bytes 245768 | tf_op jit(solution)/shard_map/ppermute | solution.py:577
  12.3 7.0 %collective-permute-done.2.strip_h = f32[4,40,128]{2,1,0:T(8,128)S(1)} collective-permute-done((f32[4,40,128]{2,1,0:T(8,128)S(1)}, f32[4,40,128]{2,1,0:T(8,128)S(1)}, u32[]{:S(2)}, u32[]{:S(2)}) %collective-permute-start.2) | collective-permute-done | bytes 81952 | tf_op jit(solution)/shard_map/ppermute | solution.py:577
  19.3 0.5 collective-permute-done.1.ro
  19.7 0.9 shard_map.39
  20.7 2.7 %collective-permute-start.3 = (f32[512,128]{1,0:T(8,128)S(1)}, f32[512,128]{1,0:T(8,128)S(1)}, u32[]{:S(2)}, u32[]{:S(2)}) collective-permute-start(f32[512,128]{1,0:T(8,128)S(1)} %get-tuple-element.66), channel_id=1, source_target_pairs={{0,1},{1,0},{2,3},{3,2},{4,5},{5,4},{6,7},{7,6},{8,9},{9,8},{10,11... | collective-permute-start | bytes 786440 | tf_op jit(solution)/shard_map/ppermute | solution.py:556
  23.4 4.5 %collective-permute-start.5 = (f32[384,128]{1,0:T(8,128)S(1)}, f32[384,128]{1,0:T(8,128)S(1)}, u32[]{:S(2)}, u32[]{:S(2)}) collective-permute-start(f32[384,128]{1,0:T(8,128)S(1)} %get-tuple-element.68.csc), channel_id=1, source_target_pairs={{0,1},{1,0},{2,3},{3,2},{4,5},{5,4},{6,7},{7,6},{8,9},{9,8},{10,11... | collective-permute-start | bytes 589832 | tf_op jit(solution)/shard_map/ppermute | solution.py:556
  27.9 1.1 collective-permute-done.5.crc
  28.9 8.8 %collective-permute-done.6.cro = f32[384,128]{1,0:T(8,128)S(1)} collective-permute-done((f32[384,128]{1,0:T(8,128)S(1)}, f32[384,128]{1,0:T(8,128)S(1)}, u32[]{:S(2)}, u32[]{:S(2)}) %collective-permute-start.6) | collective-permute-done | bytes 196640 | tf_op jit(solution)/shard_map/ppermute | solution.py:559
  37.7 2.4 %shard_map.40 = (f32[8,272,128]{2,1,0:T(8,128)S(1)}, f32[8,272,128]{2,1,0:T(8,128)S(1)}, f32[4,144,128]{2,1,0:T(8,128)S(1)}) custom-call(f32[8,272,128]{2,1,0:T(8,128)S(1)} %get-tuple-element.64.u2, f32[8,256,128]{2,1,0:T(8,128)S(1)} %copy-done, f32[384,128]{1,0:T(8,128)S(1)} %get-tuple-element.68.csc, f32[384,128]{1,0:T(8,128)S(1)} %get-tuple-element.69.cso, ...), custom_call_target="tpu_custom_call" | custom-call | tf_op jit(solution)/shard_map/pallas_call | solution.py:524
  40.2 0.9 shard_map.41
  41.0 22.2 %all_to_all.10 = f32[16,144,128]{2,1,0:T(8,128)S(1)} all-to-all(f32[16,144,128]{2,1,0:T(8,128)S(1)} %get-tuple-element.80), channel_id=1, replica_groups=mesh['y'=4,'l'=2,'z'=8,'h'=2,'c'=2] {'y','l','h'}, dimensions={0} | all-to-all | bytes 2359296 | tf_op jit(solution)/shard_map/all_to_all | solution.py:601
  63.2 1.5 %collective-permute-start.8 = (f32[8,288,128]{2,1,0:T(8,128)S(1)}, f32[8,288,128]{2,1,0:T(8,128)S(1)}, u32[]{:S(2)}, u32[]{:S(2)}) collective-permute-start(f32[8,288,128]{2,1,0:T(8,128)S(1)} %bitcast.1), channel_id=1, source_target_pairs={{0,1},{1,0},{2,3},{3,2},{4,5},{5,4},{6,7},{7,6},{8,9},{9,8},{10,11... | collective-permute-start | bytes 3538952 | tf_op jit(solution)/shard_map/ppermute | solution.py:556
  64.7 3.6 %collective-permute-start.10 = (f32[8,40,128]{2,1,0:T(8,128)S(1)}, f32[8,40,128]{2,1,0:T(8,128)S(1)}, u32[]{:S(2)}, u32[]{:S(2)}) collective-permute-start(f32[8,40,128]{2,1,0:T(8,128)S(1)} %get-tuple-element.84.kown), channel_id=1, source_target_pairs={{4,8},{8,4},{12,16},{16,12},{20,24},{24,20},{0,28},{28,0},{5,9},{9... | collective-permute-start | bytes 491528 | tf_op jit(solution)/shard_map/ppermute | solution.py:590
  68.4 4.6 %collective-permute-done.10.kodd = f32[8,40,128]{2,1,0:T(8,128)S(1)} collective-permute-done((f32[8,40,128]{2,1,0:T(8,128)S(1)}, f32[8,40,128]{2,1,0:T(8,128)S(1)}, u32[]{:S(2)}, u32[]{:S(2)}) %collective-permute-start.10) | collective-permute-done | bytes 163872 | tf_op jit(solution)/shard_map/ppermute | solution.py:590
  72.9 0.9 collective-permute-done.9.keven
  73.9 0.4 collective-permute-start.11
  74.3 1.5 %collective-permute-start.12 = (f32[976,128]{1,0:T(8,128)S(1)}, f32[976,128]{1,0:T(8,128)S(1)}, u32[]{:S(2)}, u32[]{:S(2)}) collective-permute-start(f32[976,128]{1,0:T(8,128)S(1)} %get-tuple-element.86), channel_id=1, source_target_pairs={{4,8},{8,4},{12,16},{16,12},{20,24},{24,20},{0,28},{28,0},{5,9},{9... | collective-permute-start | bytes 1499144 | tf_op jit(solution)/shard_map/ppermute | solution.py:606
  75.8 0.3 collective-permute-start.7
  76.1 9.8 %collective-permute-done.11.even = f32[976,128]{1,0:T(8,128)S(1)} collective-permute-done((f32[976,128]{1,0:T(8,128)S(1)}, f32[976,128]{1,0:T(8,128)S(1)}, u32[]{:S(2)}, u32[]{:S(2)}) %collective-permute-start.11) | collective-permute-done | bytes 499744 | tf_op jit(solution)/shard_map/ppermute | solution.py:605
  85.8 2.0 %collective-permute-start.13 = (f32[976,128]{1,0:T(8,128)S(1)}, f32[976,128]{1,0:T(8,128)S(1)}, u32[]{:S(2)}, u32[]{:S(2)}) collective-permute-start(f32[976,128]{1,0:T(8,128)S(1)} %collective-permute-done.11.even), channel_id=1, source_target_pairs={{0,1},{1,0},{2,3},{3,2},{4,5},{5,4},{6,7},{7,6},{8,9},{9,8},{10,11... | collective-permute-start | bytes 1499144 | tf_op jit(solution)/shard_map/ppermute | solution.py:556
  87.8 1.5 %collective-permute-start.14 = (f32[976,128]{1,0:T(8,128)S(1)}, f32[976,128]{1,0:T(8,128)S(1)}, u32[]{:S(2)}, u32[]{:S(2)}) collective-permute-start(f32[976,128]{1,0:T(8,128)S(1)} %collective-permute-done.12.odd), channel_id=1, source_target_pairs={{0,1},{1,0},{2,3},{3,2},{4,5},{5,4},{6,7},{7,6},{8,9},{9,8},{10,11... | collective-permute-start | bytes 1499144 | tf_op jit(solution)/shard_map/ppermute | solution.py:556
  89.3 2.2 %collective-permute-done.15.pkall = f32[24,40,128]{2,1,0:T(8,128)S(1)} collective-permute-done((f32[24,40,128]{2,1,0:T(8,128)S(1)}, f32[24,40,128]{2,1,0:T(8,128)S(1)}, u32[]{:S(2)}, u32[]{:S(2)}) %collective-permute-start.15) | collective-permute-done | bytes 491552 | tf_op jit(solution)/shard_map/ppermute | solution.py:556
  91.5 1.3 %shard_map.43 = (f32[40,40,128]{2,1,0:T(8,128)S(1)}, f32[40,40,128]{2,1,0:T(8,128)S(1)}, f32[40,40,128]{2,1,0:T(8,128)S(1)}, f32[40,40,128]{2,1,0:T(8,128)S(1)}, f32[40,40,128]{2,1,0:T(8,128)S(1)}) custom-call(f32[24,40,128]{2,1,0:T(8,128)S(1)} %get-tuple-element.87.kall, f32[24,40,128]{2,1,0:T(8,128)S(1)} %collective-permute-done.15.pkall), custom_call_target="tpu_custom_call" | custom-call | tf_op jit(solution)/shard_map/pallas_call | solution.py:524
  92.9 4.1 %shard_map.44 = f32[16,4,8,128]{3,2,1,0:T(8,128)} custom-call(f32[8,288,128]{2,1,0:T(8,128)S(1)} %bitcast.3, f32[8,288,128]{2,1,0:T(8,128)S(1)} %collective-permute-done.8.part, f32[976,128]{1,0:T(8,128)S(1)} %collective-permute-done.11.even, f32[976,128]{1,0:T(8,128)S(1)} %collective-permute-done.12.odd, f32[976,128]{1,0:T(8,128)S(1)} %collective-permute-done.13.peven, ...), custom_call_target="tpu_custom_call" | custom-call | tf_op jit(solution)/shard_map/pallas_call | solution.py:524
  97.0 3.5 %all-to-all-start.1 = ((f32[16,4,8,128]{3,2,1,0:T(8,128)}), f32[16,4,8,128]{3,2,1,0:T(8,128)S(1)}, u32[]{:S(2)}, u32[]{:S(2)}) async-start(f32[16,4,8,128]{3,2,1,0:T(8,128)} %shard_map.44), calls=%async_computation.1 | async-start | bytes 524288 | tf_op jit(solution)/shard_map/all_to_all | solution.py:619
  100.5 0.7 collective-permute-done.7.h_in
  101.2 6.7 %all-to-all-done.1.y_in = f32[16,4,8,128]{3,2,1,0:T(8,128)S(1)} async-done(((f32[16,4,8,128]{3,2,1,0:T(8,128)}), f32[16,4,8,128]{3,2,1,0:T(8,128)S(1)}, u32[]{:S(2)}, u32[]{:S(2)}) %all-to-all-start.1) | async-done | bytes 262176 | tf_op jit(solution)/shard_map/all_to_all | solution.py:619
  107.9 1.1 shard_map.45
  (14 shorter events, 0.1 us)
Async XLA Ops:
  0.0 6.9 %copy-start = (f32[8,256,128]{2,1,0:T(8,128)S(1)}, f32[8,256,128]{2,1,0:T(8,128)}, u32[]{:S(2)}) copy-start(f32[8,256,128]{2,1,0:T(8,128)} %src.9) | copy-start | bytes 3145732
  2.6 16.6 %collective-permute-start = (f32[768,128]{1,0:T(8,128)S(1)}, f32[768,128]{1,0:T(8,128)S(1)}, u32[]{:S(2)}, u32[]{:S(2)}) collective-permute-start(f32[768,128]{1,0:T(8,128)S(1)} %get-tuple-element.49.sc), channel_id=1, source_target_pairs={{0,1},{1,0},{2,3},{3,2},{4,5},{5,4},{6,7},{7,6},{8,9},{9,8},{10,11... | collective-permute-start | bytes 1179656 | tf_op jit(solution)/shard_map/ppermute | solution.py:556
  5.9 13.8 %collective-permute-start.1 = (f32[768,128]{1,0:T(8,128)S(1)}, f32[768,128]{1,0:T(8,128)S(1)}, u32[]{:S(2)}, u32[]{:S(2)}) collective-permute-start(f32[768,128]{1,0:T(8,128)S(1)} %get-tuple-element.50.so), channel_id=1, source_target_pairs={{1,2},{2,1},{3,4},{4,3},{5,6},{6,5},{7,8},{8,7},{9,10},{10,9},{11,... | collective-permute-start | bytes 1179656 | tf_op jit(solution)/shard_map/ppermute | solution.py:559
  10.6 8.6 %collective-permute-start.2 = (f32[4,40,128]{2,1,0:T(8,128)S(1)}, f32[4,40,128]{2,1,0:T(8,128)S(1)}, u32[]{:S(2)}, u32[]{:S(2)}) collective-permute-start(f32[4,40,128]{2,1,0:T(8,128)S(1)} %get-tuple-element.56), channel_id=1, source_target_pairs={{0,2},{2,0},{1,3},{3,1},{4,6},{6,4},{5,7},{7,5},{8,10},{10,8},{9,1... | collective-permute-start | bytes 245768 | tf_op jit(solution)/shard_map/ppermute | solution.py:577
  20.7 19.5 %collective-permute-start.3 = (f32[512,128]{1,0:T(8,128)S(1)}, f32[512,128]{1,0:T(8,128)S(1)}, u32[]{:S(2)}, u32[]{:S(2)}) collective-permute-start(f32[512,128]{1,0:T(8,128)S(1)} %get-tuple-element.66), channel_id=1, source_target_pairs={{0,1},{1,0},{2,3},{3,2},{4,5},{5,4},{6,7},{7,6},{8,9},{9,8},{10,11... | collective-permute-start | bytes 786440 | tf_op jit(solution)/shard_map/ppermute | solution.py:556
  23.4 16.7 %collective-permute-start.4 = (f32[512,128]{1,0:T(8,128)S(1)}, f32[512,128]{1,0:T(8,128)S(1)}, u32[]{:S(2)}, u32[]{:S(2)}) collective-permute-start(f32[512,128]{1,0:T(8,128)S(1)} %get-tuple-element.67), channel_id=1, source_target_pairs={{1,2},{2,1},{3,4},{4,3},{5,6},{6,5},{7,8},{8,7},{9,10},{10,9},{11,... | collective-permute-start | bytes 786440 | tf_op jit(solution)/shard_map/ppermute | solution.py:559
  23.4 5.5 %collective-permute-start.5 = (f32[384,128]{1,0:T(8,128)S(1)}, f32[384,128]{1,0:T(8,128)S(1)}, u32[]{:S(2)}, u32[]{:S(2)}) collective-permute-start(f32[384,128]{1,0:T(8,128)S(1)} %get-tuple-element.68.csc), channel_id=1, source_target_pairs={{0,1},{1,0},{2,3},{3,2},{4,5},{5,4},{6,7},{7,6},{8,9},{9,8},{10,11... | collective-permute-start | bytes 589832 | tf_op jit(solution)/shard_map/ppermute | solution.py:556
  27.9 9.9 %collective-permute-start.6 = (f32[384,128]{1,0:T(8,128)S(1)}, f32[384,128]{1,0:T(8,128)S(1)}, u32[]{:S(2)}, u32[]{:S(2)}) collective-permute-start(f32[384,128]{1,0:T(8,128)S(1)} %get-tuple-element.69.cso), channel_id=1, source_target_pairs={{1,2},{2,1},{3,4},{4,3},{5,6},{6,5},{7,8},{8,7},{9,10},{10,9},{11,... | collective-permute-start | bytes 589832 | tf_op jit(solution)/shard_map/ppermute | solution.py:559
  63.2 29.6 %collective-permute-start.8 = (f32[8,288,128]{2,1,0:T(8,128)S(1)}, f32[8,288,128]{2,1,0:T(8,128)S(1)}, u32[]{:S(2)}, u32[]{:S(2)}) collective-permute-start(f32[8,288,128]{2,1,0:T(8,128)S(1)} %bitcast.1), channel_id=1, source_target_pairs={{0,1},{1,0},{2,3},{3,2},{4,5},{5,4},{6,7},{7,6},{8,9},{9,8},{10,11... | collective-permute-start | bytes 3538952 | tf_op jit(solution)/shard_map/ppermute | solution.py:556
  64.7 8.2 %collective-permute-start.10 = (f32[8,40,128]{2,1,0:T(8,128)S(1)}, f32[8,40,128]{2,1,0:T(8,128)S(1)}, u32[]{:S(2)}, u32[]{:S(2)}) collective-permute-start(f32[8,40,128]{2,1,0:T(8,128)S(1)} %get-tuple-element.84.kown), channel_id=1, source_target_pairs={{4,8},{8,4},{12,16},{16,12},{20,24},{24,20},{0,28},{28,0},{5,9},{9... | collective-permute-start | bytes 491528 | tf_op jit(solution)/shard_map/ppermute | solution.py:590
  68.4 5.5 %collective-permute-start.9 = (f32[8,40,128]{2,1,0:T(8,128)S(1)}, f32[8,40,128]{2,1,0:T(8,128)S(1)}, u32[]{:S(2)}, u32[]{:S(2)}) collective-permute-start(f32[8,40,128]{2,1,0:T(8,128)S(1)} %get-tuple-element.84.kown), channel_id=1, source_target_pairs={{0,4},{4,0},{8,12},{12,8},{16,20},{20,16},{24,28},{28,24},{1,5},{5... | collective-permute-start | bytes 491528 | tf_op jit(solution)/shard_map/ppermute | solution.py:589
  73.9 11.9 %collective-permute-start.11 = (f32[976,128]{1,0:T(8,128)S(1)}, f32[976,128]{1,0:T(8,128)S(1)}, u32[]{:S(2)}, u32[]{:S(2)}) collective-permute-start(f32[976,128]{1,0:T(8,128)S(1)} %get-tuple-element.85), channel_id=1, source_target_pairs={{0,4},{4,0},{8,12},{12,8},{16,20},{20,16},{24,28},{28,24},{1,5},{5... | collective-permute-start | bytes 1499144 | tf_op jit(solution)/shard_map/ppermute | solution.py:605
  74.3 13.5 %collective-permute-start.12 = (f32[976,128]{1,0:T(8,128)S(1)}, f32[976,128]{1,0:T(8,128)S(1)}, u32[]{:S(2)}, u32[]{:S(2)}) collective-permute-start(f32[976,128]{1,0:T(8,128)S(1)} %get-tuple-element.86), channel_id=1, source_target_pairs={{4,8},{8,4},{12,16},{16,12},{20,24},{24,20},{0,28},{28,0},{5,9},{9... | collective-permute-start | bytes 1499144 | tf_op jit(solution)/shard_map/ppermute | solution.py:606
  75.8 25.4 %collective-permute-start.7 = (f32[8,256,128]{2,1,0:T(8,128)S(1)}, f32[8,256,128]{2,1,0:T(8,128)S(1)}, u32[]{:S(2)}, u32[]{:S(2)}) collective-permute-start(f32[8,256,128]{2,1,0:T(8,128)S(1)} %get-tuple-element.82), channel_id=1, source_target_pairs={{0,32},{32,64},{64,96},{96,128},{128,160},{160,192},{192,224},{224... | collective-permute-start | bytes 3145736 | tf_op jit(solution)/shard_map/ppermute | solution.py:609
  85.8 7.0 %collective-permute-start.13 = (f32[976,128]{1,0:T(8,128)S(1)}, f32[976,128]{1,0:T(8,128)S(1)}, u32[]{:S(2)}, u32[]{:S(2)}) collective-permute-start(f32[976,128]{1,0:T(8,128)S(1)} %collective-permute-done.11.even), channel_id=1, source_target_pairs={{0,1},{1,0},{2,3},{3,2},{4,5},{5,4},{6,7},{7,6},{8,9},{9,8},{10,11... | collective-permute-start | bytes 1499144 | tf_op jit(solution)/shard_map/ppermute | solution.py:556
  87.8 5.0 %collective-permute-start.14 = (f32[976,128]{1,0:T(8,128)S(1)}, f32[976,128]{1,0:T(8,128)S(1)}, u32[]{:S(2)}, u32[]{:S(2)}) collective-permute-start(f32[976,128]{1,0:T(8,128)S(1)} %collective-permute-done.12.odd), channel_id=1, source_target_pairs={{0,1},{1,0},{2,3},{3,2},{4,5},{5,4},{6,7},{7,6},{8,9},{9,8},{10,11... | collective-permute-start | bytes 1499144 | tf_op jit(solution)/shard_map/ppermute | solution.py:556
  89.3 2.2 %collective-permute-start.15 = (f32[24,40,128]{2,1,0:T(8,128)S(1)}, f32[24,40,128]{2,1,0:T(8,128)S(1)}, u32[]{:S(2)}, u32[]{:S(2)}) collective-permute-start(f32[24,40,128]{2,1,0:T(8,128)S(1)} %get-tuple-element.87.kall), channel_id=1, source_target_pairs={{0,1},{1,0},{2,3},{3,2},{4,5},{5,4},{6,7},{7,6},{8,9},{9,8},{10,11... | collective-permute-start | bytes 1474568 | tf_op jit(solution)/shard_map/ppermute | solution.py:556
  97.0 10.9 %all-to-all-start.1 = ((f32[16,4,8,128]{3,2,1,0:T(8,128)}), f32[16,4,8,128]{3,2,1,0:T(8,128)S(1)}, u32[]{:S(2)}, u32[]{:S(2)}) async-start(f32[16,4,8,128]{3,2,1,0:T(8,128)} %shard_map.44), calls=%async_computation.1 | async-start | bytes 524288 | tf_op jit(solution)/shard_map/all_to_all | solution.py:619

commit v5 on v4

--- a/solution.py
+++ b/solution.py
@@ -159,25 +159,34 @@
     return jnp.where(index > 0, F32(1), F32(0)), jnp.where(index < 31, F32(1), F32(0))
 
 
-def first_kernel(u_in, mat, src, sc, so, kp, up, edge, numbers, ends, u_sem, m_sem, s_sem):
-    inside = pl.ds(PAD, NY)
-    order = (0, 7, 1, 6, 2, 5, 3, 4)
-    for side, r in ((0, 0), (1, ROWS - 1)):
-        pltpu.make_async_copy(src.at[r], ends.at[side], s_sem.at[side]).start()
-    for r in order:
+EDGES = (0, 7, 1, 6)
+ALL_ROWS = tuple(range(ROWS))
+
+
+def start_rows(rows, u_in, mat, up, numbers, u_sem, m_sem):
+    for r in rows:
         pltpu.make_async_copy(mat.at[r], numbers.at[r], m_sem.at[r]).start()
-        pltpu.make_async_copy(u_in.at[0, r], up.at[r, inside], u_sem.at[r]).start()
+        pltpu.make_async_copy(u_in.at[0, r], up.at[r, pl.ds(PAD, NY)], u_sem.at[r]).start()
+
+
+def take_rows(rows, u_in, mat, kp, up, numbers, u_sem, m_sem):
     clear_margin(kp, NY)
     clear_margin(up, NY)
-    for r in order:
+    for r in rows:
         pltpu.make_async_copy(mat.at[r], numbers.at[r], m_sem.at[r]).wait()
         for a, n in pieces(NY):
             kp[r, PAD + a : PAD + a + n] = lookup(numbers[r, a : a + n])
-    for r in range(ROWS):
-        pltpu.make_async_copy(u_in.at[0, r], up.at[r, inside], u_sem.at[r]).wait()
+    for r in rows:
+        pltpu.make_async_copy(u_in.at[0, r], up.at[r, pl.ds(PAD, NY)], u_sem.at[r]).wait()
+
+
+def first_kernel(u_in, mat, src, sc, so, kp, up, edge, numbers, ends, u_sem, m_sem, s_sem):
+    start_rows(EDGES, u_in, mat, up, numbers, u_sem, m_sem)
+    for side, r in ((0, 0), (1, ROWS - 1)):
+        pltpu.make_async_copy(src.at[r], ends.at[side], s_sem.at[side]).start()
+    take_rows(EDGES, u_in, mat, kp, up, numbers, u_sem, m_sem)
     for side, r in ((0, 0), (1, ROWS - 1)):
         pltpu.make_async_copy(src.at[r], ends.at[side], s_sem.at[side]).wait()
-    for side, r in ((0, 0), (1, ROWS - 1)):
         for a, n in pieces(NY):
             edge[side, EK + a : EK + a + n] = kp[r, PAD + a : PAD + a + n]
             edge[side, EU + a : EU + a + n] = up[r, PAD + a : PAD + a + n]
@@ -188,8 +197,15 @@
 
 
 def coef_kernel(
-    kp, up, src, cx, cyp, cym, cz, dg, ccx, ccyp, ccym, ccz, cdg, b1, b2, cb1, ucp, csc, cso, strip, strip_h, kw, kcp, edge,
+    u_in, mat, src_in, _, cx, cyp, cym, cz, dg, ccx, ccyp, ccym, ccz, cdg, b1, b2, cb1, ucp, csc, cso, strip, strip_h, up, src,
+    kw, kcp, edge, kp, numbers, u_sem, m_sem, s_sem,
 ):
+    start_rows(ALL_ROWS, u_in, mat, up, numbers, u_sem, m_sem)
+    for r in range(ROWS):
+        pltpu.make_async_copy(src_in.at[r], src.at[r], s_sem.at[r]).start()
+    take_rows(ALL_ROWS, u_in, mat, kp, up, numbers, u_sem, m_sem)
+    for r in range(ROWS):
+        pltpu.make_async_copy(src_in.at[r], src.at[r], s_sem.at[r]).wait()
     clear_margin(kcp, CY)
     clear_margin(ucp, CY)
     for x in range(HALF):
@@ -293,12 +309,9 @@
 
 
 def second_kernel(
-    src, sc, so, rc, ro, up, b1, b2, strip, strip_h, cx, cyp, cym, cz, dg, u1, u2, faces, tc, to, kown, own, got, store, edge,
+    src, sc, so, rc, ro, up, b1, b2, cx, cyp, cym, cz, dg, u1, u2, faces, tc, to, own, got, store, edge,
 ):
     c = place("c")
-    h = place("h")
-    kown[pl.ds(4 * h, HALF)] = strip[...]
-    kown[pl.ds(4 * (1 - h), HALF)] = strip_h[...]
     live = lives()
     own[1 - c] = sc[...]
     own[c] = so[...]
@@ -378,6 +391,12 @@
             strips[b, x * YW : (x + 1) * YW] = wp[x, b * YB + WM - YM : b * YB + WM - YM + YW]
 
 
+def merge_kernel(strip, strip_h, kown):
+    h = place("h")
+    kown[pl.ds(4 * h, HALF)] = strip[...]
+    kown[pl.ds(4 * (1 - h), HALF)] = strip_h[...]
+
+
 def pack_kernel(own, kown, keven, kodd, even, odd, kall):
     kall[0:8] = kown[...]
     kall[8:16] = keven[...]
@@ -559,35 +578,34 @@
         return lax.ppermute(x, SPACE, pairs(32, 1))
 
     dma = pltpu.SemaphoreType.DMA
-    sc, so, kp, up = call(
-        first_kernel,
-        ((EDGE, NZ), (EDGE, NZ), padded, padded),
-        ((2, EDGE, NZ), pltpu.VMEM(fine, jnp.int32), (2, NY, NZ), dma((ROWS,)), dma((ROWS,)), dma((2,))),
-        *(pltpu.with_memory_space_constraint(x, pltpu.HBM) for x in (starts, material, source)),
-        specs=[pl.BlockSpec(memory_space=pltpu.HBM)] * 3,
+    in_hbm = [pl.BlockSpec(memory_space=pltpu.HBM)] * 3
+    inputs = [pltpu.with_memory_space_constraint(x, pltpu.HBM) for x in (starts, material, source)]
+    numbers = pltpu.VMEM(fine, jnp.int32)
+    sc, so = call(
+        first_kernel, ((EDGE, NZ), (EDGE, NZ)),
+        (padded, padded, (2, EDGE, NZ), numbers, (2, NY, NZ), dma((ROWS,)), dma((ROWS,)), dma((2,))),
+        *inputs, specs=in_hbm,
     )
     ro = swap_o(so)
     rc = swap_c(sc)
     edges = (CEDGE, NZ)
-    *coefs, b1, b2, cb1, ucp, csc, cso, strip, strip_h = call(
-        coef_kernel, (fine,) * 5 + (crs,) * 5 + (padded, padded, cpad, cpad, edges, edges, strip_shape, strip_shape),
-        ((HALF, CY + 2 * WM, NZ), cpad, (2, CEDGE, NZ)),
-        kp, up, source,
+    *coefs, b1, b2, cb1, ucp, csc, cso, strip, strip_h, up, source = call(
+        coef_kernel,
+        (fine,) * 5 + (crs,) * 5 + (padded, padded, cpad, cpad, edges, edges, strip_shape, strip_shape, padded, fine),
+        ((HALF, CY + 2 * WM, NZ), cpad, (2, CEDGE, NZ), padded, numbers, dma((ROWS,)), dma((ROWS,)), dma((ROWS,))),
+        *inputs, sc, specs=in_hbm + [pl.BlockSpec(memory_space=pl.ANY)], limit=8,
     )
-    strip_h = lax.ppermute(strip_h, "h", pairs(2, 0))
     crc = swap_c(csc)
-    strip_h, cso = lax.optimization_barrier((strip_h, cso))
     cro = swap_o(cso)
-    _, u2, faces, tc, to, kown = call(
+    _, u2, faces, tc, to = call(
         second_kernel,
-        (padded, padded, (2, NY, NZ), (2 * NY, NZ), (2 * NY, NZ), (8, KW, NZ)),
+        (padded, padded, (2, NY, NZ), (2 * NY, NZ), (2 * NY, NZ)),
         ((2, EDGE, NZ), (2, EDGE, NZ), (2, NY, NZ), (2, 2 * NY, NZ)),
-        source, sc, so, rc, ro, up, b1, b2, strip, strip_h, *coefs[:5], alias=((6, 0), (7, 1)),
+        source, sc, so, rc, ro, up, b1, b2, *coefs[:5], alias=((6, 0), (7, 1)),
     )
     ro2 = swap_o(to)
     rc2 = swap_c(tc)
-    keven = lax.ppermute(kown, "z", pairs(8, 0))
-    kodd = lax.ppermute(kown, "z", pairs(8, 1))
+    strip_h = lax.ppermute(strip_h, "h", pairs(2, 0))
     b3, b4, au = call(
         middle_kernel, (padded, padded, cpad), ((2, CEDGE, NZ), (2, CEDGE, NZ), (2, CY, NZ), (2, CY, NZ), cpad),
         u2, source, csc, cso, crc, cro, ucp, cb1, *coefs,
@@ -599,6 +617,10 @@
         u2, source, faces, rc2, ro2, b3, b4, au, *coefs[:5], alias=((5, 0), (6, 1)),
     )
     own = lax.all_to_all(strips, PLANE, 0, 0, tiled=True)
+    strip, _ = lax.optimization_barrier((strip, strips))
+    (kown,) = call(merge_kernel, ((8, KW, NZ),), (), strip, strip_h)
+    keven = lax.ppermute(kown, "z", pairs(8, 0))
+    kodd = lax.ppermute(kown, "z", pairs(8, 1))
     own, moved = lax.optimization_barrier((own, moved))
     own = own.reshape(SLABS, 8 * YW, NZ)
     even, odd, kall = call(pack_kernel, ((NSEND, NZ), (NSEND, NZ), (24, KW, NZ)), (), own, kown, keven, kodd)

time: 109 us -> 108 us (level)
  blocking collectives: 22.2 us -> 0 us
  starting transfers between devices: 27.5 us -> 41 us
  waiting for transfers between devices: 42.1 us -> 46.6 us
  Pallas kernels: 17.1 us -> 19.8 us
    all_to_all x1 -> x0, blocking collectives: 22.2 us -> none  [steps(): own = lax.all_to_all(strips, PLANE, 0, 0, tiled=True)]
    all_to_all x0 -> x1, waiting for transfers between devices: none -> 13.9 us  [steps(): own = lax.all_to_all(strips, PLANE, 0, 0, tiled=True)]
    ppermute x1, waiting for transfers between devices: 6.98 us -> 0.01 us  [steps(): strip_h = lax.ppermute(strip_h, 'h', pairs(2, 0))]
    ppermute x3, starting transfers between devices: 1.03 us -> 6.24 us  [swap_o(): return lax.ppermute(x, SPACE, pairs(32, 1))]
    all_to_all x0 -> x1, starting transfers between devices: none -> 4.32 us  [steps(): own = lax.all_to_all(strips, PLANE, 0, 0, tiled=True)]
    pallas_call x9 -> x10, Pallas kernels: 17.1 us -> 19.8 us  [call(): pl.pallas_call(kernel, out_shape=[jax.ShapeDtypeStruct(s, F32) for s in o...]
    all_to_all x1, starting transfers between devices: 3.53 us -> 5.4 us  [steps(): fixes = lax.all_to_all(fixes, PLANE, 0, 0, tiled=True)]
    ppermute x7, starting transfers between devices: 15.5 us -> 17.1 us  [swap_c(): return lax.ppermute(x, 'c', pairs(2, 0))]
  transfers between devices with their start and end apart: 17 -> 18, of which waited for: 10 -> 8; matrix products, arithmetic and copies ran while one was open for 0% -> 0% of each run, Pallas kernels for 11% -> 13%
where the time goes in v5:
time: 108 us
  waiting for transfers between devices  46.6 us (43%)
  starting transfers between devices  41 us (38%)
  Pallas kernels  19.8 us (18%)
    pallas_call x10, Pallas kernels, call(): pl.pallas_call(kernel, out_shape=[jax.ShapeDtypeStruct(s, F32) for s in o...  19.8 us
    ppermute x7, starting transfers between devices, swap_c(): return lax.ppermute(x, 'c', pairs(2, 0))  17.1 us
    all_to_all x1, waiting for transfers between devices, steps(): own = lax.all_to_all(strips, PLANE, 0, 0, tiled=True)  13.9 us
    ppermute x1, waiting for transfers between devices, steps(): even = lax.ppermute(even, 'z', pairs(8, 0))  9.59 us
    ppermute x3, waiting for transfers between devices, swap_o(): return lax.ppermute(x, SPACE, pairs(32, 1))  7.64 us
    all_to_all x1, waiting for transfers between devices, steps(): fixes = lax.all_to_all(fixes, PLANE, 0, 0, tiled=True)  7.36 us
    ppermute x3, starting transfers between devices, swap_o(): return lax.ppermute(x, SPACE, pairs(32, 1))  6.24 us
    all_to_all x1, starting transfers between devices, steps(): fixes = lax.all_to_all(fixes, PLANE, 0, 0, tiled=True)  5.4 us
  transfers between devices with their start and end apart: 18, of which 8 were waited for; matrix products, arithmetic and copies ran while one was open for 0% of the time, Pallas kernels for 13%

profile of v5, /device:TPU:1, one launch (start us, length us, event | category | flops | bytes accessed | tf_op | source)
XLA Modules:
  0.0 107.6 jit_solution(3561242711123511342)
XLA Ops:
  0.0 2.1 %shard_map.37 = (f32[768,128]{1,0:T(8,128)S(1)}, f32[768,128]{1,0:T(8,128)S(1)}) custom-call(f32[1,8,256,128]{3,2,1,0:T(8,128)} %u_in.3, s32[8,256,128]{2,1,0:T(8,128)} %mat.3, f32[8,256,128]{2,1,0:T(8,128)} %src_in.1), custom_call_target="tpu_custom_call" | custom-call | tf_op jit(solution)/shard_map/pallas_call | solution.py:543
  2.1 4.2 %collective-permute-start.1 = (f32[768,128]{1,0:T(8,128)S(1)}, f32[768,128]{1,0:T(8,128)S(1)}, u32[]{:S(2)}, u32[]{:S(2)}) collective-permute-start(f32[768,128]{1,0:T(8,128)S(1)} %get-tuple-element.49.so), channel_id=1, source_target_pairs={{1,2},{2,1},{3,4},{4,3},{5,6},{6,5},{7,8},{8,7},{9,10},{10,9},{11,... | collective-permute-start | bytes 1179656 | tf_op jit(solution)/shard_map/ppermute | solution.py:578
  6.3 5.1 %collective-permute-start = (f32[768,128]{1,0:T(8,128)S(1)}, f32[768,128]{1,0:T(8,128)S(1)}, u32[]{:S(2)}, u32[]{:S(2)}) collective-permute-start(f32[768,128]{1,0:T(8,128)S(1)} %get-tuple-element.47._.sc), channel_id=1, source_target_pairs={{0,1},{1,0},{2,3},{3,2},{4,5},{5,4},{6,7},{7,6},{8,9},{9,8},{10,11... | collective-permute-start | bytes 1179656 | tf_op jit(solution)/shard_map/ppermute | solution.py:575
  11.5 5.8 %shard_map.38 = (f32[8,256,128]{2,1,0:T(8,128)S(1)}, f32[8,256,128]{2,1,0:T(8,128)S(1)}, f32[8,256,128]{2,1,0:T(8,128)S(1)}, f32[8,256,128]{2,1,0:T(8,128)S(1)},...) custom-call(f32[1,8,256,128]{3,2,1,0:T(8,128)} %u_in.3, ...), custom_call_target="tpu_custom_call" | custom-call | tf_op jit(solution)/shard_map/pallas_call | solution.py:543
  17.3 0.9 shard_map.39
  18.3 0.1 collective-permute-start.2
  18.4 2.0 %collective-permute-start.3 = (f32[512,128]{1,0:T(8,128)S(1)}, f32[512,128]{1,0:T(8,128)S(1)}, u32[]{:S(2)}, u32[]{:S(2)}) collective-permute-start(f32[512,128]{1,0:T(8,128)S(1)} %get-tuple-element.61), channel_id=1, source_target_pairs={{1,2},{2,1},{3,4},{4,3},{5,6},{6,5},{7,8},{8,7},{9,10},{10,9},{11,... | collective-permute-start | bytes 786440 | tf_op jit(solution)/shard_map/ppermute | solution.py:578
  20.4 5.7 %collective-permute-start.4 = (f32[384,128]{1,0:T(8,128)S(1)}, f32[384,128]{1,0:T(8,128)S(1)}, u32[]{:S(2)}, u32[]{:S(2)}) collective-permute-start(f32[384,128]{1,0:T(8,128)S(1)} %get-tuple-element.62.csc), channel_id=1, source_target_pairs={{0,1},{1,0},{2,3},{3,2},{4,5},{5,4},{6,7},{7,6},{8,9},{9,8},{10,11... | collective-permute-start | bytes 589832 | tf_op jit(solution)/shard_map/ppermute | solution.py:575
  26.1 1.1 collective-permute-done.4.crc
  27.2 7.6 %collective-permute-done.5.cro = f32[384,128]{1,0:T(8,128)S(1)} collective-permute-done((f32[384,128]{1,0:T(8,128)S(1)}, f32[384,128]{1,0:T(8,128)S(1)}, u32[]{:S(2)}, u32[]{:S(2)}) %collective-permute-start.5) | collective-permute-done | bytes 196640 | tf_op jit(solution)/shard_map/ppermute | solution.py:578
  34.8 2.4 %shard_map.40 = (f32[8,272,128]{2,1,0:T(8,128)S(1)}, f32[8,272,128]{2,1,0:T(8,128)S(1)}, f32[4,144,128]{2,1,0:T(8,128)S(1)}) custom-call(f32[8,272,128]{2,1,0:T(8,128)S(1)} %get-tuple-element.58.u2, f32[8,256,128]{2,1,0:T(8,128)S(1)} %get-tuple-element.48.src, f32[384,128]{1,0:T(8,128)S(1)} %get-tuple-element.62.csc, f32[384,128]{1,0:T(8,128)S(1)} %get-tuple-element.63.cso, ...), custom_call_target="tpu_custom_call" | custom-call | tf_op jit(solution)/shard_map/pallas_call | solution.py:543
  37.2 1.9 %shard_map.41 = (f32[8,272,128]{2,1,0:T(8,128)S(1)}, f32[8,272,128]{2,1,0:T(8,128)S(1)}, f32[8,256,128]{2,1,0:T(8,128)S(1)}, f32[16,144,128]{2,1,0:T(8,128)}) custom-call(f32[8,272,128]{2,1,0:T(8,128)S(1)} %get-tuple-element.58.u2, f32[8,256,128]{2,1,0:T(8,128)S(1)} %get-tuple-element.48.src, ...), custom_call_target="tpu_custom_call", output_to_operand_aliasing={{0}: (5, {}), {1}: (6, {})} | custom-call | tf_op jit(solution)/shard_map/pallas_call | solution.py:543
  39.1 4.3 %all-to-all-start = ((f32[16,144,128]{2,1,0:T(8,128)}), f32[16,144,128]{2,1,0:T(8,128)S(1)}, u32[]{:S(2)}, u32[]{:S(2)}) async-start(f32[16,144,128]{2,1,0:T(8,128)} %get-tuple-element.74), calls=%async_computation | async-start | bytes 2359296 | tf_op jit(solution)/shard_map/all_to_all | solution.py:619
  43.5 2.9 %collective-permute-start.8 = (f32[4,40,128]{2,1,0:T(8,128)S(1)}, f32[4,40,128]{2,1,0:T(8,128)S(1)}, u32[]{:S(2)}, u32[]{:S(2)}) collective-permute-start(f32[4,40,128]{2,1,0:T(8,128)S(1)} %get-tuple-element.80), channel_id=1, source_target_pairs={{0,2},{2,0},{1,3},{3,1},{4,6},{6,4},{5,7},{7,5},{8,10},{10,8},{9,1... | collective-permute-start | bytes 245768 | tf_op jit(solution)/shard_map/ppermute | solution.py:608
  46.3 13.9 %all-to-all-done = f32[16,144,128]{2,1,0:T(8,128)S(1)} async-done(((f32[16,144,128]{2,1,0:T(8,128)}), f32[16,144,128]{2,1,0:T(8,128)S(1)}, u32[]{:S(2)}, u32[]{:S(2)}) %all-to-all-start) | async-done | bytes 1179680 | tf_op jit(solution)/shard_map/all_to_all | solution.py:619
  60.3 2.1 %collective-permute-start.7 = (f32[8,288,128]{2,1,0:T(8,128)S(1)}, f32[8,288,128]{2,1,0:T(8,128)S(1)}, u32[]{:S(2)}, u32[]{:S(2)}) collective-permute-start(f32[8,288,128]{2,1,0:T(8,128)S(1)} %bitcast.1), channel_id=1, source_target_pairs={{0,1},{1,0},{2,3},{3,2},{4,5},{5,4},{6,7},{7,6},{8,9},{9,8},{10,11... | collective-permute-start | bytes 3538952 | tf_op jit(solution)/shard_map/ppermute | solution.py:575
  62.4 3.1 %collective-permute-start.10 = (f32[8,40,128]{2,1,0:T(8,128)S(1)}, f32[8,40,128]{2,1,0:T(8,128)S(1)}, u32[]{:S(2)}, u32[]{:S(2)}) collective-permute-start(f32[8,40,128]{2,1,0:T(8,128)S(1)} %shard_map.42.kown), channel_id=1, source_target_pairs={{4,8},{8,4},{12,16},{16,12},{20,24},{24,20},{0,28},{28,0},{5,9},{9... | collective-permute-start | bytes 491528 | tf_op jit(solution)/shard_map/ppermute | solution.py:623
  65.5 3.6 %collective-permute-done.10.kodd = f32[8,40,128]{2,1,0:T(8,128)S(1)} collective-permute-done((f32[8,40,128]{2,1,0:T(8,128)S(1)}, f32[8,40,128]{2,1,0:T(8,128)S(1)}, u32[]{:S(2)}, u32[]{:S(2)}) %collective-permute-start.10) | collective-permute-done | bytes 163872 | tf_op jit(solution)/shard_map/ppermute | solution.py:623
  69.2 1.2 %collective-permute-done.9.keven = f32[8,40,128]{2,1,0:T(8,128)S(1)} collective-permute-done((f32[8,40,128]{2,1,0:T(8,128)S(1)}, f32[8,40,128]{2,1,0:T(8,128)S(1)}, u32[]{:S(2)}, u32[]{:S(2)}) %collective-permute-start.9) | collective-permute-done | bytes 163872 | tf_op jit(solution)/shard_map/ppermute | solution.py:622
  70.4 0.1 shard_map.43
  70.5 0.6 collective-permute-start.11
  71.0 1.3 %collective-permute-start.12 = (f32[976,128]{1,0:T(8,128)S(1)}, f32[976,128]{1,0:T(8,128)S(1)}, u32[]{:S(2)}, u32[]{:S(2)}) collective-permute-start(f32[976,128]{1,0:T(8,128)S(1)} %get-tuple-element.82), channel_id=1, source_target_pairs={{4,8},{8,4},{12,16},{16,12},{20,24},{24,20},{0,28},{28,0},{5,9},{9... | collective-permute-start | bytes 1499144 | tf_op jit(solution)/shard_map/ppermute | solution.py:628
  72.3 9.6 %collective-permute-done.11.even = f32[976,128]{1,0:T(8,128)S(1)} collective-permute-done((f32[976,128]{1,0:T(8,128)S(1)}, f32[976,128]{1,0:T(8,128)S(1)}, u32[]{:S(2)}, u32[]{:S(2)}) %collective-permute-start.11) | collective-permute-done | bytes 499744 | tf_op jit(solution)/shard_map/ppermute | solution.py:627
  81.9 2.6 %collective-permute-start.13 = (f32[976,128]{1,0:T(8,128)S(1)}, f32[976,128]{1,0:T(8,128)S(1)}, u32[]{:S(2)}, u32[]{:S(2)}) collective-permute-start(f32[976,128]{1,0:T(8,128)S(1)} %collective-permute-done.11.even), channel_id=1, source_target_pairs={{0,1},{1,0},{2,3},{3,2},{4,5},{5,4},{6,7},{7,6},{8,9},{9,8},{10,11... | collective-permute-start | bytes 1499144 | tf_op jit(solution)/shard_map/ppermute | solution.py:575
  84.6 1.5 %collective-permute-start.14 = (f32[976,128]{1,0:T(8,128)S(1)}, f32[976,128]{1,0:T(8,128)S(1)}, u32[]{:S(2)}, u32[]{:S(2)}) collective-permute-start(f32[976,128]{1,0:T(8,128)S(1)} %collective-permute-done.12.odd), channel_id=1, source_target_pairs={{0,1},{1,0},{2,3},{3,2},{4,5},{5,4},{6,7},{7,6},{8,9},{9,8},{10,11... | collective-permute-start | bytes 1499144 | tf_op jit(solution)/shard_map/ppermute | solution.py:575
  86.1 0.0 collective-permute-start.15
  86.1 2.2 %collective-permute-done.15.pkall = f32[24,40,128]{2,1,0:T(8,128)S(1)} collective-permute-done((f32[24,40,128]{2,1,0:T(8,128)S(1)}, f32[24,40,128]{2,1,0:T(8,128)S(1)}, u32[]{:S(2)}, u32[]{:S(2)}) %collective-permute-start.15) | collective-permute-done | bytes 491552 | tf_op jit(solution)/shard_map/ppermute | solution.py:575
  88.3 1.3 %shard_map.44 = (f32[40,40,128]{2,1,0:T(8,128)S(1)}, f32[40,40,128]{2,1,0:T(8,128)S(1)}, f32[40,40,128]{2,1,0:T(8,128)S(1)}, f32[40,40,128]{2,1,0:T(8,128)S(1)}, f32[40,40,128]{2,1,0:T(8,128)S(1)}) custom-call(f32[24,40,128]{2,1,0:T(8,128)S(1)} %get-tuple-element.83.kall, f32[24,40,128]{2,1,0:T(8,128)S(1)} %collective-permute-done.15.pkall), custom_call_target="tpu_custom_call" | custom-call | tf_op jit(solution)/shard_map/pallas_call | solution.py:543
  89.6 4.1 %shard_map.45 = f32[16,4,8,128]{3,2,1,0:T(8,128)} custom-call(f32[8,288,128]{2,1,0:T(8,128)S(1)} %bitcast.3, f32[8,288,128]{2,1,0:T(8,128)S(1)} %collective-permute-done.7.part, f32[976,128]{1,0:T(8,128)S(1)} %collective-permute-done.11.even, f32[976,128]{1,0:T(8,128)S(1)} %collective-permute-done.12.odd, f32[976,128]{1,0:T(8,128)S(1)} %collective-permute-done.13.peven, ...), custom_call_target="tpu_custom_call" | custom-call | tf_op jit(solution)/shard_map/pallas_call | solution.py:543
  93.7 5.4 %all-to-all-start.1 = ((f32[16,4,8,128]{3,2,1,0:T(8,128)}), f32[16,4,8,128]{3,2,1,0:T(8,128)S(1)}, u32[]{:S(2)}, u32[]{:S(2)}) async-start(f32[16,4,8,128]{3,2,1,0:T(8,128)} %shard_map.45), calls=%async_computation.1 | async-start | bytes 524288 | tf_op jit(solution)/shard_map/all_to_all | solution.py:641
  99.1 7.4 %all-to-all-done.1.y_in = f32[16,4,8,128]{3,2,1,0:T(8,128)S(1)} async-done(((f32[16,4,8,128]{3,2,1,0:T(8,128)}), f32[16,4,8,128]{3,2,1,0:T(8,128)S(1)}, u32[]{:S(2)}, u32[]{:S(2)}) %all-to-all-start.1) | async-done | bytes 262176 | tf_op jit(solution)/shard_map/all_to_all | solution.py:641
  106.5 1.1 shard_map.46
  (14 shorter events, 0.1 us)
Async XLA Ops:
  2.1 15.2 %collective-permute-start.1 = (f32[768,128]{1,0:T(8,128)S(1)}, f32[768,128]{1,0:T(8,128)S(1)}, u32[]{:S(2)}, u32[]{:S(2)}) collective-permute-start(f32[768,128]{1,0:T(8,128)S(1)} %get-tuple-element.49.so), channel_id=1, source_target_pairs={{1,2},{2,1},{3,4},{4,3},{5,6},{6,5},{7,8},{8,7},{9,10},{10,9},{11,... | collective-permute-start | bytes 1179656 | tf_op jit(solution)/shard_map/ppermute | solution.py:578
  6.3 11.0 %collective-permute-start = (f32[768,128]{1,0:T(8,128)S(1)}, f32[768,128]{1,0:T(8,128)S(1)}, u32[]{:S(2)}, u32[]{:S(2)}) collective-permute-start(f32[768,128]{1,0:T(8,128)S(1)} %get-tuple-element.47._.sc), channel_id=1, source_target_pairs={{0,1},{1,0},{2,3},{3,2},{4,5},{5,4},{6,7},{7,6},{8,9},{9,8},{10,11... | collective-permute-start | bytes 1179656 | tf_op jit(solution)/shard_map/ppermute | solution.py:575
  18.3 18.9 %collective-permute-start.2 = (f32[512,128]{1,0:T(8,128)S(1)}, f32[512,128]{1,0:T(8,128)S(1)}, u32[]{:S(2)}, u32[]{:S(2)}) collective-permute-start(f32[512,128]{1,0:T(8,128)S(1)} %get-tuple-element.60), channel_id=1, source_target_pairs={{0,1},{1,0},{2,3},{3,2},{4,5},{5,4},{6,7},{7,6},{8,9},{9,8},{10,11... | collective-permute-start | bytes 786440 | tf_op jit(solution)/shard_map/ppermute | solution.py:575
  18.4 18.9 %collective-permute-start.3 = (f32[512,128]{1,0:T(8,128)S(1)}, f32[512,128]{1,0:T(8,128)S(1)}, u32[]{:S(2)}, u32[]{:S(2)}) collective-permute-start(f32[512,128]{1,0:T(8,128)S(1)} %get-tuple-element.61), channel_id=1, source_target_pairs={{1,2},{2,1},{3,4},{4,3},{5,6},{6,5},{7,8},{8,7},{9,10},{10,9},{11,... | collective-permute-start | bytes 786440 | tf_op jit(solution)/shard_map/ppermute | solution.py:578
  20.4 6.8 %collective-permute-start.4 = (f32[384,128]{1,0:T(8,128)S(1)}, f32[384,128]{1,0:T(8,128)S(1)}, u32[]{:S(2)}, u32[]{:S(2)}) collective-permute-start(f32[384,128]{1,0:T(8,128)S(1)} %get-tuple-element.62.csc), channel_id=1, source_target_pairs={{0,1},{1,0},{2,3},{3,2},{4,5},{5,4},{6,7},{7,6},{8,9},{9,8},{10,11... | collective-permute-start | bytes 589832 | tf_op jit(solution)/shard_map/ppermute | solution.py:575
  26.1 8.7 %collective-permute-start.5 = (f32[384,128]{1,0:T(8,128)S(1)}, f32[384,128]{1,0:T(8,128)S(1)}, u32[]{:S(2)}, u32[]{:S(2)}) collective-permute-start(f32[384,128]{1,0:T(8,128)S(1)} %get-tuple-element.63.cso), channel_id=1, source_target_pairs={{1,2},{2,1},{3,4},{4,3},{5,6},{6,5},{7,8},{8,7},{9,10},{10,9},{11,... | collective-permute-start | bytes 589832 | tf_op jit(solution)/shard_map/ppermute | solution.py:578
  39.1 21.1 %all-to-all-start = ((f32[16,144,128]{2,1,0:T(8,128)}), f32[16,144,128]{2,1,0:T(8,128)S(1)}, u32[]{:S(2)}, u32[]{:S(2)}) async-start(f32[16,144,128]{2,1,0:T(8,128)} %get-tuple-element.74), calls=%async_computation | async-start | bytes 2359296 | tf_op jit(solution)/shard_map/all_to_all | solution.py:619
  43.5 18.9 %collective-permute-start.8 = (f32[4,40,128]{2,1,0:T(8,128)S(1)}, f32[4,40,128]{2,1,0:T(8,128)S(1)}, u32[]{:S(2)}, u32[]{:S(2)}) collective-permute-start(f32[4,40,128]{2,1,0:T(8,128)S(1)} %get-tuple-element.80), channel_id=1, source_target_pairs={{0,2},{2,0},{1,3},{3,1},{4,6},{6,4},{5,7},{7,5},{8,10},{10,8},{9,1... | collective-permute-start | bytes 245768 | tf_op jit(solution)/shard_map/ppermute | solution.py:608
  60.3 29.3 %collective-permute-start.7 = (f32[8,288,128]{2,1,0:T(8,128)S(1)}, f32[8,288,128]{2,1,0:T(8,128)S(1)}, u32[]{:S(2)}, u32[]{:S(2)}) collective-permute-start(f32[8,288,128]{2,1,0:T(8,128)S(1)} %bitcast.1), channel_id=1, source_target_pairs={{0,1},{1,0},{2,3},{3,2},{4,5},{5,4},{6,7},{7,6},{8,9},{9,8},{10,11... | collective-permute-start | bytes 3538952 | tf_op jit(solution)/shard_map/ppermute | solution.py:575
  62.4 6.8 %collective-permute-start.10 = (f32[8,40,128]{2,1,0:T(8,128)S(1)}, f32[8,40,128]{2,1,0:T(8,128)S(1)}, u32[]{:S(2)}, u32[]{:S(2)}) collective-permute-start(f32[8,40,128]{2,1,0:T(8,128)S(1)} %shard_map.42.kown), channel_id=1, source_target_pairs={{4,8},{8,4},{12,16},{16,12},{20,24},{24,20},{0,28},{28,0},{5,9},{9... | collective-permute-start | bytes 491528 | tf_op jit(solution)/shard_map/ppermute | solution.py:623
  65.5 4.8 %collective-permute-start.9 = (f32[8,40,128]{2,1,0:T(8,128)S(1)}, f32[8,40,128]{2,1,0:T(8,128)S(1)}, u32[]{:S(2)}, u32[]{:S(2)}) collective-permute-start(f32[8,40,128]{2,1,0:T(8,128)S(1)} %shard_map.42.kown), channel_id=1, source_target_pairs={{0,4},{4,0},{8,12},{12,8},{16,20},{20,16},{24,28},{28,24},{1,5},{5... | collective-permute-start | bytes 491528 | tf_op jit(solution)/shard_map/ppermute | solution.py:622
  70.5 11.5 %collective-permute-start.11 = (f32[976,128]{1,0:T(8,128)S(1)}, f32[976,128]{1,0:T(8,128)S(1)}, u32[]{:S(2)}, u32[]{:S(2)}) collective-permute-start(f32[976,128]{1,0:T(8,128)S(1)} %get-tuple-element.81), channel_id=1, source_target_pairs={{0,4},{4,0},{8,12},{12,8},{16,20},{20,16},{24,28},{28,24},{1,5},{5... | collective-permute-start | bytes 1499144 | tf_op jit(solution)/shard_map/ppermute | solution.py:627
  71.0 13.5 %collective-permute-start.12 = (f32[976,128]{1,0:T(8,128)S(1)}, f32[976,128]{1,0:T(8,128)S(1)}, u32[]{:S(2)}, u32[]{:S(2)}) collective-permute-start(f32[976,128]{1,0:T(8,128)S(1)} %get-tuple-element.82), channel_id=1, source_target_pairs={{4,8},{8,4},{12,16},{16,12},{20,24},{24,20},{0,28},{28,0},{5,9},{9... | collective-permute-start | bytes 1499144 | tf_op jit(solution)/shard_map/ppermute | solution.py:628
  72.3 26.8 %collective-permute-start.6 = (f32[8,256,128]{2,1,0:T(8,128)S(1)}, f32[8,256,128]{2,1,0:T(8,128)S(1)}, u32[]{:S(2)}, u32[]{:S(2)}) collective-permute-start(f32[8,256,128]{2,1,0:T(8,128)S(1)} %get-tuple-element.76), channel_id=1, source_target_pairs={{0,32},{32,64},{64,96},{96,128},{128,160},{160,192},{192,224},{224... | collective-permute-start | bytes 3145736 | tf_op jit(solution)/shard_map/ppermute | solution.py:631
  81.9 7.6 %collective-permute-start.13 = (f32[976,128]{1,0:T(8,128)S(1)}, f32[976,128]{1,0:T(8,128)S(1)}, u32[]{:S(2)}, u32[]{:S(2)}) collective-permute-start(f32[976,128]{1,0:T(8,128)S(1)} %collective-permute-done.11.even), channel_id=1, source_target_pairs={{0,1},{1,0},{2,3},{3,2},{4,5},{5,4},{6,7},{7,6},{8,9},{9,8},{10,11... | collective-permute-start | bytes 1499144 | tf_op jit(solution)/shard_map/ppermute | solution.py:575
  84.6 5.0 %collective-permute-start.14 = (f32[976,128]{1,0:T(8,128)S(1)}, f32[976,128]{1,0:T(8,128)S(1)}, u32[]{:S(2)}, u32[]{:S(2)}) collective-permute-start(f32[976,128]{1,0:T(8,128)S(1)} %collective-permute-done.12.odd), channel_id=1, source_target_pairs={{0,1},{1,0},{2,3},{3,2},{4,5},{5,4},{6,7},{7,6},{8,9},{9,8},{10,11... | collective-permute-start | bytes 1499144 | tf_op jit(solution)/shard_map/ppermute | solution.py:575
  86.1 2.2 %collective-permute-start.15 = (f32[24,40,128]{2,1,0:T(8,128)S(1)}, f32[24,40,128]{2,1,0:T(8,128)S(1)}, u32[]{:S(2)}, u32[]{:S(2)}) collective-permute-start(f32[24,40,128]{2,1,0:T(8,128)S(1)} %get-tuple-element.83.kall), channel_id=1, source_target_pairs={{0,1},{1,0},{2,3},{3,2},{4,5},{5,4},{6,7},{7,6},{8,9},{9,8},{10,11... | collective-permute-start | bytes 1474568 | tf_op jit(solution)/shard_map/ppermute | solution.py:575
  93.7 12.8 %all-to-all-start.1 = ((f32[16,4,8,128]{3,2,1,0:T(8,128)}), f32[16,4,8,128]{3,2,1,0:T(8,128)S(1)}, u32[]{:S(2)}, u32[]{:S(2)}) async-start(f32[16,4,8,128]{3,2,1,0:T(8,128)} %shard_map.45), calls=%async_computation.1 | async-start | bytes 524288 | tf_op jit(solution)/shard_map/all_to_all | solution.py:641
